TPU v7x, 32 devices: a whole 2x2x4 slice. The times are simulated.
32 devices in a mesh: lat: 8 (over y, x, core), lon: 4 (over z).
Axes of the slice: x: 2, y: 2, z: 4, core: 2. Of those that a mesh axis runs over, the one named last changes fastest.
Arguments:
- noise: float32 [4, 8, 128, 1024], P(None, None, 'lat', 'lon'), may hold values from -6 to 6
- diff_lat: float32 [8, 128, 1024], P(None, 'lat', 'lon'), may hold values from 0.05 to 0.24
- diff_lon: float32 [8, 128, 1024], P(None, 'lat', 'lon'), may hold values from 0.05 to 0.24
- shear: float32 [8, 128, 1024], P(None, 'lat', 'lon'), may hold values from -0.9 to 0.9
- sea_mask: int32 [8, 128, 1024], P(None, 'lat', 'lon'), may hold values from 0 to 1, as said below
Outputs:
- normalized: float32 [4, 8, 128, 1024], P(None, None, 'lat', 'lon')
- mean_var: float32 [], replicated
Inputs may be any that keep to these rules, and one draw needn't show every extreme that they name: `sea_mask`: every block of 16 latitude rows by 256 longitude columns has its own chance for each cell to be wet, from a quarter to one; the block of the first rows and first columns is wet at every level.
All inputs are finite; a program needn't handle non-finite values.
Results may differ from a plain program's by a relative error of at most 0.0003.
Values sent between devices are 32-bit elements; how exact they have to be, the bound alone decides.
No kernel may reach another device: no remote copies, remote signals or barrier semaphores. Data moves between devices by JAX's collectives and lax.ppermute only.
A program may use at most 64 MiB of HBM per device.

v0:
```python
import jax
import jax.numpy as jnp
from jax import lax
from jax.sharding import PartitionSpec as P

SAMPLES = 4
ITERS = 4


def with_halo(x, sides, width, wrap):
    for axis, dim in sides:
        size, length = (lax.axis_size(axis), x.shape[dim])
        up = [(i, (i + 1) % size) for i in range(size if wrap else size - 1)]
        down = [(j, i) for i, j in up]
        last = lax.slice_in_dim(x, length - width, length, axis=dim)
        first = lax.slice_in_dim(x, 0, width, axis=dim)
        before = lax.ppermute(last, axis, up)
        after = lax.ppermute(first, axis, down)
        x = jnp.concatenate([before, x, after], axis=dim)
    return x


def widen(field, width):
    field = with_halo(field, (("lon", 3),), width, True)
    return with_halo(field, (("lat", 2),), width, False)


def adjoint_step(padded, tensors):
    height = padded.shape[2]
    breadth = padded.shape[3]
    k11 = tensors[0]
    k22 = tensors[1]
    cross = tensors[2] * jnp.sqrt(k11 * k22)
    masked = tensors[3] * padded
    table = [
        ((0, 0), 1.0 - 2.0 * (k11 + k22)),
        ((1, 0), k11),
        ((-1, 0), k11),
        ((0, 1), k22),
        ((0, -1), k22),
        ((1, 1), 0.5 * cross),
        ((-1, -1), 0.5 * cross),
        ((1, -1), -0.5 * cross),
        ((-1, 1), -0.5 * cross),
    ]
    total = jnp.zeros(padded.shape[:2] + (height - 2, breadth - 2), jnp.float32)
    for offset, weight in table:
        product = weight * masked
        total = (
            total
            + product[
                :,
                :,
                1 - offset[0] : height - 1 - offset[0],
                1 - offset[1] : breadth - 1 - offset[1],
            ]
        )
    return total


def shards(noise, diff_lat, diff_lon, shear, sea_mask):
    rows = noise.shape[2]
    cols = noise.shape[3]
    wet = sea_mask.astype(jnp.float32)
    stacked = jnp.stack([diff_lat, diff_lon, shear, wet], axis=0)
    wide_tensors = widen(stacked, ITERS)
    field = noise
    field = widen(field, ITERS)
    for step in range(ITERS):
        reach = ITERS - step
        tensors = wide_tensors[
            :, :, ITERS - reach : ITERS + rows + reach, ITERS - reach : ITERS + cols + reach
        ]
        field = adjoint_step(field, tensors)
    var = jnp.sum(field * field, axis=0) / SAMPLES
    wet_sum, wet_count = lax.psum((jnp.sum(wet * var), jnp.sum(wet)), ("lat", "lon"))
    mean_var = wet_sum / wet_count
    safe = jnp.where(wet > 0, var, 1.0)
    factor = wet * jnp.sqrt(mean_var / (safe + 1e-06))
    return (field * factor, mean_var)


def solution(mesh):
    return jax.shard_map(
        shards,
        mesh=mesh,
        in_specs=(
            P(None, None, "lat", "lon"),
            P(None, "lat", "lon"),
            P(None, "lat", "lon"),
            P(None, "lat", "lon"),
            P(None, "lat", "lon"),
        ),
        out_specs=(P(None, None, "lat", "lon"), P()),
        check_vma=False,
    )
```

profile of v0, /device:TPU:0, one launch (start us, length us, event | category | flops | bytes accessed | tf_op | source)
XLA Modules:
  0.0 102.8 jit_solution(17644934202735698330)
XLA Ops:
  0.6 0.0 copy-start.4
  0.6 0.0 copy-start.3
  0.7 0.0 copy-start.2
  0.7 1.0 convert_bitcast_fusion
  1.6 1.1 %pad_maximum_fusion.1 = f32[4,8,16,256]{3,2,1,0:T(8,128)S(1)} fusion(f32[1,8,16,256]{3,2,1,0:T(8,128)S(1)} %convert_bitcast_fusion, f32[1,8,16,256]{3,2,1,0:T(8,128)} %bitcast.53, f32[1,8,16,256]{3,2,1,0:T(8,128)} %bitcast.56, f32[1,8,16,256]{3,2,1,0:T(8,128)} %bitcast.59), kind=kLoop, calls=%fused_computation.57 | loop fusion | flops 393216 | bytes 1048576 | tf_op jit(solution)/shard_map/stack | solution.py:65
  2.7 0.0 copy-start
  2.7 0.1 fusion.7
  2.9 3.1 %collective-permute-start = (f32[4,8,16,4]{3,2,1,0:T(8,128)S(1)}, f32[4,8,16,4]{3,2,1,0:T(8,128)S(1)}, u32[]{:S(2)}, u32[]{:S(2)}) collective-permute-start(f32[4,8,16,4]{3,2,1,0:T(8,128)S(1)} %get-tuple-element.58), channel_id=1, source_target_pairs={{0,1},{1,2},{2,3},{3,0},{4,5},{5,6},{6,7},{7,4},{8,9},{9,10},{10,1... | collective-permute-start | bytes 24584 | tf_op jit(solution)/shard_map/ppermute | solution.py:17
  6.0 2.1 %collective-permute-start.1 = (f32[4,8,16,4]{3,2,1,0:T(8,128)S(1)}, f32[4,8,16,4]{3,2,1,0:T(8,128)S(1)}, u32[]{:S(2)}, u32[]{:S(2)}) collective-permute-start(f32[4,8,16,4]{3,2,1,0:T(8,128)S(1)} %get-tuple-element.59), channel_id=1, source_target_pairs={{1,0},{2,1},{3,2},{0,3},{5,4},{6,5},{7,6},{4,7},{9,8},{10,9},{11,1... | collective-permute-start | bytes 24584 | tf_op jit(solution)/shard_map/ppermute | solution.py:18
  8.0 7.1 %collective-permute-done = f32[4,8,16,4]{3,2,1,0:T(8,128)S(1)} collective-permute-done((f32[4,8,16,4]{3,2,1,0:T(8,128)S(1)}, f32[4,8,16,4]{3,2,1,0:T(8,128)S(1)}, u32[]{:S(2)}, u32[]{:S(2)}) %collective-permute-start) | collective-permute-done | bytes 8224 | tf_op jit(solution)/shard_map/ppermute | solution.py:17
  15.2 4.2 %collective-permute-done.1 = f32[4,8,16,4]{3,2,1,0:T(8,128)S(1)} collective-permute-done((f32[4,8,16,4]{3,2,1,0:T(8,128)S(1)}, f32[4,8,16,4]{3,2,1,0:T(8,128)S(1)}, u32[]{:S(2)}, u32[]{:S(2)}) %collective-permute-start.1) | collective-permute-done | bytes 8224 | tf_op jit(solution)/shard_map/ppermute | solution.py:18
  19.4 0.3 pad_maximum_fusion.10
  19.7 1.4 %collective-permute-start.2 = (f32[4,8,4,264]{3,2,1,0:T(4,128)S(1)}, f32[4,8,4,264]{3,2,1,0:T(4,128)S(1)}, u32[]{:S(2)}, u32[]{:S(2)}) collective-permute-start(f32[4,8,4,264]{3,2,1,0:T(4,128)S(1)} %get-tuple-element.54), channel_id=1, source_target_pairs={{0,4},{4,8},{8,12},{12,16},{16,20},{20,24},{24,28},{1,5},{5,9},{9,... | collective-permute-start | bytes 405512 | tf_op jit(solution)/shard_map/ppermute | solution.py:17
  21.1 1.3 %collective-permute-start.3 = (f32[4,8,4,264]{3,2,1,0:T(4,128)S(1)}, f32[4,8,4,264]{3,2,1,0:T(4,128)S(1)}, u32[]{:S(2)}, u32[]{:S(2)}) collective-permute-start(f32[4,8,4,264]{3,2,1,0:T(4,128)S(1)} %get-tuple-element.55), channel_id=1, source_target_pairs={{4,0},{8,4},{12,8},{16,12},{20,16},{24,20},{28,24},{5,1},{9,5},{13... | collective-permute-start | bytes 405512 | tf_op jit(solution)/shard_map/ppermute | solution.py:18
  22.4 0.1 fusion.6
  22.5 1.7 %collective-permute-start.4 = (f32[4,8,16,4]{3,2,1,0:T(8,128)S(1)}, f32[4,8,16,4]{3,2,1,0:T(8,128)S(1)}, u32[]{:S(2)}, u32[]{:S(2)}) collective-permute-start(f32[4,8,16,4]{3,2,1,0:T(8,128)S(1)} %get-tuple-element.56), channel_id=1, source_target_pairs={{0,1},{1,2},{2,3},{3,0},{4,5},{5,6},{6,7},{7,4},{8,9},{9,10},{10,1... | collective-permute-start | bytes 24584 | tf_op jit(solution)/shard_map/ppermute | solution.py:17
  24.3 2.1 %collective-permute-start.5 = (f32[4,8,16,4]{3,2,1,0:T(8,128)S(1)}, f32[4,8,16,4]{3,2,1,0:T(8,128)S(1)}, u32[]{:S(2)}, u32[]{:S(2)}) collective-permute-start(f32[4,8,16,4]{3,2,1,0:T(8,128)S(1)} %get-tuple-element.57), channel_id=1, source_target_pairs={{1,0},{2,1},{3,2},{0,3},{5,4},{6,5},{7,6},{4,7},{9,8},{10,9},{11,1... | collective-permute-start | bytes 24584 | tf_op jit(solution)/shard_map/ppermute | solution.py:18
  26.4 5.5 %collective-permute-done.4 = f32[4,8,16,4]{3,2,1,0:T(8,128)S(1)} collective-permute-done((f32[4,8,16,4]{3,2,1,0:T(8,128)S(1)}, f32[4,8,16,4]{3,2,1,0:T(8,128)S(1)}, u32[]{:S(2)}, u32[]{:S(2)}) %collective-permute-start.4) | collective-permute-done | bytes 8224 | tf_op jit(solution)/shard_map/ppermute | solution.py:17
  31.9 7.0 %collective-permute-done.5 = f32[4,8,16,4]{3,2,1,0:T(8,128)S(1)} collective-permute-done((f32[4,8,16,4]{3,2,1,0:T(8,128)S(1)}, f32[4,8,16,4]{3,2,1,0:T(8,128)S(1)}, u32[]{:S(2)}, u32[]{:S(2)}) %collective-permute-start.5) | collective-permute-done | bytes 8224 | tf_op jit(solution)/shard_map/ppermute | solution.py:18
  38.9 0.3 pad_maximum_fusion.4
  39.2 2.0 %collective-permute-start.6 = (f32[4,8,4,264]{3,2,1,0:T(4,128)S(1)}, f32[4,8,4,264]{3,2,1,0:T(4,128)S(1)}, u32[]{:S(2)}, u32[]{:S(2)}) collective-permute-start(f32[4,8,4,264]{3,2,1,0:T(4,128)S(1)} %get-tuple-element.52), channel_id=1, source_target_pairs={{0,4},{4,8},{8,12},{12,16},{16,20},{20,24},{24,28},{1,5},{5,9},{9,... | collective-permute-start | bytes 405512 | tf_op jit(solution)/shard_map/ppermute | solution.py:17
  41.2 1.3 %collective-permute-start.7 = (f32[4,8,4,264]{3,2,1,0:T(4,128)S(1)}, f32[4,8,4,264]{3,2,1,0:T(4,128)S(1)}, u32[]{:S(2)}, u32[]{:S(2)}) collective-permute-start(f32[4,8,4,264]{3,2,1,0:T(4,128)S(1)} %get-tuple-element.53), channel_id=1, source_target_pairs={{4,0},{8,4},{12,8},{16,12},{20,16},{24,20},{28,24},{5,1},{9,5},{13... | collective-permute-start | bytes 405512 | tf_op jit(solution)/shard_map/ppermute | solution.py:18
  42.5 0.0 collective-permute-done.2
  42.5 0.0 collective-permute-done.3
  42.6 0.5 pad_maximum_fusion
  43.1 0.2 subtract_bitcast_fusion
  43.2 0.4 subtract_bitcast_fusion.1
  43.6 0.4 subtract_bitcast_fusion.2
  44.1 0.4 subtract_bitcast_fusion.3
  44.5 0.1 slice.269
  44.6 0.1 slice.280
  44.8 0.1 slice.291
  44.9 0.1 slice.302
  45.0 1.7 %collective-permute-done.7 = f32[4,8,4,264]{3,2,1,0:T(4,128)S(1)} collective-permute-done((f32[4,8,4,264]{3,2,1,0:T(4,128)S(1)}, f32[4,8,4,264]{3,2,1,0:T(4,128)S(1)}, u32[]{:S(2)}, u32[]{:S(2)}) %collective-permute-start.7) | collective-permute-done | bytes 135200 | tf_op jit(solution)/shard_map/ppermute | solution.py:18
  46.7 0.6 broadcast_multiply_fusion.15
  47.3 0.3 broadcast_multiply_fusion.14
  47.7 2.0 %broadcast_multiply_fusion.11 = (f32[4,8,22,262]{3,2,1,0:T(8,128)S(1)}, f32[4,8,22,262]{3,2,1,0:T(8,128)S(1)}) fusion(f32[8,22,262]{2,1,0:T(8,128)S(1)} %get-tuple-element.39, f32[4,8,24,264]{3,2,1,0:T(8,128)S(1)} %get-tuple-element.51, f32[4,8,24,264]{3,2,1,0:T(8,128)S(1)} %get-tuple-element.50, f32[4,8,24,264]{3,2,1,0:T(8,128)S(1)} %get-tuple-element.49, ...), kind=kLoop, calls=%fused_computation.43 | loop fusion | flops 2028928 | bytes 8669056 | tf_op jit(solution)/shard_map/mul | solution.py:48
  49.7 0.3 broadcast_multiply_fusion.10
  50.0 2.0 %broadcast_multiply_fusion.7 = (f32[4,8,20,260]{3,2,1,0:T(8,128)S(1)}, f32[4,8,20,260]{3,2,1,0:T(8,128)S(1)}) fusion(f32[8,20,260]{2,1,0:T(8,128)S(1)} %get-tuple-element.30, f32[4,8,22,262]{3,2,1,0:T(8,128)S(1)} %get-tuple-element.42, f32[4,8,22,262]{3,2,1,0:T(8,128)S(1)} %get-tuple-element.41, f32[4,8,22,262]{3,2,1,0:T(8,128)S(1)} %get-tuple-element.40, ...), kind=kLoop, calls=%fused_computation.39 | loop fusion | flops 1830400 | bytes 7820800 | tf_op jit(solution)/shard_map/mul | solution.py:48
  52.0 0.3 broadcast_multiply_fusion.6
  52.4 2.0 %broadcast_multiply_fusion.3 = (f32[4,8,18,258]{3,2,1,0:T(8,128)S(1)}, f32[4,8,18,258]{3,2,1,0:T(8,128)S(1)}) fusion(f32[8,18,258]{2,1,0:T(8,128)S(1)} %get-tuple-element.21, f32[4,8,20,260]{3,2,1,0:T(8,128)S(1)} %get-tuple-element.33, f32[4,8,20,260]{3,2,1,0:T(8,128)S(1)} %get-tuple-element.32, f32[4,8,20,260]{3,2,1,0:T(8,128)S(1)} %get-tuple-element.31, ...), kind=kLoop, calls=%fused_computation.35 | loop fusion | flops 1634688 | bytes 6984576 | tf_op jit(solution)/shard_map/mul | solution.py:48
  54.4 0.3 broadcast_multiply_fusion.2
  54.7 0.0 copy-start.1
  54.7 0.9 multiply_reduce_fusion
  55.6 0.6 convert_reduce_fusion
  56.3 43.2 %all-reduce = (f32[]{:T(128)}, f32[]{:T(128)}) all-reduce(f32[]{:T(128)} %get-tuple-element.3, f32[]{:T(128)} %get-tuple-element.2), channel_id=1, replica_groups=mesh['lat'=8,'lon'=4] {'lat','lon'}, use_global_device_ids=true, to_apply=%region_2.0 | all-reduce | flops 2 | bytes 16 | tf_op jit(solution)/shard_map/psum | solution.py:76
  100.8 0.1 sqrt_multiply_fusion
  100.9 0.9 broadcast_multiply_fusion.16
  (6 shorter events, 0.0 us)
Async XLA Ops:
  0.6 18.7 %copy-start.4 = (f32[8,16,256]{2,1,0:T(8,128)S(1)}, f32[8,16,256]{2,1,0:T(8,128)}, u32[]{:S(2)}) copy-start(f32[8,16,256]{2,1,0:T(8,128)} %param.6) | copy-start | bytes 393220
  0.6 18.7 %copy-start.3 = (f32[8,16,256]{2,1,0:T(8,128)S(1)}, f32[8,16,256]{2,1,0:T(8,128)}, u32[]{:S(2)}) copy-start(f32[8,16,256]{2,1,0:T(8,128)} %param.7) | copy-start | bytes 393220
  0.7 18.7 %copy-start.2 = (f32[8,16,256]{2,1,0:T(8,128)S(1)}, f32[8,16,256]{2,1,0:T(8,128)}, u32[]{:S(2)}) copy-start(f32[8,16,256]{2,1,0:T(8,128)} %param.8) | copy-start | bytes 393220
  2.7 19.7 %copy-start = (f32[4,8,16,256]{3,2,1,0:T(8,128)S(1)}, f32[4,8,16,256]{3,2,1,0:T(8,128)}, u32[]{:S(2)}) copy-start(f32[4,8,16,256]{3,2,1,0:T(8,128)} %param.5) | copy-start | bytes 1572868
  2.9 12.3 %collective-permute-start = (f32[4,8,16,4]{3,2,1,0:T(8,128)S(1)}, f32[4,8,16,4]{3,2,1,0:T(8,128)S(1)}, u32[]{:S(2)}, u32[]{:S(2)}) collective-permute-start(f32[4,8,16,4]{3,2,1,0:T(8,128)S(1)} %get-tuple-element.58), channel_id=1, source_target_pairs={{0,1},{1,2},{2,3},{3,0},{4,5},{5,6},{6,7},{7,4},{8,9},{9,10},{10,1... | collective-permute-start | bytes 24584 | tf_op jit(solution)/shard_map/ppermute | solution.py:17
  6.0 13.4 %collective-permute-start.1 = (f32[4,8,16,4]{3,2,1,0:T(8,128)S(1)}, f32[4,8,16,4]{3,2,1,0:T(8,128)S(1)}, u32[]{:S(2)}, u32[]{:S(2)}) collective-permute-start(f32[4,8,16,4]{3,2,1,0:T(8,128)S(1)} %get-tuple-element.59), channel_id=1, source_target_pairs={{1,0},{2,1},{3,2},{0,3},{5,4},{6,5},{7,6},{4,7},{9,8},{10,9},{11,1... | collective-permute-start | bytes 24584 | tf_op jit(solution)/shard_map/ppermute | solution.py:18
  19.7 22.8 %collective-permute-start.2 = (f32[4,8,4,264]{3,2,1,0:T(4,128)S(1)}, f32[4,8,4,264]{3,2,1,0:T(4,128)S(1)}, u32[]{:S(2)}, u32[]{:S(2)}) collective-permute-start(f32[4,8,4,264]{3,2,1,0:T(4,128)S(1)} %get-tuple-element.54), channel_id=1, source_target_pairs={{0,4},{4,8},{8,12},{12,16},{16,20},{20,24},{24,28},{1,5},{5,9},{9,... | collective-permute-start | bytes 405512 | tf_op jit(solution)/shard_map/ppermute | solution.py:17
  21.1 21.5 %collective-permute-start.3 = (f32[4,8,4,264]{3,2,1,0:T(4,128)S(1)}, f32[4,8,4,264]{3,2,1,0:T(4,128)S(1)}, u32[]{:S(2)}, u32[]{:S(2)}) collective-permute-start(f32[4,8,4,264]{3,2,1,0:T(4,128)S(1)} %get-tuple-element.55), channel_id=1, source_target_pairs={{4,0},{8,4},{12,8},{16,12},{20,16},{24,20},{28,24},{5,1},{9,5},{13... | collective-permute-start | bytes 405512 | tf_op jit(solution)/shard_map/ppermute | solution.py:18
  22.5 9.4 %collective-permute-start.4 = (f32[4,8,16,4]{3,2,1,0:T(8,128)S(1)}, f32[4,8,16,4]{3,2,1,0:T(8,128)S(1)}, u32[]{:S(2)}, u32[]{:S(2)}) collective-permute-start(f32[4,8,16,4]{3,2,1,0:T(8,128)S(1)} %get-tuple-element.56), channel_id=1, source_target_pairs={{0,1},{1,2},{2,3},{3,0},{4,5},{5,6},{6,7},{7,4},{8,9},{9,10},{10,1... | collective-permute-start | bytes 24584 | tf_op jit(solution)/shard_map/ppermute | solution.py:17
  24.3 14.6 %collective-permute-start.5 = (f32[4,8,16,4]{3,2,1,0:T(8,128)S(1)}, f32[4,8,16,4]{3,2,1,0:T(8,128)S(1)}, u32[]{:S(2)}, u32[]{:S(2)}) collective-permute-start(f32[4,8,16,4]{3,2,1,0:T(8,128)S(1)} %get-tuple-element.57), channel_id=1, source_target_pairs={{1,0},{2,1},{3,2},{0,3},{5,4},{6,5},{7,6},{4,7},{9,8},{10,9},{11,1... | collective-permute-start | bytes 24584 | tf_op jit(solution)/shard_map/ppermute | solution.py:18
  39.2 5.8 %collective-permute-start.6 = (f32[4,8,4,264]{3,2,1,0:T(4,128)S(1)}, f32[4,8,4,264]{3,2,1,0:T(4,128)S(1)}, u32[]{:S(2)}, u32[]{:S(2)}) collective-permute-start(f32[4,8,4,264]{3,2,1,0:T(4,128)S(1)} %get-tuple-element.52), channel_id=1, source_target_pairs={{0,4},{4,8},{8,12},{12,16},{16,20},{20,24},{24,28},{1,5},{5,9},{9,... | collective-permute-start | bytes 405512 | tf_op jit(solution)/shard_map/ppermute | solution.py:17
  41.2 5.5 %collective-permute-start.7 = (f32[4,8,4,264]{3,2,1,0:T(4,128)S(1)}, f32[4,8,4,264]{3,2,1,0:T(4,128)S(1)}, u32[]{:S(2)}, u32[]{:S(2)}) collective-permute-start(f32[4,8,4,264]{3,2,1,0:T(4,128)S(1)} %get-tuple-element.53), channel_id=1, source_target_pairs={{4,0},{8,4},{12,8},{16,12},{20,16},{24,20},{28,24},{5,1},{9,5},{13... | collective-permute-start | bytes 405512 | tf_op jit(solution)/shard_map/ppermute | solution.py:18
  54.7 0.9 copy-start.1
where the time goes:
time: 103 us
  blocking collectives  43.2 us (42%)
  waiting for transfers between devices  25.4 us (25%)
  starting transfers between devices  15.1 us (15%)
  other arithmetic  15 us (15%)
  between operations  3.33 us (3%)
    psum x1, blocking collectives, shards(): lax.psum((jnp.sum(wet * var), jnp.sum(wet)), ('lat', 'lon'))  43.2 us
    ppermute x4, waiting for transfers between devices, with_halo(): after = lax.ppermute(first, axis, down)  12.8 us
    ppermute x4, waiting for transfers between devices, with_halo(): before = lax.ppermute(last, axis, up)  12.6 us
    mul x12, other arithmetic, adjoint_step(): product = weight * masked  9.35 us
    ppermute x4, starting transfers between devices, with_halo(): before = lax.ppermute(last, axis, up)  8.25 us
    ppermute x4, starting transfers between devices, with_halo(): after = lax.ppermute(first, axis, down)  6.81 us
  transfers between devices with their start and end apart: 8, of which 5 were waited for; matrix products, arithmetic and copies ran while one was open for 3% of the time, Pallas kernels for 0%

commit v1 on v0

v1 whole, which is shorter than its diff:
```python
import functools

import jax
import jax.numpy as jnp
from jax import lax
from jax.experimental import pallas as pl
from jax.experimental.pallas import tpu as pltpu
from jax.sharding import PartitionSpec as P

ITERS = 4
LANES = 128
SEG = 32
F32 = jnp.float32


def cell_weights(k11, k22, shear, mask):
    m = mask.astype(F32)
    return m * k11, m * k22, m * (0.5 * (shear * jnp.sqrt(k11 * k22)))


def centre_weight(wa, wb):
    return jnp.where(wa > 0, 1.0, 0.0) - 2.0 * (wa + wb)


def roll(x, shift):
    n = x.shape[-1]
    shift = shift % n
    return x if shift == 0 else pltpu.roll(x, shift, x.ndim - 1)


def lane_parts(shape):
    lane = lax.broadcasted_iota(jnp.int32, shape, 1)
    return lane, lane // SEG, lane % SEG


def stencil(rows, get_y, get_w, first, last, put):
    def products(r):
        y = get_y(r)
        w0, wa, wb, wc = get_w(r)
        return w0 * y, wa * y, wb * y, wc * y

    prev, here = products(first - 1), products(first)
    for r in range(first, last):
        after = products(r + 1)
        d, _, b, _ = here
        g = prev[3] - after[3]
        put(r, d + (prev[1] + after[1]) + roll(b + g, 1) + roll(b - g, -1))
        prev, here = here, after


def edge_kernel(n_ref, a_ref, b_ref, s_ref, m_ref, top_ref, bot_ref, n_to, a_to, b_to, s_to, m_to, sem):
    samples, levels, tiles = n_ref.shape[0], top_ref.shape[2], n_to.shape[0]
    rows = n_ref.shape[1] // levels
    copies = []
    for c in range(tiles):
        lanes = pl.ds(c * LANES, LANES)
        for k, (ref, to) in enumerate(((a_ref, a_to), (b_ref, b_to), (s_ref, s_to), (m_ref, m_to))):
            copies.append(pltpu.make_async_copy(ref.at[:, lanes], to.at[c], sem.at[c, k]))
        copies.append(pltpu.make_async_copy(n_ref.at[:, :, lanes], n_to.at[c], sem.at[c, 4]))
    for copy in copies:
        copy.start()
    for copy in copies:
        copy.wait()
    for i in range(ITERS):
        for out, r in ((top_ref, i), (bot_ref, rows - ITERS + i)):
            at = pl.ds(r, levels, stride=rows)
            for c in range(tiles):
                lanes = pl.ds(c * LANES, LANES)
                for s in range(samples):
                    out[i, s, :, lanes] = n_to[c, s, at]
                w = cell_weights(a_to[c, at], b_to[c, at], s_to[c, at], m_to[c, at])
                for k in range(3):
                    out[i, samples + k, :, lanes] = w[k]


def message(get, samples, parts):
    _, seg, l32 = parts
    acc = None
    for s in range(samples):
        v = jnp.where(l32 < SEG // 2, roll(get(s, 1), SEG * s + 4), roll(get(s, 0), SEG * s + 28))
        acc = v if acc is None else jnp.where(seg == s, v, acc)
    w = None
    for k in range(3):
        v = jnp.where(l32 < SEG // 2, roll(get(samples + k, 1), 4 * k + 8), roll(get(samples + k, 0), 24 - 4 * k))
        w = v if w is None else jnp.where((l32 // 4 == k + 1) | (l32 // 4 == 6 - k), v, w)
    w = replicate(w, seg)
    return jnp.where((l32 < 4) | (l32 >= 28), acc, w)


def replicate(v, seg):
    v = jnp.where(seg == 1, roll(v, SEG), v)
    return jnp.where(seg >= 2, roll(v, 2 * SEG), v)


def own_kernel(n_ref, a_ref, b_ref, s_ref, m_ref, y_ref, w_ref, msg_ref):
    rows, samples, levels, cols = y_ref.shape
    parts = lane_parts((levels, LANES))
    tiles = cols // LANES
    for r in range(rows):
        at = pl.ds(r, levels, stride=rows)
        edge = {}
        for c in range(tiles):
            lanes = pl.ds(c * LANES, LANES)
            vals = [n_ref[c, s, at] for s in range(samples)]
            for s in range(samples):
                y_ref[r, s, :, lanes] = vals[s]
            w = cell_weights(a_ref[c, at], b_ref[c, at], s_ref[c, at], m_ref[c, at])
            w_ref[r, 0, :, lanes] = centre_weight(w[0], w[1])
            for k in range(3):
                w_ref[r, 1 + k, :, lanes] = w[k]
            if c == 0:
                edge[0] = vals + list(w)
            if c == tiles - 1:
                edge[1] = vals + list(w)
        msg_ref[r] = message(lambda g, side: edge[side][g], samples, parts)


def join_kernel(own_ref, before_ref, after_ref, msg_ref):
    rows = own_ref.shape[0]
    samples, cols = before_ref.shape[1] - 3, before_ref.shape[3]
    parts = lane_parts(own_ref.shape[1:])
    msg_ref[ITERS : ITERS + rows] = own_ref[...]
    for i in range(ITERS):
        for ref, to in ((before_ref, i), (after_ref, ITERS + rows + i)):
            msg_ref[to] = message(
                lambda g, side: ref[i, g, :, pl.ds(side * (cols - LANES), LANES)], samples, parts
            )


def main_kernel(y_ref, w_ref, before_ref, after_ref, x_ref, sy_ref, sw_ref, wh_ref, p_ref, q_ref):
    rows, samples, levels, cols = y_ref.shape
    high = rows + 2 * ITERS
    _, seg, l32 = lane_parts((levels, LANES))

    def halo(r):
        return (before_ref, r) if r < ITERS else (after_ref, r - ITERS - rows)

    def own(r):
        return ITERS <= r < ITERS + rows

    for r in range(high):
        if not own(r):
            ref, i = halo(r)
            slot = r if r < ITERS else r - rows
            w = [ref[i, samples + k] for k in range(3)]
            wh_ref[slot, 0] = centre_weight(w[0], w[1])
            for k in range(3):
                wh_ref[slot, 1 + k] = w[k]

    def get_w(r):
        if own(r):
            return [w_ref[r - ITERS, k] for k in range(4)]
        return [wh_ref[r if r < ITERS else r - rows, k] for k in range(4)]

    left, right = pl.ds(0, LANES), pl.ds(cols - LANES, LANES)
    for r in range(high):
        acc = None
        for s in range(samples):
            ref, i = (y_ref, r - ITERS) if own(r) else halo(r)
            v = jnp.where(l32 < SEG // 2, roll(ref[i, s, :, left], SEG * s + 4), roll(ref[i, s, :, right], SEG * s + 28))
            acc = v if acc is None else jnp.where(seg == s, v, acc)
        sy_ref[r] = acc
        for k in range(3):
            ref, i, g = (w_ref, r - ITERS, 1 + k) if own(r) else halo(r) + (samples + k,)
            v = jnp.where(l32 < SEG // 2, roll(ref[i, g, :, left], 4), roll(ref[i, g, :, right], 28))
            sw_ref[r, k] = replicate(v, seg)

    def sample(s, carry):
        def first_y(r):
            ref, i = (y_ref, r - ITERS) if own(r) else halo(r)
            return ref[i, s]

        source = first_y
        for step in range(ITERS):
            target = (p_ref, q_ref)[step % 2]

            def put(r, v, target=target, step=step):
                if step == ITERS - 1:
                    x_ref[r - ITERS, s] = v
                else:
                    target[r, s] = v

            stencil(high, source, get_w, step + 1, high - 1 - step, put)
            source = functools.partial(lambda r, target: target[r, s], target=target)
        return carry

    lax.fori_loop(0, samples, sample, 0)


def strip_kernel(x_ref, w_ref, sy_ref, sw_ref, left_ref, right_ref, out_ref, var_ref, sum_ref):
    rows, samples, levels, cols = x_ref.shape
    high = rows + 2 * ITERS
    lane, seg, l32 = lane_parts((levels, LANES))
    from_left, from_right = l32 < 4, l32 >= 28

    def get_w(r):
        w = [
            jnp.where(
                from_left,
                roll(left_ref[r], -4 * (k + 1)),
                jnp.where(from_right, roll(right_ref[r], 4 * (k + 1)), sw_ref[r, k]),
            )
            for k in range(3)
        ]
        return (centre_weight(w[0], w[1]), *w)

    weights = [get_w(r) for r in range(high)]
    field = {
        r: jnp.where(from_left, left_ref[r], jnp.where(from_right, right_ref[r], sy_ref[r]))
        for r in range(high)
    }
    for step in range(ITERS):
        new = {}
        stencil(high, field.__getitem__, weights.__getitem__, step + 1, high - 1 - step, new.__setitem__)
        field = new

    total, count = None, None
    for r in range(rows):
        strip = field[ITERS + r]
        for c in range(0, cols, LANES):
            lanes = pl.ds(c, LANES)
            square = None
            for s in range(samples):
                v = x_ref[r, s, :, lanes]
                if c == 0:
                    v = jnp.where(lane < 4, roll(strip, -(SEG * s + 4)), v)
                if c == cols - LANES:
                    v = jnp.where(lane >= LANES - 4, roll(strip, LANES - SEG * s - 28), v)
                out_ref[r, s, :, lanes] = v
                square = v * v if square is None else square + v * v
            var = square / samples
            var_ref[r, :, lanes] = var
            m = jnp.where(w_ref[r, 1, :, lanes] > 0, 1.0, 0.0)
            total = m * var if total is None else total + m * var
            count = m if count is None else count + m
    sum_ref[0:1] = jnp.sum(total, axis=0, keepdims=True)
    sum_ref[1:2] = jnp.sum(count, axis=0, keepdims=True)


def scale_kernel(x_ref, w_ref, var_ref, all_ref, out_ref, stage, sem):
    rows, samples, levels, cols = x_ref.shape
    sums = jnp.sum(jnp.sum(all_ref[...], axis=0), axis=1, keepdims=True)
    mean = sums[0:1] / sums[1:2]
    copies = []
    for c in range(cols // LANES):
        lanes = pl.ds(c * LANES, LANES)
        for r in range(rows):
            wet = w_ref[r, 1, :, lanes] > 0
            safe = jnp.where(wet, var_ref[r, :, lanes], 1.0)
            factor = jnp.where(wet, jnp.sqrt(mean / (safe + 1e-06)), 0.0)
            for s in range(samples):
                stage[c, s, pl.ds(r, levels, stride=rows)] = x_ref[r, s, :, lanes] * factor
        copies.append(pltpu.make_async_copy(stage.at[c], out_ref.at[:, :, lanes], sem.at[c]))
        copies[-1].start()
    for copy in copies:
        copy.wait()


def call(kernel, out, *args, scratch=(), flops=0, in_space=None, out_space=None):
    out = [o if isinstance(o, jax.ShapeDtypeStruct) else jax.ShapeDtypeStruct(o, F32) for o in out]
    scratch = [pltpu.VMEM(o, F32) if isinstance(o, tuple) else o for o in scratch]
    return pl.pallas_call(
        kernel,
        out_shape=out,
        in_specs=[pl.BlockSpec(memory_space=in_space or pltpu.VMEM)] * len(args),
        out_specs=[pl.BlockSpec(memory_space=out_space or pltpu.VMEM)] * len(out),
        scratch_shapes=scratch,
        cost_estimate=pl.CostEstimate(flops=flops, bytes_accessed=sum(a.size * 4 for a in args), transcendentals=0),
        compiler_params=pltpu.CompilerParams(vmem_limit_bytes=12 << 20),
        name=kernel.__name__,
    )(*args)


def shards(noise, diff_lat, diff_lon, shear, sea_mask):
    samples, levels, rows, cols = noise.shape
    high = rows + 2 * ITERS
    flat = [noise.reshape(samples, levels * rows, cols)] + [
        a.reshape(levels * rows, cols) for a in (diff_lat, diff_lon, shear, sea_mask)
    ]
    n_lat, n_lon = lax.axis_size("lat"), lax.axis_size("lon")
    up = [(i, i + 1) for i in range(n_lat - 1)]
    down = [(j, i) for i, j in up]
    east = [(i, (i + 1) % n_lon) for i in range(n_lon)]
    west = [(j, i) for i, j in east]

    halo = (ITERS, samples + 3, levels, cols)
    tiles = cols // LANES
    plane = (tiles, levels * rows, LANES)
    top, bottom, *staged = call(
        edge_kernel,
        [halo, halo, (tiles, samples, levels * rows, LANES)] + [plane] * 3 + [jax.ShapeDtypeStruct(plane, sea_mask.dtype)],
        *flat,
        scratch=[pltpu.SemaphoreType.DMA((tiles, 5))],
        in_space=pl.ANY,
    )
    after = lax.ppermute(top, "lat", down)
    before = lax.ppermute(bottom, "lat", up)
    y, w, own_msg = call(
        own_kernel,
        [(rows, samples, levels, cols), (rows, 4, levels, cols), (rows, levels, LANES)],
        *staged,
        flops=10**6,
    )
    (msg,) = call(join_kernel, [(high, levels, LANES)], own_msg, before, after)
    left = lax.ppermute(msg, "lon", east)
    right = lax.ppermute(msg, "lon", west)
    buffer = (high, samples, levels, cols)
    x, sy, sw = call(
        main_kernel,
        [y.shape, (high, levels, LANES), (high, 3, levels, LANES)],
        y,
        w,
        before,
        after,
        scratch=[(2 * ITERS, 4, levels, cols), buffer, buffer],
        flops=10**7,
    )
    x, var, part = call(
        strip_kernel, [y.shape, (rows, levels, cols), (2, LANES)], x, w, sy, sw, left, right
    )
    spread = jnp.broadcast_to(part, (n_lat * n_lon, 2, LANES))
    every = lax.all_to_all(spread, ("lat", "lon"), 0, 0, tiled=True)
    (out,) = call(
        scale_kernel,
        [(samples, levels * rows, cols)],
        x,
        w,
        var,
        every,
        scratch=[(tiles, samples, levels * rows, LANES), pltpu.SemaphoreType.DMA((tiles,))],
        out_space=pl.ANY,
    )
    sums = jnp.sum(every, axis=(0, 2))
    return out.reshape(noise.shape), sums[0] / sums[1]


def solution(mesh):
    grid = P(None, "lat", "lon")
    field = P(None, None, "lat", "lon")
    return jax.shard_map(
        shards,
        mesh=mesh,
        in_specs=(field, grid, grid, grid, grid),
        out_specs=(field, P()),
        check_vma=False,
    )
```

time: 103 us -> 47.7 us (0.46)
  blocking collectives: 43.2 us -> 16.6 us
  waiting for transfers between devices: 25.4 us -> 3.25 us
  other arithmetic: 15 us -> 0.15 us
  Pallas kernels: 0 us -> 11.6 us
  starting transfers between devices: 15.1 us -> 7.36 us
  local copies, waits for them, and re-layouts: 0.81 us -> 5.25 us
    psum x1 -> x0, blocking collectives: 43.2 us -> none  [shards(): lax.psum((jnp.sum(wet * var), jnp.sum(wet)), ('lat', 'lon'))]
    ppermute x8 -> x4, waiting for transfers between devices: 25.4 us -> 3.25 us  [the longest x1 3.24 us: shards(): after = lax.ppermute(top, 'lat', down)]
    all_to_all x0 -> x1, blocking collectives: none -> 16.6 us  [shards(): every = lax.all_to_all(spread, ('lat', 'lon'), 0, 0, tiled=True)]
    pallas_call x0 -> x6, Pallas kernels: none -> 11.6 us  [call(): pl.pallas_call(kernel, out_shape=out, in_specs=[pl.BlockSpec(memory_space...]
    mul x14 -> x0, other arithmetic: 10.3 us -> none  [the longest x12 9.35 us: adjoint_step(): product = weight * masked]
    ppermute x8 -> x4, starting transfers between devices: 15.1 us -> 7.36 us  [the longest x1 3.65 us: shards(): right = lax.ppermute(msg, 'lon', west)]
    unnamed x10, local copies, waits for them, and re-layouts: 0.03 us -> 4.65 us
    another operation x2 -> x0, other arithmetic: 2.04 us -> none  [shards(): stacked = jnp.stack([diff_lat, diff_lon, shear, wet], axis=0)]
  transfers between devices with their start and end apart: 8 -> 4, of which waited for: 5 -> 1; matrix products, arithmetic and copies ran while one was open for 3% -> 0% of each run, Pallas kernels for 0% -> 19%
where the time goes in v1:
time: 47.7 us; the launch traced here: 47.4 us
  blocking collectives  16.6 us (35%)
  Pallas kernels  11.6 us (24%)
  starting transfers between devices  7.36 us (15%)
  local copies, waits for them, and re-layouts  5.25 us (11%)
  waiting for transfers between devices  3.25 us (7%)
  between operations  3.2 us (7%)
    all_to_all x1, blocking collectives, shards(): every = lax.all_to_all(spread, ('lat', 'lon'), 0, 0, tiled=True)  16.6 us
    pallas_call x6, Pallas kernels, call(): pl.pallas_call(kernel, out_shape=out, in_specs=[pl.BlockSpec(memory_space...  11.6 us
    unnamed x10, local copies, waits for them, and re-layouts  4.65 us
    ppermute x1, starting transfers between devices, shards(): right = lax.ppermute(msg, 'lon', west)  3.65 us
    ppermute x1, waiting for transfers between devices, shards(): after = lax.ppermute(top, 'lat', down)  3.24 us
    ppermute x1, starting transfers between devices, shards(): before = lax.ppermute(bottom, 'lat', up)  2.41 us
    ppermute x1, starting transfers between devices, shards(): after = lax.ppermute(top, 'lat', down)  1.29 us
  transfers between devices with their start and end apart: 4, of which 1 were waited for; matrix products, arithmetic and copies ran while one was open for 0% of the time, Pallas kernels for 19%

profile of v1, /device:TPU:0, one launch (start us, length us, event | category | flops | bytes accessed | tf_op | source)
XLA Modules:
  0.0 47.4 jit_solution(11111764129307359249)
XLA Ops:
  0.6 0.0 copy-start
  0.6 1.0 %copy-done = f32[4,8,16,256]{3,2,1,0:T(8,128)S(1)} copy-done((f32[4,8,16,256]{3,2,1,0:T(8,128)S(1)}, f32[4,8,16,256]{3,2,1,0:T(8,128)}, u32[]{:S(2)}) %copy-start) | copy-done | bytes 524312
  1.7 0.0 copy-start.1
  1.7 0.9 %copy-done.1 = f32[8,16,256]{2,1,0:T(8,128)S(1)} copy-done((f32[8,16,256]{2,1,0:T(8,128)S(1)}, f32[8,16,256]{2,1,0:T(8,128)}, u32[]{:S(2)}) %copy-start.1) | copy-done | bytes 131096
  2.6 0.0 copy-start.2
  2.6 0.9 %copy-done.2 = f32[8,16,256]{2,1,0:T(8,128)S(1)} copy-done((f32[8,16,256]{2,1,0:T(8,128)S(1)}, f32[8,16,256]{2,1,0:T(8,128)}, u32[]{:S(2)}) %copy-start.2) | copy-done | bytes 131096
  3.5 0.0 copy-start.3
  3.5 0.9 %copy-done.3 = f32[8,16,256]{2,1,0:T(8,128)S(1)} copy-done((f32[8,16,256]{2,1,0:T(8,128)S(1)}, f32[8,16,256]{2,1,0:T(8,128)}, u32[]{:S(2)}) %copy-start.3) | copy-done | bytes 131096
  4.4 0.0 copy-start.4
  4.4 0.9 %copy-done.4 = s32[8,16,256]{2,1,0:T(8,128)S(1)} copy-done((s32[8,16,256]{2,1,0:T(8,128)S(1)}, s32[8,16,256]{2,1,0:T(8,128)}, u32[]{:S(2)}) %copy-start.4) | copy-done | bytes 131096
  5.3 0.4 edge_kernel.1
  5.7 2.4 %collective-permute-start = (f32[4,7,8,256]{3,2,1,0:T(8,128)S(1)}, f32[4,7,8,256]{3,2,1,0:T(8,128)S(1)}, u32[]{:S(2)}, u32[]{:S(2)}) collective-permute-start(f32[4,7,8,256]{3,2,1,0:T(8,128)S(1)} %get-tuple-element.25), channel_id=1, source_target_pairs={{0,4},{4,8},{8,12},{12,16},{16,20},{20,24},{24,28},{1,5},{5,9},{9,... | collective-permute-start | bytes 688136 | tf_op jit(solution)/shard_map/ppermute | solution.py:297
  8.1 1.3 %collective-permute-start.1 = (f32[4,7,8,256]{3,2,1,0:T(8,128)S(1)}, f32[4,7,8,256]{3,2,1,0:T(8,128)S(1)}, u32[]{:S(2)}, u32[]{:S(2)}) collective-permute-start(f32[4,7,8,256]{3,2,1,0:T(8,128)S(1)} %get-tuple-element.26), channel_id=1, source_target_pairs={{4,0},{8,4},{12,8},{16,12},{20,16},{24,20},{28,24},{5,1},{9,5},{13... | collective-permute-start | bytes 688136 | tf_op jit(solution)/shard_map/ppermute | solution.py:296
  9.4 0.9 %own_kernel.1 = (f32[16,4,8,256]{3,2,1,0:T(8,128)S(1)}, f32[16,4,8,256]{3,2,1,0:T(8,128)S(1)}, f32[16,8,128]{2,1,0:T(8,128)S(1)}) custom-call(f32[2,4,128,128]{3,2,1,0:T(8,128)S(1)} %get-tuple-element.18.n_ref, f32[2,128,128]{2,1,0:T(8,128)S(1)} %get-tuple-element.19.a_ref, f32[2,128,128]{2,1,0:T(8,128)S(1)} %get-tuple-element.20.b_ref, ...), custom_call_target="tpu_custom_call" | custom-call | flops 1000000 | bytes 1048576 | tf_op jit(solution)/shard_map/own_kernel/pallas_call | solution.py:262
  10.3 0.0 collective-permute-done.before_ref
  10.3 3.2 %collective-permute-done.1.after_ref = f32[4,7,8,256]{3,2,1,0:T(8,128)S(1)} collective-permute-done((f32[4,7,8,256]{3,2,1,0:T(8,128)S(1)}, f32[4,7,8,256]{3,2,1,0:T(8,128)S(1)}, u32[]{:S(2)}, u32[]{:S(2)}) %collective-permute-start.1) | collective-permute-done | bytes 229408 | tf_op jit(solution)/shard_map/ppermute | solution.py:296
  13.6 0.3 join_kernel.1
  13.8 3.7 %collective-permute-start.3 = (f32[24,8,128]{2,1,0:T(8,128)S(1)}, f32[24,8,128]{2,1,0:T(8,128)S(1)}, u32[]{:S(2)}, u32[]{:S(2)}) collective-permute-start(f32[24,8,128]{2,1,0:T(8,128)S(1)} %join_kernel.1), channel_id=1, source_target_pairs={{1,0},{2,1},{3,2},{0,3},{5,4},{6,5},{7,6},{4,7},{9,8},{10,9},{11,1... | collective-permute-start | bytes 294920 | tf_op jit(solution)/shard_map/ppermute | solution.py:306
  17.5 0.0 collective-permute-start.2
  17.5 8.2 %main_kernel.1 = (f32[16,4,8,256]{3,2,1,0:T(8,128)S(1)}, f32[24,8,128]{2,1,0:T(8,128)S(1)}, f32[24,3,8,128]{3,2,1,0:T(8,128)S(1)}) custom-call(f32[16,4,8,256]{3,2,1,0:T(8,128)S(1)} %get-tuple-element.23.y_ref, f32[16,4,8,256]{3,2,1,0:T(8,128)S(1)} %get-tuple-element.24.w_ref, f32[4,7,8,256]{3,2,1,0:T(8,128)S(1)} %collective-permute-done.before_ref, ...), custom_call_target="tpu_custom_call" | custom-call | flops 10000000 | bytes 1507328 | tf_op jit(solution)/shard_map/main_kernel/pallas_call | solution.py:262
  25.7 0.0 collective-permute-done.3.right_ref
  25.7 0.0 collective-permute-done.2.left_ref
  25.8 0.7 %strip_kernel.1 = (f32[16,4,8,256]{3,2,1,0:T(8,128)S(1)}, f32[16,8,256]{2,1,0:T(8,128)S(1)}, f32[2,128]{1,0:T(2,128)S(1)}) custom-call(f32[16,4,8,256]{3,2,1,0:T(8,128)S(1)} %get-tuple-element.27.x_ref, f32[16,4,8,256]{3,2,1,0:T(8,128)S(1)} %get-tuple-element.24.w_ref, f32[24,8,128]{2,1,0:T(8,128)S(1)} %get-tuple-element.28.sy_ref, ...), custom_call_target="tpu_custom_call" | custom-call | bytes 1638400 | tf_op jit(solution)/shard_map/strip_kernel/pallas_call | solution.py:262
  26.4 16.6 %all_to_all.5.all_ref = f32[32,2,128]{2,1,0:T(2,128)S(1)} all-to-all(f32[32,2,128]{2,1,0:T(2,128)S(1)} %broadcast_in_dim.3), channel_id=1, replica_groups=mesh['lat'=8,'lon'=4] {'lat','lon'}, dimensions={0} | all-to-all | bytes 65536 | tf_op jit(solution)/shard_map/all_to_all | solution.py:322
  43.1 0.1 reduce_sum.9
  43.2 0.6 %fusion = (f32[1]{0:T(128)}, f32[1]{0:T(128)}) fusion(f32[2]{0:T(128)S(1)} %reduce_sum.9), kind=kLoop, calls=%fused_computation | loop fusion | bytes 16 | tf_op jit(solution)/shard_map/slice | solution.py:334
  45.1 1.1 %scale_kernel.1 = f32[4,128,256]{2,1,0:T(8,128)} custom-call(f32[16,4,8,256]{3,2,1,0:T(8,128)S(1)} %get-tuple-element.31.x_ref, f32[16,4,8,256]{3,2,1,0:T(8,128)S(1)} %get-tuple-element.24.w_ref, f32[16,8,256]{2,1,0:T(8,128)S(1)} %get-tuple-element.32.var_ref, f32[32,2,128]{2,1,0:T(2,128)S(1)} %all_to_all.5.all_ref), custom_call_target="tpu_custom_call" | custom-call | bytes 1212416 | tf_op jit(solution)/shard_map/scale_kernel/pallas_call | solution.py:262
  (1 shorter events, 0.0 us)
Async XLA Ops:
  0.6 1.0 %copy-start = (f32[4,8,16,256]{3,2,1,0:T(8,128)S(1)}, f32[4,8,16,256]{3,2,1,0:T(8,128)}, u32[]{:S(2)}) copy-start(f32[4,8,16,256]{3,2,1,0:T(8,128)} %param.5) | copy-start | bytes 1572868
  1.7 0.9 %copy-start.1 = (f32[8,16,256]{2,1,0:T(8,128)S(1)}, f32[8,16,256]{2,1,0:T(8,128)}, u32[]{:S(2)}) copy-start(f32[8,16,256]{2,1,0:T(8,128)} %param.6) | copy-start | bytes 393220
  2.6 0.9 %copy-start.2 = (f32[8,16,256]{2,1,0:T(8,128)S(1)}, f32[8,16,256]{2,1,0:T(8,128)}, u32[]{:S(2)}) copy-start(f32[8,16,256]{2,1,0:T(8,128)} %param.7) | copy-start | bytes 393220
  3.5 0.9 %copy-start.3 = (f32[8,16,256]{2,1,0:T(8,128)S(1)}, f32[8,16,256]{2,1,0:T(8,128)}, u32[]{:S(2)}) copy-start(f32[8,16,256]{2,1,0:T(8,128)} %param.8) | copy-start | bytes 393220
  4.4 0.9 %copy-start.4 = (s32[8,16,256]{2,1,0:T(8,128)S(1)}, s32[8,16,256]{2,1,0:T(8,128)}, u32[]{:S(2)}) copy-start(s32[8,16,256]{2,1,0:T(8,128)} %param.9) | copy-start | bytes 393220
  5.7 4.6 %collective-permute-start = (f32[4,7,8,256]{3,2,1,0:T(8,128)S(1)}, f32[4,7,8,256]{3,2,1,0:T(8,128)S(1)}, u32[]{:S(2)}, u32[]{:S(2)}) collective-permute-start(f32[4,7,8,256]{3,2,1,0:T(8,128)S(1)} %get-tuple-element.25), channel_id=1, source_target_pairs={{0,4},{4,8},{8,12},{12,16},{16,20},{20,24},{24,28},{1,5},{5,9},{9,... | collective-permute-start | bytes 688136 | tf_op jit(solution)/shard_map/ppermute | solution.py:297
  8.1 5.5 %collective-permute-start.1 = (f32[4,7,8,256]{3,2,1,0:T(8,128)S(1)}, f32[4,7,8,256]{3,2,1,0:T(8,128)S(1)}, u32[]{:S(2)}, u32[]{:S(2)}) collective-permute-start(f32[4,7,8,256]{3,2,1,0:T(8,128)S(1)} %get-tuple-element.26), channel_id=1, source_target_pairs={{4,0},{8,4},{12,8},{16,12},{20,16},{24,20},{28,24},{5,1},{9,5},{13... | collective-permute-start | bytes 688136 | tf_op jit(solution)/shard_map/ppermute | solution.py:296
  13.8 11.9 %collective-permute-start.3 = (f32[24,8,128]{2,1,0:T(8,128)S(1)}, f32[24,8,128]{2,1,0:T(8,128)S(1)}, u32[]{:S(2)}, u32[]{:S(2)}) collective-permute-start(f32[24,8,128]{2,1,0:T(8,128)S(1)} %join_kernel.1), channel_id=1, source_target_pairs={{1,0},{2,1},{3,2},{0,3},{5,4},{6,5},{7,6},{4,7},{9,8},{10,9},{11,1... | collective-permute-start | bytes 294920 | tf_op jit(solution)/shard_map/ppermute | solution.py:306
  17.5 8.2 %collective-permute-start.2 = (f32[24,8,128]{2,1,0:T(8,128)S(1)}, f32[24,8,128]{2,1,0:T(8,128)S(1)}, u32[]{:S(2)}, u32[]{:S(2)}) collective-permute-start(f32[24,8,128]{2,1,0:T(8,128)S(1)} %join_kernel.1), channel_id=1, source_target_pairs={{0,1},{1,2},{2,3},{3,0},{4,5},{5,6},{6,7},{7,4},{8,9},{9,10},{10,1... | collective-permute-start | bytes 294920 | tf_op jit(solution)/shard_map/ppermute | solution.py:305

commit v2 on v1

--- a/solution.py
+++ b/solution.py
@@ -73,64 +73,110 @@
                     out[i, samples + k, :, lanes] = w[k]
 
 
-def message(get, samples, parts):
+BATCH = 4
+
+
+def replicate(values, seg):
+    turned = [roll(v, SEG) for v in values]
+    values = [jnp.where(seg == 1, t, v) for t, v in zip(turned, values)]
+    turned = [roll(v, 2 * SEG) for v in values]
+    return [jnp.where(seg >= 2, t, v) for t, v in zip(turned, values)]
+
+
+def line_up(gets, samples, parts, low, high):
     _, seg, l32 = parts
-    acc = None
-    for s in range(samples):
-        v = jnp.where(l32 < SEG // 2, roll(get(s, 1), SEG * s + 4), roll(get(s, 0), SEG * s + 28))
-        acc = v if acc is None else jnp.where(seg == s, v, acc)
-    w = None
-    for k in range(3):
-        v = jnp.where(l32 < SEG // 2, roll(get(samples + k, 1), 4 * k + 8), roll(get(samples + k, 0), 24 - 4 * k))
-        w = v if w is None else jnp.where((l32 // 4 == k + 1) | (l32 // 4 == 6 - k), v, w)
-    w = replicate(w, seg)
-    return jnp.where((l32 < 4) | (l32 >= 28), acc, w)
-
-
-def replicate(v, seg):
-    v = jnp.where(seg == 1, roll(v, SEG), v)
-    return jnp.where(seg >= 2, roll(v, 2 * SEG), v)
-
-
-def own_kernel(n_ref, a_ref, b_ref, s_ref, m_ref, y_ref, w_ref, msg_ref):
+    turned = [
+        [(roll(get(s, low), SEG * s + 4), roll(get(s, high), SEG * s + 28)) for s in range(samples)] for get in gets
+    ]
+    lines = []
+    for row in turned:
+        line = None
+        for s, (a, b) in enumerate(row):
+            v = jnp.where(l32 < SEG // 2, a, b)
+            line = v if line is None else jnp.where(seg == s, v, line)
+        lines.append(line)
+    return lines
+
+
+def messages(gets, samples, parts):
+    _, seg, l32 = parts
+    lines = line_up(gets, samples, parts, 1, 0)
+    turned = [
+        [(roll(get(samples + k, 1), 4 * k + 8), roll(get(samples + k, 0), 24 - 4 * k)) for k in range(3)] for get in gets
+    ]
+    packed = []
+    for row in turned:
+        line = None
+        for k, (a, b) in enumerate(row):
+            v = jnp.where(l32 < SEG // 2, a, b)
+            line = v if line is None else jnp.where((l32 // 4 == k + 1) | (l32 // 4 == 6 - k), v, line)
+        packed.append(line)
+    packed = replicate(packed, seg)
+    return [jnp.where((l32 < 4) | (l32 >= 28), a, b) for a, b in zip(lines, packed)]
+
+
+def strips(gets, samples, parts):
+    _, seg, l32 = parts
+    lines = line_up(gets, samples, parts, 0, 1)
+    turned = [(roll(get(samples + k, 0), 4), roll(get(samples + k, 1), 28)) for get in gets for k in range(3)]
+    weights = replicate([jnp.where(l32 < SEG // 2, a, b) for a, b in turned], seg)
+    return lines, [weights[3 * i : 3 * i + 3] for i in range(len(gets))]
+
+
+def own_kernel(n_ref, a_ref, b_ref, s_ref, m_ref, y_ref, w_ref, msg_ref, sy_ref, sw_ref):
     rows, samples, levels, cols = y_ref.shape
     parts = lane_parts((levels, LANES))
     tiles = cols // LANES
-    for r in range(rows):
+
+    def read(r):
         at = pl.ds(r, levels, stride=rows)
-        edge = {}
-        for c in range(tiles):
-            lanes = pl.ds(c * LANES, LANES)
-            vals = [n_ref[c, s, at] for s in range(samples)]
-            for s in range(samples):
-                y_ref[r, s, :, lanes] = vals[s]
-            w = cell_weights(a_ref[c, at], b_ref[c, at], s_ref[c, at], m_ref[c, at])
-            w_ref[r, 0, :, lanes] = centre_weight(w[0], w[1])
+        return [
+            [n_ref[c, s, at] for s in range(samples)]
+            + list(cell_weights(a_ref[c, at], b_ref[c, at], s_ref[c, at], m_ref[c, at]))
+            for c in range(tiles)
+        ]
+
+    for first in range(0, rows, BATCH):
+        batch = range(first, first + BATCH)
+        data = [read(r) for r in batch]
+        gets = [lambda g, side, row=row: row[side * (tiles - 1)][g] for row in data]
+        sent = messages(gets, samples, parts)
+        lines, weights = strips(gets, samples, parts)
+        for i, r in enumerate(batch):
+            for c in range(tiles):
+                lanes = pl.ds(c * LANES, LANES)
+                values = data[i][c]
+                for s in range(samples):
+                    y_ref[r, s, :, lanes] = values[s]
+                w_ref[r, 0, :, lanes] = centre_weight(values[samples], values[samples + 1])
+                for k in range(3):
+                    w_ref[r, 1 + k, :, lanes] = values[samples + k]
+            msg_ref[r] = sent[i]
+            sy_ref[r] = lines[i]
             for k in range(3):
-                w_ref[r, 1 + k, :, lanes] = w[k]
-            if c == 0:
-                edge[0] = vals + list(w)
-            if c == tiles - 1:
-                edge[1] = vals + list(w)
-        msg_ref[r] = message(lambda g, side: edge[side][g], samples, parts)
+                sw_ref[r, k] = weights[i][k]
+
+
+def halo_gets(ref):
+    last = ref.shape[3] - LANES
+    return [lambda g, side, i=i: ref[i, g, :, pl.ds(side * last, LANES)] for i in range(ITERS)]
 
 
 def join_kernel(own_ref, before_ref, after_ref, msg_ref):
     rows = own_ref.shape[0]
-    samples, cols = before_ref.shape[1] - 3, before_ref.shape[3]
+    samples = before_ref.shape[1] - 3
     parts = lane_parts(own_ref.shape[1:])
+    sent = messages(halo_gets(before_ref) + halo_gets(after_ref), samples, parts)
     msg_ref[ITERS : ITERS + rows] = own_ref[...]
     for i in range(ITERS):
-        for ref, to in ((before_ref, i), (after_ref, ITERS + rows + i)):
-            msg_ref[to] = message(
-                lambda g, side: ref[i, g, :, pl.ds(side * (cols - LANES), LANES)], samples, parts
-            )
-
-
-def main_kernel(y_ref, w_ref, before_ref, after_ref, x_ref, sy_ref, sw_ref, wh_ref, p_ref, q_ref):
+        msg_ref[i] = sent[i]
+        msg_ref[ITERS + rows + i] = sent[ITERS + i]
+
+
+def main_kernel(y_ref, w_ref, before_ref, after_ref, x_ref, hy_ref, hw_ref, wh_ref, p_ref, q_ref):
     rows, samples, levels, cols = y_ref.shape
     high = rows + 2 * ITERS
-    _, seg, l32 = lane_parts((levels, LANES))
+    parts = lane_parts((levels, LANES))
 
     def halo(r):
         return (before_ref, r) if r < ITERS else (after_ref, r - ITERS - rows)
@@ -152,18 +198,12 @@
             return [w_ref[r - ITERS, k] for k in range(4)]
         return [wh_ref[r if r < ITERS else r - rows, k] for k in range(4)]
 
-    left, right = pl.ds(0, LANES), pl.ds(cols - LANES, LANES)
-    for r in range(high):
-        acc = None
-        for s in range(samples):
-            ref, i = (y_ref, r - ITERS) if own(r) else halo(r)
-            v = jnp.where(l32 < SEG // 2, roll(ref[i, s, :, left], SEG * s + 4), roll(ref[i, s, :, right], SEG * s + 28))
-            acc = v if acc is None else jnp.where(seg == s, v, acc)
-        sy_ref[r] = acc
-        for k in range(3):
-            ref, i, g = (w_ref, r - ITERS, 1 + k) if own(r) else halo(r) + (samples + k,)
-            v = jnp.where(l32 < SEG // 2, roll(ref[i, g, :, left], 4), roll(ref[i, g, :, right], 28))
-            sw_ref[r, k] = replicate(v, seg)
+    for side, ref in enumerate((before_ref, after_ref)):
+        lines, weights = strips(halo_gets(ref), samples, parts)
+        for i in range(ITERS):
+            hy_ref[side * ITERS + i] = lines[i]
+            for k in range(3):
+                hw_ref[side * ITERS + i, k] = weights[i][k]
 
     def sample(s, carry):
         def first_y(r):
@@ -187,28 +227,35 @@
     lax.fori_loop(0, samples, sample, 0)
 
 
-def strip_kernel(x_ref, w_ref, sy_ref, sw_ref, left_ref, right_ref, out_ref, var_ref, sum_ref):
+def strip_kernel(x_ref, w_ref, sy_ref, sw_ref, hy_ref, hw_ref, left_ref, right_ref, out_ref, var_ref, sum_ref):
     rows, samples, levels, cols = x_ref.shape
     high = rows + 2 * ITERS
     lane, seg, l32 = lane_parts((levels, LANES))
     from_left, from_right = l32 < 4, l32 >= 28
 
+    def strip_at(r):
+        if ITERS <= r < ITERS + rows:
+            return sy_ref, sw_ref, r - ITERS
+        return hy_ref, hw_ref, r if r < ITERS else r - rows
+
+    def get_y(r):
+        ref, _, i = strip_at(r)
+        return jnp.where(from_left, left_ref[r], jnp.where(from_right, right_ref[r], ref[i]))
+
     def get_w(r):
+        _, ref, i = strip_at(r)
         w = [
             jnp.where(
                 from_left,
                 roll(left_ref[r], -4 * (k + 1)),
-                jnp.where(from_right, roll(right_ref[r], 4 * (k + 1)), sw_ref[r, k]),
+                jnp.where(from_right, roll(right_ref[r], 4 * (k + 1)), ref[i, k]),
             )
             for k in range(3)
         ]
         return (centre_weight(w[0], w[1]), *w)
 
     weights = [get_w(r) for r in range(high)]
-    field = {
-        r: jnp.where(from_left, left_ref[r], jnp.where(from_right, right_ref[r], sy_ref[r]))
-        for r in range(high)
-    }
+    field = {r: get_y(r) for r in range(high)}
     for step in range(ITERS):
         new = {}
         stencil(high, field.__getitem__, weights.__getitem__, step + 1, high - 1 - step, new.__setitem__)
@@ -237,10 +284,11 @@
     sum_ref[1:2] = jnp.sum(count, axis=0, keepdims=True)
 
 
-def scale_kernel(x_ref, w_ref, var_ref, all_ref, out_ref, stage, sem):
+def scale_kernel(x_ref, w_ref, var_ref, all_ref, out_ref, mean_ref, stage, sem):
     rows, samples, levels, cols = x_ref.shape
     sums = jnp.sum(jnp.sum(all_ref[...], axis=0), axis=1, keepdims=True)
     mean = sums[0:1] / sums[1:2]
+    mean_ref[...] = mean
     copies = []
     for c in range(cols // LANES):
         lanes = pl.ds(c * LANES, LANES)
@@ -263,7 +311,7 @@
         kernel,
         out_shape=out,
         in_specs=[pl.BlockSpec(memory_space=in_space or pltpu.VMEM)] * len(args),
-        out_specs=[pl.BlockSpec(memory_space=out_space or pltpu.VMEM)] * len(out),
+        out_specs=[pl.BlockSpec(memory_space=m) for m in out_space or [pltpu.VMEM] * len(out)],
         scratch_shapes=scratch,
         cost_estimate=pl.CostEstimate(flops=flops, bytes_accessed=sum(a.size * 4 for a in args), transcendentals=0),
         compiler_params=pltpu.CompilerParams(vmem_limit_bytes=12 << 20),
@@ -286,18 +334,19 @@
     halo = (ITERS, samples + 3, levels, cols)
     tiles = cols // LANES
     plane = (tiles, levels * rows, LANES)
+    flat = [pltpu.with_memory_space_constraint(a, pltpu.HBM) for a in flat]
     top, bottom, *staged = call(
         edge_kernel,
         [halo, halo, (tiles, samples, levels * rows, LANES)] + [plane] * 3 + [jax.ShapeDtypeStruct(plane, sea_mask.dtype)],
         *flat,
         scratch=[pltpu.SemaphoreType.DMA((tiles, 5))],
-        in_space=pl.ANY,
+        in_space=pltpu.HBM,
     )
     after = lax.ppermute(top, "lat", down)
     before = lax.ppermute(bottom, "lat", up)
-    y, w, own_msg = call(
+    y, w, own_msg, sy, sw = call(
         own_kernel,
-        [(rows, samples, levels, cols), (rows, 4, levels, cols), (rows, levels, LANES)],
+        [(rows, samples, levels, cols), (rows, 4, levels, cols), (rows, levels, LANES), (rows, levels, LANES), (rows, 3, levels, LANES)],
         *staged,
         flops=10**6,
     )
@@ -305,9 +354,9 @@
     left = lax.ppermute(msg, "lon", east)
     right = lax.ppermute(msg, "lon", west)
     buffer = (high, samples, levels, cols)
-    x, sy, sw = call(
+    x, hy, hw = call(
         main_kernel,
-        [y.shape, (high, levels, LANES), (high, 3, levels, LANES)],
+        [y.shape, (2 * ITERS, levels, LANES), (2 * ITERS, 3, levels, LANES)],
         y,
         w,
         before,
@@ -316,22 +365,21 @@
         flops=10**7,
     )
     x, var, part = call(
-        strip_kernel, [y.shape, (rows, levels, cols), (2, LANES)], x, w, sy, sw, left, right
+        strip_kernel, [y.shape, (rows, levels, cols), (2, LANES)], x, w, sy, sw, hy, hw, left, right
     )
     spread = jnp.broadcast_to(part, (n_lat * n_lon, 2, LANES))
     every = lax.all_to_all(spread, ("lat", "lon"), 0, 0, tiled=True)
-    (out,) = call(
+    out, mean = call(
         scale_kernel,
-        [(samples, levels * rows, cols)],
+        [(samples, levels * rows, cols), (1, 1)],
         x,
         w,
         var,
         every,
         scratch=[(tiles, samples, levels * rows, LANES), pltpu.SemaphoreType.DMA((tiles,))],
-        out_space=pl.ANY,
-    )
-    sums = jnp.sum(every, axis=(0, 2))
-    return out.reshape(noise.shape), sums[0] / sums[1]
+        out_space=[pl.ANY, pltpu.VMEM],
+    )
+    return out.reshape(noise.shape), mean.reshape(())
 
 
 def solution(mesh):

time: 47.7 us -> 36.4 us (0.76)
  local copies, waits for them, and re-layouts: 5.25 us -> 0.01 us
  waiting for transfers between devices: 3.25 us -> 7.7 us
  Pallas kernels: 11.6 us -> 7.61 us
  blocking collectives: 16.6 us -> 12.8 us
  between operations: 3.2 us -> 0.69 us
    ppermute x1, waiting for transfers between devices: 0.01 us -> 4.85 us  [shards(): left = lax.ppermute(msg, 'lon', east)]
    unnamed x10 -> x0, local copies, waits for them, and re-layouts: 4.65 us -> none
    pallas_call x6, Pallas kernels: 11.6 us -> 7.61 us  [call(): pl.pallas_call(kernel, out_shape=out, in_specs=[pl.BlockSpec(memory_space...]
    all_to_all x1, blocking collectives: 16.6 us -> 12.8 us  [shards(): every = lax.all_to_all(spread, ('lat', 'lon'), 0, 0, tiled=True)]
    slice x1 -> x0, local copies, waits for them, and re-layouts: 0.59 us -> none  [shards(): return (out.reshape(noise.shape), sums[0] / sums[1])]
    ppermute x1, waiting for transfers between devices: 3.24 us -> 2.69 us  [shards(): after = lax.ppermute(top, 'lat', down)]
  transfers between devices with their start and end apart: 4 -> 4, of which waited for: 1 -> 3; matrix products, arithmetic and copies ran while one was open for 0% -> 0% of each run, Pallas kernels for 19% -> 10%
where the time goes in v2:
time: 36.4 us; the launch traced here: 36.2 us
  blocking collectives  12.8 us (35%)
  waiting for transfers between devices  7.7 us (21%)
  Pallas kernels  7.61 us (21%)
  starting transfers between devices  7.36 us (20%)
  between operations  0.69 us (2%)
    all_to_all x1, blocking collectives, shards(): every = lax.all_to_all(spread, ('lat', 'lon'), 0, 0, tiled=True)  12.8 us
    pallas_call x6, Pallas kernels, call(): pl.pallas_call(kernel, out_shape=out, in_specs=[pl.BlockSpec(memory_space...  7.61 us
    ppermute x1, waiting for transfers between devices, shards(): left = lax.ppermute(msg, 'lon', east)  4.85 us
    ppermute x1, starting transfers between devices, shards(): right = lax.ppermute(msg, 'lon', west)  3.65 us
    ppermute x1, waiting for transfers between devices, shards(): after = lax.ppermute(top, 'lat', down)  2.69 us
    ppermute x1, starting transfers between devices, shards(): before = lax.ppermute(bottom, 'lat', up)  2.41 us
    ppermute x1, starting transfers between devices, shards(): after = lax.ppermute(top, 'lat', down)  1.29 us
  transfers between devices with their start and end apart: 4, of which 3 were waited for; matrix products, arithmetic and copies ran while one was open for 0% of the time, Pallas kernels for 10%

profile of v2, /device:TPU:0, one launch (start us, length us, event | category | flops | bytes accessed | tf_op | source)
XLA Modules:
  0.0 36.2 jit_solution(17232093634935627598)
XLA Ops:
  0.6 1.5 %edge_kernel.1 = (f32[4,7,8,256]{3,2,1,0:T(8,128)S(1)}, f32[4,7,8,256]{3,2,1,0:T(8,128)S(1)}, f32[2,4,128,128]{3,2,1,0:T(8,128)S(1)}, f32[2,128,128]{2,1,0:T(8,1...) custom-call(f32[4,128,256]{2,1,0:T(8,128)} %bitcast.7, ...), custom_call_target="tpu_custom_call" | custom-call | bytes 1048576 | tf_op jit(solution)/shard_map/edge_kernel/pallas_call | solution.py:310
  2.2 2.4 %collective-permute-start = (f32[4,7,8,256]{3,2,1,0:T(8,128)S(1)}, f32[4,7,8,256]{3,2,1,0:T(8,128)S(1)}, u32[]{:S(2)}, u32[]{:S(2)}) collective-permute-start(f32[4,7,8,256]{3,2,1,0:T(8,128)S(1)} %get-tuple-element.29), channel_id=1, source_target_pairs={{0,4},{4,8},{8,12},{12,16},{16,20},{20,24},{24,28},{1,5},{5,9},{9,... | collective-permute-start | bytes 688136 | tf_op jit(solution)/shard_map/ppermute | solution.py:346
  4.6 1.3 %collective-permute-start.1 = (f32[4,7,8,256]{3,2,1,0:T(8,128)S(1)}, f32[4,7,8,256]{3,2,1,0:T(8,128)S(1)}, u32[]{:S(2)}, u32[]{:S(2)}) collective-permute-start(f32[4,7,8,256]{3,2,1,0:T(8,128)S(1)} %get-tuple-element.30), channel_id=1, source_target_pairs={{4,0},{8,4},{12,8},{16,12},{20,16},{24,20},{28,24},{5,1},{9,5},{13... | collective-permute-start | bytes 688136 | tf_op jit(solution)/shard_map/ppermute | solution.py:345
  5.9 1.5 %own_kernel.1 = (f32[16,4,8,256]{3,2,1,0:T(8,128)S(1)}, f32[16,4,8,256]{3,2,1,0:T(8,128)S(1)}, f32[16,8,128]{2,1,0:T(8,128)S(1)}, f32[16,8,128]{2,1,0:T(8,128)S(1)}, f32[16,3,8,128]{3,2,1,0:T(8,128)S(1)}) custom-call(f32[2,4,128,128]{3,2,1,0:T(8,128)S(1)} %get-tuple-element.22.n_ref, f32[2,128,128]{2,1,0:T(8,128)S(1)} %get-tuple-element.23.a_ref, ...), custom_call_target="tpu_custom_call" | custom-call | flops 1000000 | bytes 1048576 | tf_op jit(solution)/shard_map/own_kernel/pallas_call | solution.py:310
  7.4 0.0 collective-permute-done.before_ref
  7.4 2.7 %collective-permute-done.1.after_ref = f32[4,7,8,256]{3,2,1,0:T(8,128)S(1)} collective-permute-done((f32[4,7,8,256]{3,2,1,0:T(8,128)S(1)}, f32[4,7,8,256]{3,2,1,0:T(8,128)S(1)}, u32[]{:S(2)}, u32[]{:S(2)}) %collective-permute-start.1) | collective-permute-done | bytes 229408 | tf_op jit(solution)/shard_map/ppermute | solution.py:345
  10.1 0.3 join_kernel.1
  10.4 3.7 %collective-permute-start.3 = (f32[24,8,128]{2,1,0:T(8,128)S(1)}, f32[24,8,128]{2,1,0:T(8,128)S(1)}, u32[]{:S(2)}, u32[]{:S(2)}) collective-permute-start(f32[24,8,128]{2,1,0:T(8,128)S(1)} %join_kernel.1), channel_id=1, source_target_pairs={{1,0},{2,1},{3,2},{0,3},{5,4},{6,5},{7,6},{4,7},{9,8},{10,9},{11,1... | collective-permute-start | bytes 294920 | tf_op jit(solution)/shard_map/ppermute | solution.py:355
  14.0 0.0 collective-permute-start.2
  14.0 2.0 %main_kernel.1 = (f32[16,4,8,256]{3,2,1,0:T(8,128)S(1)}, f32[8,8,128]{2,1,0:T(8,128)S(1)}, f32[8,3,8,128]{3,2,1,0:T(8,128)S(1)}) custom-call(f32[16,4,8,256]{3,2,1,0:T(8,128)S(1)} %get-tuple-element.27.y_ref, f32[16,4,8,256]{3,2,1,0:T(8,128)S(1)} %get-tuple-element.28.w_ref, f32[4,7,8,256]{3,2,1,0:T(8,128)S(1)} %collective-permute-done.before_ref, ...), custom_call_target="tpu_custom_call" | custom-call | flops 10000000 | bytes 1507328 | tf_op jit(solution)/shard_map/main_kernel/pallas_call | solution.py:310
  16.1 0.2 collective-permute-done.3.right_ref
  16.2 4.8 %collective-permute-done.2.left_ref = f32[24,8,128]{2,1,0:T(8,128)S(1)} collective-permute-done((f32[24,8,128]{2,1,0:T(8,128)S(1)}, f32[24,8,128]{2,1,0:T(8,128)S(1)}, u32[]{:S(2)}, u32[]{:S(2)}) %collective-permute-start.2) | collective-permute-done | bytes 98336 | tf_op jit(solution)/shard_map/ppermute | solution.py:354
  21.1 0.7 %strip_kernel.1 = (f32[16,4,8,256]{3,2,1,0:T(8,128)S(1)}, f32[16,8,256]{2,1,0:T(8,128)S(1)}, f32[2,128]{1,0:T(2,128)S(1)}) custom-call(f32[16,4,8,256]{3,2,1,0:T(8,128)S(1)} %get-tuple-element.31.x_ref, f32[16,4,8,256]{3,2,1,0:T(8,128)S(1)} %get-tuple-element.28.w_ref, f32[16,8,128]{2,1,0:T(8,128)S(1)} %get-tuple-element.32.sy_ref, ...), custom_call_target="tpu_custom_call" | custom-call | bytes 1638400 | tf_op jit(solution)/shard_map/strip_kernel/pallas_call | solution.py:310
  21.7 12.8 %all_to_all.5.all_ref = f32[32,2,128]{2,1,0:T(2,128)S(1)} all-to-all(f32[32,2,128]{2,1,0:T(2,128)S(1)} %broadcast_in_dim.3), channel_id=1, replica_groups=mesh['lat'=8,'lon'=4] {'lat','lon'}, dimensions={0} | all-to-all | bytes 65536 | tf_op jit(solution)/shard_map/all_to_all | solution.py:371
  34.5 1.6 %scale_kernel.1 = (f32[4,128,256]{2,1,0:T(8,128)}, f32[1,1]{1,0:T(1,128)}) custom-call(f32[16,4,8,256]{3,2,1,0:T(8,128)S(1)} %get-tuple-element.37.x_ref, f32[16,4,8,256]{3,2,1,0:T(8,128)S(1)} %get-tuple-element.28.w_ref, f32[16,8,256]{2,1,0:T(8,128)S(1)} %get-tuple-element.38.var_ref, f32[32,2,128]{2,1,0:T(2,128)S(1)} %all_to_all.5.all_ref), custom_call_target="tpu_custom_call" | custom-call | bytes 1212416 | tf_op jit(solution)/shard_map/scale_kernel/pallas_call | solution.py:310
  (1 shorter events, 0.0 us)
Async XLA Ops:
  2.2 5.2 %collective-permute-start = (f32[4,7,8,256]{3,2,1,0:T(8,128)S(1)}, f32[4,7,8,256]{3,2,1,0:T(8,128)S(1)}, u32[]{:S(2)}, u32[]{:S(2)}) collective-permute-start(f32[4,7,8,256]{3,2,1,0:T(8,128)S(1)} %get-tuple-element.29), channel_id=1, source_target_pairs={{0,4},{4,8},{8,12},{12,16},{16,20},{20,24},{24,28},{1,5},{5,9},{9,... | collective-permute-start | bytes 688136 | tf_op jit(solution)/shard_map/ppermute | solution.py:346
  4.6 5.5 %collective-permute-start.1 = (f32[4,7,8,256]{3,2,1,0:T(8,128)S(1)}, f32[4,7,8,256]{3,2,1,0:T(8,128)S(1)}, u32[]{:S(2)}, u32[]{:S(2)}) collective-permute-start(f32[4,7,8,256]{3,2,1,0:T(8,128)S(1)} %get-tuple-element.30), channel_id=1, source_target_pairs={{4,0},{8,4},{12,8},{16,12},{20,16},{24,20},{28,24},{5,1},{9,5},{13... | collective-permute-start | bytes 688136 | tf_op jit(solution)/shard_map/ppermute | solution.py:345
  10.4 5.9 %collective-permute-start.3 = (f32[24,8,128]{2,1,0:T(8,128)S(1)}, f32[24,8,128]{2,1,0:T(8,128)S(1)}, u32[]{:S(2)}, u32[]{:S(2)}) collective-permute-start(f32[24,8,128]{2,1,0:T(8,128)S(1)} %join_kernel.1), channel_id=1, source_target_pairs={{1,0},{2,1},{3,2},{0,3},{5,4},{6,5},{7,6},{4,7},{9,8},{10,9},{11,1... | collective-permute-start | bytes 294920 | tf_op jit(solution)/shard_map/ppermute | solution.py:355
  14.0 7.1 %collective-permute-start.2 = (f32[24,8,128]{2,1,0:T(8,128)S(1)}, f32[24,8,128]{2,1,0:T(8,128)S(1)}, u32[]{:S(2)}, u32[]{:S(2)}) collective-permute-start(f32[24,8,128]{2,1,0:T(8,128)S(1)} %join_kernel.1), channel_id=1, source_target_pairs={{0,1},{1,2},{2,3},{3,0},{4,5},{5,6},{6,7},{7,4},{8,9},{9,10},{10,1... | collective-permute-start | bytes 294920 | tf_op jit(solution)/shard_map/ppermute | solution.py:354

commit v3 on v2

--- a/solution.py
+++ b/solution.py
@@ -48,7 +48,7 @@
         prev, here = here, after
 
 
-def edge_kernel(n_ref, a_ref, b_ref, s_ref, m_ref, top_ref, bot_ref, n_to, a_to, b_to, s_to, m_to, sem):
+def edge_kernel(n_ref, a_ref, b_ref, s_ref, m_ref, top_ref, bot_ref, first_ref, last_ref, n_to, a_to, b_to, s_to, m_to, sem):
     samples, levels, tiles = n_ref.shape[0], top_ref.shape[2], n_to.shape[0]
     rows = n_ref.shape[1] // levels
     copies = []
@@ -71,6 +71,9 @@
                 w = cell_weights(a_to[c, at], b_to[c, at], s_to[c, at], m_to[c, at])
                 for k in range(3):
                     out[i, samples + k, :, lanes] = w[k]
+    parts = lane_parts((levels, LANES))
+    for out, ref in ((first_ref, top_ref), (last_ref, bot_ref)):
+        out[0], out[1] = messages(halo_gets(ref), samples, parts)
 
 
 BATCH = 4
@@ -99,20 +102,30 @@
 
 
 def messages(gets, samples, parts):
-    _, seg, l32 = parts
-    lines = line_up(gets, samples, parts, 1, 0)
-    turned = [
-        [(roll(get(samples + k, 1), 4 * k + 8), roll(get(samples + k, 0), 24 - 4 * k)) for k in range(3)] for get in gets
-    ]
-    packed = []
-    for row in turned:
-        line = None
-        for k, (a, b) in enumerate(row):
-            v = jnp.where(l32 < SEG // 2, a, b)
-            line = v if line is None else jnp.where((l32 // 4 == k + 1) | (l32 // 4 == 6 - k), v, line)
-        packed.append(line)
-    packed = replicate(packed, seg)
-    return [jnp.where((l32 < 4) | (l32 >= 28), a, b) for a, b in zip(lines, packed)]
+    lane = parts[0]
+    east = west = None
+    for j, get in enumerate(gets):
+        for g in range(samples + 3):
+            last = roll(get(g, 1), SEG * j + 4 * g + 4)
+            first = roll(get(g, 0), SEG * j + 28 - 4 * g)
+            east = last if east is None else jnp.where(lane // 4 == 8 * j + g, last, east)
+            west = first if west is None else jnp.where(lane // 4 == 8 * j + 7 - g, first, west)
+    return east, west
+
+
+def unpack(tile, samples, parts, sign):
+    _, seg, _ = parts
+    turned = [roll(tile, SEG * q) for q in range(4)]
+    rows = []
+    for j in range(4):
+        every = turned[(0 - j) % 4]
+        for q in range(1, 4):
+            every = jnp.where(seg == q, turned[(q - j) % 4], every)
+        line = every
+        for s in range(1, samples):
+            line = jnp.where(seg == s, roll(every, -sign * 4 * s), line)
+        rows.append((line, [roll(every, -sign * 4 * (samples + k)) for k in range(3)]))
+    return rows
 
 
 def strips(gets, samples, parts):
@@ -140,8 +153,9 @@
         batch = range(first, first + BATCH)
         data = [read(r) for r in batch]
         gets = [lambda g, side, row=row: row[side * (tiles - 1)][g] for row in data]
-        sent = messages(gets, samples, parts)
         lines, weights = strips(gets, samples, parts)
+        if 0 < first < rows - BATCH:
+            msg_ref[0, first // BATCH - 1], msg_ref[1, first // BATCH - 1] = messages(gets, samples, parts)
         for i, r in enumerate(batch):
             for c in range(tiles):
                 lanes = pl.ds(c * LANES, LANES)
@@ -151,7 +165,6 @@
                 w_ref[r, 0, :, lanes] = centre_weight(values[samples], values[samples + 1])
                 for k in range(3):
                     w_ref[r, 1 + k, :, lanes] = values[samples + k]
-            msg_ref[r] = sent[i]
             sy_ref[r] = lines[i]
             for k in range(3):
                 sw_ref[r, k] = weights[i][k]
@@ -160,17 +173,6 @@
 def halo_gets(ref):
     last = ref.shape[3] - LANES
     return [lambda g, side, i=i: ref[i, g, :, pl.ds(side * last, LANES)] for i in range(ITERS)]
-
-
-def join_kernel(own_ref, before_ref, after_ref, msg_ref):
-    rows = own_ref.shape[0]
-    samples = before_ref.shape[1] - 3
-    parts = lane_parts(own_ref.shape[1:])
-    sent = messages(halo_gets(before_ref) + halo_gets(after_ref), samples, parts)
-    msg_ref[ITERS : ITERS + rows] = own_ref[...]
-    for i in range(ITERS):
-        msg_ref[i] = sent[i]
-        msg_ref[ITERS + rows + i] = sent[ITERS + i]
 
 
 def main_kernel(y_ref, w_ref, before_ref, after_ref, x_ref, hy_ref, hw_ref, wh_ref, p_ref, q_ref):
@@ -230,7 +232,8 @@
 def strip_kernel(x_ref, w_ref, sy_ref, sw_ref, hy_ref, hw_ref, left_ref, right_ref, out_ref, var_ref, sum_ref):
     rows, samples, levels, cols = x_ref.shape
     high = rows + 2 * ITERS
-    lane, seg, l32 = lane_parts((levels, LANES))
+    parts = lane_parts((levels, LANES))
+    lane, _, l32 = parts
     from_left, from_right = l32 < 4, l32 >= 28
 
     def strip_at(r):
@@ -238,19 +241,17 @@
             return sy_ref, sw_ref, r - ITERS
         return hy_ref, hw_ref, r if r < ITERS else r - rows
 
+    lefts = [row for q in range(high // 4) for row in unpack(left_ref[q], samples, parts, 1)]
+    rights = [row for q in range(high // 4) for row in unpack(right_ref[q], samples, parts, -1)]
+
     def get_y(r):
         ref, _, i = strip_at(r)
-        return jnp.where(from_left, left_ref[r], jnp.where(from_right, right_ref[r], ref[i]))
+        return jnp.where(from_left, lefts[r][0], jnp.where(from_right, rights[r][0], ref[i]))
 
     def get_w(r):
         _, ref, i = strip_at(r)
         w = [
-            jnp.where(
-                from_left,
-                roll(left_ref[r], -4 * (k + 1)),
-                jnp.where(from_right, roll(right_ref[r], 4 * (k + 1)), ref[i, k]),
-            )
-            for k in range(3)
+            jnp.where(from_left, lefts[r][1][k], jnp.where(from_right, rights[r][1][k], ref[i, k])) for k in range(3)
         ]
         return (centre_weight(w[0], w[1]), *w)
 
@@ -335,24 +336,33 @@
     tiles = cols // LANES
     plane = (tiles, levels * rows, LANES)
     flat = [pltpu.with_memory_space_constraint(a, pltpu.HBM) for a in flat]
-    top, bottom, *staged = call(
+    corner = (2, levels, LANES)
+    top, bottom, first, last, *staged = call(
         edge_kernel,
-        [halo, halo, (tiles, samples, levels * rows, LANES)] + [plane] * 3 + [jax.ShapeDtypeStruct(plane, sea_mask.dtype)],
+        [halo, halo, corner, corner, (tiles, samples, levels * rows, LANES)]
+        + [plane] * 3
+        + [jax.ShapeDtypeStruct(plane, sea_mask.dtype)],
         *flat,
         scratch=[pltpu.SemaphoreType.DMA((tiles, 5))],
         in_space=pltpu.HBM,
     )
+    last_before = lax.ppermute(last, "lat", up)
+    first_after = lax.ppermute(first, "lat", down)
+    before = lax.ppermute(bottom, "lat", up)
     after = lax.ppermute(top, "lat", down)
-    before = lax.ppermute(bottom, "lat", up)
+    strip = (rows, levels, LANES)
     y, w, own_msg, sy, sw = call(
         own_kernel,
-        [(rows, samples, levels, cols), (rows, 4, levels, cols), (rows, levels, LANES), (rows, levels, LANES), (rows, 3, levels, LANES)],
+        [(rows, samples, levels, cols), (rows, 4, levels, cols), (2, rows // 4 - 2, levels, LANES), strip, (rows, 3, levels, LANES)],
         *staged,
         flops=10**6,
     )
-    (msg,) = call(join_kernel, [(high, levels, LANES)], own_msg, before, after)
-    left = lax.ppermute(msg, "lon", east)
-    right = lax.ppermute(msg, "lon", west)
+    sent = [
+        jnp.concatenate([last_before[d : d + 1], first[d : d + 1], own_msg[d], last[d : d + 1], first_after[d : d + 1]])
+        for d in range(2)
+    ]
+    left = lax.ppermute(sent[0], "lon", east)
+    right = lax.ppermute(sent[1], "lon", west)
     buffer = (high, samples, levels, cols)
     x, hy, hw = call(
         main_kernel,

time: 36.4 us -> 39 us (1.071)
  waiting for transfers between devices: 7.7 us -> 0.02 us
  starting transfers between devices: 7.36 us -> 14 us
  blocking collectives: 12.8 us -> 16.3 us
    ppermute x2 -> x4, waiting for transfers between devices: 5 us -> 0.01 us  [the longest x1 0.01 us: shards(): last_before = lax.ppermute(last, 'lat', up)]
    ppermute x2 -> x4, starting transfers between devices: 3.66 us -> 7.57 us  [the longest x1 2.4 us: shards(): last_before = lax.ppermute(last, 'lat', up)]
    all_to_all x1, blocking collectives: 12.8 us -> 16.3 us  [shards(): every = lax.all_to_all(spread, ('lat', 'lon'), 0, 0, tiled=True)]
    ppermute x1, starting transfers between devices: 2.41 us -> 5.14 us  [shards(): before = lax.ppermute(bottom, 'lat', up)]
    ppermute x1, waiting for transfers between devices: 2.69 us -> 0.01 us  [shards(): after = lax.ppermute(top, 'lat', down)]
    pallas_call x6 -> x5, Pallas kernels: 7.61 us -> 7.71 us  [call(): pl.pallas_call(kernel, out_shape=out, in_specs=[pl.BlockSpec(memory_space...]
  transfers between devices with their start and end apart: 4 -> 6, of which waited for: 3 -> 0; matrix products, arithmetic and copies ran while one was open for 0% -> 0% of each run, Pallas kernels for 10% -> 8%
where the time goes in v3:
time: 39 us; the launch traced here: 38.8 us
  blocking collectives  16.3 us (42%)
  starting transfers between devices  14 us (36%)
  Pallas kernels  7.71 us (20%)
  between operations  0.76 us (2%)
    all_to_all x1, blocking collectives, shards(): every = lax.all_to_all(spread, ('lat', 'lon'), 0, 0, tiled=True)  16.3 us
    pallas_call x5, Pallas kernels, call(): pl.pallas_call(kernel, out_shape=out, in_specs=[pl.BlockSpec(memory_space...  7.71 us
    ppermute x1, starting transfers between devices, shards(): before = lax.ppermute(bottom, 'lat', up)  5.14 us
    ppermute x1, starting transfers between devices, shards(): last_before = lax.ppermute(last, 'lat', up)  2.4 us
    ppermute x1, starting transfers between devices, shards(): right = lax.ppermute(sent[1], 'lon', west)  2.25 us
    ppermute x1, starting transfers between devices, shards(): left = lax.ppermute(sent[0], 'lon', east)  1.63 us
    ppermute x1, starting transfers between devices, shards(): first_after = lax.ppermute(first, 'lat', down)  1.29 us
    ppermute x1, starting transfers between devices, shards(): after = lax.ppermute(top, 'lat', down)  1.29 us
  transfers between devices with their start and end apart: 6, of which 0 were waited for; matrix products, arithmetic and copies ran while one was open for 0% of the time, Pallas kernels for 8%

profile of v3, /device:TPU:0, one launch (start us, length us, event | category | flops | bytes accessed | tf_op | source)
XLA Modules:
  0.0 38.8 jit_solution(13817297820395444405)
XLA Ops:
  0.6 1.6 %edge_kernel.1 = (f32[4,7,8,256]{3,2,1,0:T(8,128)S(1)}, f32[4,7,8,256]{3,2,1,0:T(8,128)S(1)}, f32[2,8,128]{2,1,0:T(8,128)S(1)}, f32[2,8,128]{2,1,0:T(8,128)S(1)}...) custom-call(f32[4,128,256]{2,1,0:T(8,128)} %bitcast.11, ...), custom_call_target="tpu_custom_call" | custom-call | bytes 1048576 | tf_op jit(solution)/shard_map/edge_kernel/pallas_call | solution.py:311
  2.3 2.4 %collective-permute-start.2 = (f32[2,8,128]{2,1,0:T(8,128)S(1)}, f32[2,8,128]{2,1,0:T(8,128)S(1)}, u32[]{:S(2)}, u32[]{:S(2)}) collective-permute-start(f32[2,8,128]{2,1,0:T(8,128)S(1)} %get-tuple-element.38), channel_id=1, source_target_pairs={{0,4},{4,8},{8,12},{12,16},{16,20},{20,24},{24,28},{1,5},{5,9},{9,... | collective-permute-start | bytes 24584 | tf_op jit(solution)/shard_map/ppermute | solution.py:349
  4.7 1.3 %collective-permute-start.3 = (f32[2,8,128]{2,1,0:T(8,128)S(1)}, f32[2,8,128]{2,1,0:T(8,128)S(1)}, u32[]{:S(2)}, u32[]{:S(2)}) collective-permute-start(f32[2,8,128]{2,1,0:T(8,128)S(1)} %get-tuple-element.39), channel_id=1, source_target_pairs={{4,0},{8,4},{12,8},{16,12},{20,16},{24,20},{28,24},{5,1},{9,5},{13... | collective-permute-start | bytes 24584 | tf_op jit(solution)/shard_map/ppermute | solution.py:350
  6.0 5.1 %collective-permute-start = (f32[4,7,8,256]{3,2,1,0:T(8,128)S(1)}, f32[4,7,8,256]{3,2,1,0:T(8,128)S(1)}, u32[]{:S(2)}, u32[]{:S(2)}) collective-permute-start(f32[4,7,8,256]{3,2,1,0:T(8,128)S(1)} %get-tuple-element.31), channel_id=1, source_target_pairs={{0,4},{4,8},{8,12},{12,16},{16,20},{20,24},{24,28},{1,5},{5,9},{9,... | collective-permute-start | bytes 688136 | tf_op jit(solution)/shard_map/ppermute | solution.py:351
  11.1 1.3 %collective-permute-start.1 = (f32[4,7,8,256]{3,2,1,0:T(8,128)S(1)}, f32[4,7,8,256]{3,2,1,0:T(8,128)S(1)}, u32[]{:S(2)}, u32[]{:S(2)}) collective-permute-start(f32[4,7,8,256]{3,2,1,0:T(8,128)S(1)} %get-tuple-element.32), channel_id=1, source_target_pairs={{4,0},{8,4},{12,8},{16,12},{20,16},{24,20},{28,24},{5,1},{9,5},{13... | collective-permute-start | bytes 688136 | tf_op jit(solution)/shard_map/ppermute | solution.py:352
  12.4 0.9 %own_kernel.1 = (f32[16,4,8,256]{3,2,1,0:T(8,128)S(1)}, f32[16,4,8,256]{3,2,1,0:T(8,128)S(1)}, f32[2,2,8,128]{3,2,1,0:T(8,128)S(1)}, f32[16,8,128]{2,1,0:T(8,128)S(1)}, f32[16,3,8,128]{3,2,1,0:T(8,128)S(1)}) custom-call(f32[2,4,128,128]{3,2,1,0:T(8,128)S(1)} %get-tuple-element.24.n_ref, f32[2,128,128]{2,1,0:T(8,128)S(1)} %get-tuple-element.25.a_ref, ...), custom_call_target="tpu_custom_call" | custom-call | flops 1000000 | bytes 1048576 | tf_op jit(solution)/shard_map/own_kernel/pallas_call | solution.py:311
  13.3 0.0 collective-permute-done.2
  13.4 0.0 collective-permute-done.3
  13.4 1.6 %collective-permute-start.4 = (f32[6,8,128]{2,1,0:T(8,128)S(1)}, f32[6,8,128]{2,1,0:T(8,128)S(1)}, u32[]{:S(2)}, u32[]{:S(2)}) collective-permute-start(f32[6,8,128]{2,1,0:T(8,128)S(1)} %get-tuple-element.49), channel_id=1, source_target_pairs={{0,1},{1,2},{2,3},{3,0},{4,5},{5,6},{6,7},{7,4},{8,9},{9,10},{10,1... | collective-permute-start | bytes 73736 | tf_op jit(solution)/shard_map/ppermute | solution.py:364
  15.0 2.2 %collective-permute-start.5 = (f32[6,8,128]{2,1,0:T(8,128)S(1)}, f32[6,8,128]{2,1,0:T(8,128)S(1)}, u32[]{:S(2)}, u32[]{:S(2)}) collective-permute-start(f32[6,8,128]{2,1,0:T(8,128)S(1)} %get-tuple-element.48), channel_id=1, source_target_pairs={{1,0},{2,1},{3,2},{0,3},{5,4},{6,5},{7,6},{4,7},{9,8},{10,9},{11,1... | collective-permute-start | bytes 73736 | tf_op jit(solution)/shard_map/ppermute | solution.py:365
  17.3 0.0 collective-permute-done.before_ref
  17.3 0.0 collective-permute-done.1.after_ref
  17.3 2.0 %main_kernel.1 = (f32[16,4,8,256]{3,2,1,0:T(8,128)S(1)}, f32[8,8,128]{2,1,0:T(8,128)S(1)}, f32[8,3,8,128]{3,2,1,0:T(8,128)S(1)}) custom-call(f32[16,4,8,256]{3,2,1,0:T(8,128)S(1)} %get-tuple-element.29.y_ref, f32[16,4,8,256]{3,2,1,0:T(8,128)S(1)} %get-tuple-element.30.w_ref, f32[4,7,8,256]{3,2,1,0:T(8,128)S(1)} %collective-permute-done.before_ref, ...), custom_call_target="tpu_custom_call" | custom-call | flops 10000000 | bytes 1507328 | tf_op jit(solution)/shard_map/main_kernel/pallas_call | solution.py:311
  19.3 0.0 collective-permute-done.4.left_ref
  19.3 0.0 collective-permute-done.5.right_ref
  19.4 1.5 %strip_kernel.1 = (f32[16,4,8,256]{3,2,1,0:T(8,128)S(1)}, f32[16,8,256]{2,1,0:T(8,128)S(1)}, f32[2,128]{1,0:T(2,128)S(1)}) custom-call(f32[16,4,8,256]{3,2,1,0:T(8,128)S(1)} %get-tuple-element.33.x_ref, f32[16,4,8,256]{3,2,1,0:T(8,128)S(1)} %get-tuple-element.30.w_ref, f32[16,8,128]{2,1,0:T(8,128)S(1)} %get-tuple-element.34.sy_ref, ...), custom_call_target="tpu_custom_call" | custom-call | bytes 1490944 | tf_op jit(solution)/shard_map/strip_kernel/pallas_call | solution.py:311
  20.9 16.3 %all_to_all.5.all_ref = f32[32,2,128]{2,1,0:T(2,128)S(1)} all-to-all(f32[32,2,128]{2,1,0:T(2,128)S(1)} %broadcast_in_dim.3), channel_id=1, replica_groups=mesh['lat'=8,'lon'=4] {'lat','lon'}, dimensions={0} | all-to-all | bytes 65536 | tf_op jit(solution)/shard_map/all_to_all | solution.py:381
  37.2 1.6 %scale_kernel.1 = (f32[4,128,256]{2,1,0:T(8,128)}, f32[1,1]{1,0:T(1,128)}) custom-call(f32[16,4,8,256]{3,2,1,0:T(8,128)S(1)} %get-tuple-element.41.x_ref, f32[16,4,8,256]{3,2,1,0:T(8,128)S(1)} %get-tuple-element.30.w_ref, f32[16,8,256]{2,1,0:T(8,128)S(1)} %get-tuple-element.42.var_ref, f32[32,2,128]{2,1,0:T(2,128)S(1)} %all_to_all.5.all_ref), custom_call_target="tpu_custom_call" | custom-call | bytes 1212416 | tf_op jit(solution)/shard_map/scale_kernel/pallas_call | solution.py:311
  (6 shorter events, 0.0 us)
Async XLA Ops:
  2.3 11.1 %collective-permute-start.2 = (f32[2,8,128]{2,1,0:T(8,128)S(1)}, f32[2,8,128]{2,1,0:T(8,128)S(1)}, u32[]{:S(2)}, u32[]{:S(2)}) collective-permute-start(f32[2,8,128]{2,1,0:T(8,128)S(1)} %get-tuple-element.38), channel_id=1, source_target_pairs={{0,4},{4,8},{8,12},{12,16},{16,20},{20,24},{24,28},{1,5},{5,9},{9,... | collective-permute-start | bytes 24584 | tf_op jit(solution)/shard_map/ppermute | solution.py:349
  4.7 8.7 %collective-permute-start.3 = (f32[2,8,128]{2,1,0:T(8,128)S(1)}, f32[2,8,128]{2,1,0:T(8,128)S(1)}, u32[]{:S(2)}, u32[]{:S(2)}) collective-permute-start(f32[2,8,128]{2,1,0:T(8,128)S(1)} %get-tuple-element.39), channel_id=1, source_target_pairs={{4,0},{8,4},{12,8},{16,12},{20,16},{24,20},{28,24},{5,1},{9,5},{13... | collective-permute-start | bytes 24584 | tf_op jit(solution)/shard_map/ppermute | solution.py:350
  6.0 11.3 %collective-permute-start = (f32[4,7,8,256]{3,2,1,0:T(8,128)S(1)}, f32[4,7,8,256]{3,2,1,0:T(8,128)S(1)}, u32[]{:S(2)}, u32[]{:S(2)}) collective-permute-start(f32[4,7,8,256]{3,2,1,0:T(8,128)S(1)} %get-tuple-element.31), channel_id=1, source_target_pairs={{0,4},{4,8},{8,12},{12,16},{16,20},{20,24},{24,28},{1,5},{5,9},{9,... | collective-permute-start | bytes 688136 | tf_op jit(solution)/shard_map/ppermute | solution.py:351
  11.1 6.2 %collective-permute-start.1 = (f32[4,7,8,256]{3,2,1,0:T(8,128)S(1)}, f32[4,7,8,256]{3,2,1,0:T(8,128)S(1)}, u32[]{:S(2)}, u32[]{:S(2)}) collective-permute-start(f32[4,7,8,256]{3,2,1,0:T(8,128)S(1)} %get-tuple-element.32), channel_id=1, source_target_pairs={{4,0},{8,4},{12,8},{16,12},{20,16},{24,20},{28,24},{5,1},{9,5},{13... | collective-permute-start | bytes 688136 | tf_op jit(solution)/shard_map/ppermute | solution.py:352
  13.4 5.9 %collective-permute-start.4 = (f32[6,8,128]{2,1,0:T(8,128)S(1)}, f32[6,8,128]{2,1,0:T(8,128)S(1)}, u32[]{:S(2)}, u32[]{:S(2)}) collective-permute-start(f32[6,8,128]{2,1,0:T(8,128)S(1)} %get-tuple-element.49), channel_id=1, source_target_pairs={{0,1},{1,2},{2,3},{3,0},{4,5},{5,6},{6,7},{7,4},{8,9},{9,10},{10,1... | collective-permute-start | bytes 73736 | tf_op jit(solution)/shard_map/ppermute | solution.py:364
  15.0 4.3 %collective-permute-start.5 = (f32[6,8,128]{2,1,0:T(8,128)S(1)}, f32[6,8,128]{2,1,0:T(8,128)S(1)}, u32[]{:S(2)}, u32[]{:S(2)}) collective-permute-start(f32[6,8,128]{2,1,0:T(8,128)S(1)} %get-tuple-element.48), channel_id=1, source_target_pairs={{1,0},{2,1},{3,2},{0,3},{5,4},{6,5},{7,6},{4,7},{9,8},{10,9},{11,1... | collective-permute-start | bytes 73736 | tf_op jit(solution)/shard_map/ppermute | solution.py:365

commit v4 on v2

--- a/solution.py
+++ b/solution.py
@@ -112,7 +112,12 @@
             line = v if line is None else jnp.where((l32 // 4 == k + 1) | (l32 // 4 == 6 - k), v, line)
         packed.append(line)
     packed = replicate(packed, seg)
-    return [jnp.where((l32 < 4) | (l32 >= 28), a, b) for a, b in zip(lines, packed)]
+    both = [jnp.where((l32 < 4) | (l32 >= 28), a, b) for a, b in zip(lines, packed)]
+    east, west = [], []
+    for a, b in zip(both[0::2], both[1::2]):
+        east.append(jnp.where(l32 < SEG // 2, a, roll(b, SEG // 2)))
+        west.append(jnp.where(l32 < SEG // 2, roll(a, -SEG // 2), b))
+    return east, west
 
 
 def strips(gets, samples, parts):
@@ -140,7 +145,10 @@
         batch = range(first, first + BATCH)
         data = [read(r) for r in batch]
         gets = [lambda g, side, row=row: row[side * (tiles - 1)][g] for row in data]
-        sent = messages(gets, samples, parts)
+        east, west = messages(gets, samples, parts)
+        for i in range(BATCH // 2):
+            msg_ref[0, first // 2 + i] = east[i]
+            msg_ref[1, first // 2 + i] = west[i]
         lines, weights = strips(gets, samples, parts)
         for i, r in enumerate(batch):
             for c in range(tiles):
@@ -151,7 +159,6 @@
                 w_ref[r, 0, :, lanes] = centre_weight(values[samples], values[samples + 1])
                 for k in range(3):
                     w_ref[r, 1 + k, :, lanes] = values[samples + k]
-            msg_ref[r] = sent[i]
             sy_ref[r] = lines[i]
             for k in range(3):
                 sw_ref[r, k] = weights[i][k]
@@ -162,15 +169,16 @@
     return [lambda g, side, i=i: ref[i, g, :, pl.ds(side * last, LANES)] for i in range(ITERS)]
 
 
-def join_kernel(own_ref, before_ref, after_ref, msg_ref):
-    rows = own_ref.shape[0]
+def join_kernel(own_ref, before_ref, after_ref, east_ref, west_ref):
+    pairs, half = own_ref.shape[1], ITERS // 2
     samples = before_ref.shape[1] - 3
-    parts = lane_parts(own_ref.shape[1:])
+    parts = lane_parts(own_ref.shape[2:])
     sent = messages(halo_gets(before_ref) + halo_gets(after_ref), samples, parts)
-    msg_ref[ITERS : ITERS + rows] = own_ref[...]
-    for i in range(ITERS):
-        msg_ref[i] = sent[i]
-        msg_ref[ITERS + rows + i] = sent[ITERS + i]
+    for d, ref in enumerate((east_ref, west_ref)):
+        ref[half : half + pairs] = own_ref[d]
+        for i in range(half):
+            ref[i] = sent[d][i]
+            ref[half + pairs + i] = sent[d][half + i]
 
 
 def main_kernel(y_ref, w_ref, before_ref, after_ref, x_ref, hy_ref, hw_ref, wh_ref, p_ref, q_ref):
@@ -240,15 +248,18 @@
 
     def get_y(r):
         ref, _, i = strip_at(r)
-        return jnp.where(from_left, left_ref[r], jnp.where(from_right, right_ref[r], ref[i]))
+        a, b = (left_ref[r // 2], roll(right_ref[r // 2], 16)) if r % 2 == 0 else (roll(left_ref[r // 2], -16), right_ref[r // 2])
+        return jnp.where(from_left, a, jnp.where(from_right, b, ref[i]))
 
     def get_w(r):
         _, ref, i = strip_at(r)
+        a, b = left_ref[r // 2], right_ref[r // 2]
+        skip = (0, 16) if r % 2 == 0 else (16, 0)
         w = [
             jnp.where(
                 from_left,
-                roll(left_ref[r], -4 * (k + 1)),
-                jnp.where(from_right, roll(right_ref[r], 4 * (k + 1)), ref[i, k]),
+                roll(a, -4 * (k + 1) - skip[0]),
+                jnp.where(from_right, roll(b, 4 * (k + 1) + skip[1]), ref[i, k]),
             )
             for k in range(3)
         ]
@@ -292,14 +303,16 @@
     copies = []
     for c in range(cols // LANES):
         lanes = pl.ds(c * LANES, LANES)
+        factors = []
         for r in range(rows):
             wet = w_ref[r, 1, :, lanes] > 0
             safe = jnp.where(wet, var_ref[r, :, lanes], 1.0)
-            factor = jnp.where(wet, jnp.sqrt(mean / (safe + 1e-06)), 0.0)
-            for s in range(samples):
-                stage[c, s, pl.ds(r, levels, stride=rows)] = x_ref[r, s, :, lanes] * factor
-        copies.append(pltpu.make_async_copy(stage.at[c], out_ref.at[:, :, lanes], sem.at[c]))
-        copies[-1].start()
+            factors.append(jnp.where(wet, jnp.sqrt(mean / (safe + 1e-06)), 0.0))
+        for s in range(samples):
+            for r in range(rows):
+                stage[c, s, pl.ds(r, levels, stride=rows)] = x_ref[r, s, :, lanes] * factors[r]
+            copies.append(pltpu.make_async_copy(stage.at[c, s], out_ref.at[s, :, lanes], sem.at[c, s]))
+            copies[-1].start()
     for copy in copies:
         copy.wait()
 
@@ -346,13 +359,14 @@
     before = lax.ppermute(bottom, "lat", up)
     y, w, own_msg, sy, sw = call(
         own_kernel,
-        [(rows, samples, levels, cols), (rows, 4, levels, cols), (rows, levels, LANES), (rows, levels, LANES), (rows, 3, levels, LANES)],
+        [(rows, samples, levels, cols), (rows, 4, levels, cols), (2, rows // 2, levels, LANES), (rows, levels, LANES), (rows, 3, levels, LANES)],
         *staged,
         flops=10**6,
     )
-    (msg,) = call(join_kernel, [(high, levels, LANES)], own_msg, before, after)
-    left = lax.ppermute(msg, "lon", east)
-    right = lax.ppermute(msg, "lon", west)
+    message = (high // 2, levels, LANES)
+    to_east, to_west = call(join_kernel, [message, message], own_msg, before, after)
+    left = lax.ppermute(to_east, "lon", east)
+    right = lax.ppermute(to_west, "lon", west)
     buffer = (high, samples, levels, cols)
     x, hy, hw = call(
         main_kernel,
@@ -376,7 +390,7 @@
         w,
         var,
         every,
-        scratch=[(tiles, samples, levels * rows, LANES), pltpu.SemaphoreType.DMA((tiles,))],
+        scratch=[(tiles, samples, levels * rows, LANES), pltpu.SemaphoreType.DMA((tiles, samples))],
         out_space=[pl.ANY, pltpu.VMEM],
     )
     return out.reshape(noise.shape), mean.reshape(())

time: 36.4 us -> 35 us (0.962)
  waiting for transfers between devices: 7.7 us -> 2.82 us
  blocking collectives: 12.8 us -> 15.8 us
    ppermute x2, waiting for transfers between devices: 5 us -> 0.31 us  [the longest x1 0.2 us: shards(): right = lax.ppermute(to_west, 'lon', west)]
    all_to_all x1, blocking collectives: 12.8 us -> 15.8 us  [shards(): every = lax.all_to_all(spread, ('lat', 'lon'), 0, 0, tiled=True)]
  transfers between devices with their start and end apart: 4 -> 4, of which waited for: 3 -> 3; matrix products, arithmetic and copies ran while one was open for 0% -> 0% of each run, Pallas kernels for 10% -> 11%
where the time goes in v4:
time: 35 us; the launch traced here: 34.8 us
  blocking collectives  15.8 us (45%)
  Pallas kernels  7.85 us (22%)
  starting transfers between devices  7.58 us (22%)
  waiting for transfers between devices  2.82 us (8%)
  between operations  0.69 us (2%)
    all_to_all x1, blocking collectives, shards(): every = lax.all_to_all(spread, ('lat', 'lon'), 0, 0, tiled=True)  15.8 us
    pallas_call x6, Pallas kernels, call(): pl.pallas_call(kernel, out_shape=out, in_specs=[pl.BlockSpec(memory_space...  7.85 us
    ppermute x1, waiting for transfers between devices, shards(): after = lax.ppermute(top, 'lat', down)  2.51 us
    ppermute x1, starting transfers between devices, shards(): before = lax.ppermute(bottom, 'lat', up)  2.41 us
    ppermute x1, starting transfers between devices, shards(): right = lax.ppermute(to_west, 'lon', west)  2.25 us
    ppermute x1, starting transfers between devices, shards(): left = lax.ppermute(to_east, 'lon', east)  1.63 us
    ppermute x1, starting transfers between devices, shards(): after = lax.ppermute(top, 'lat', down)  1.29 us
  transfers between devices with their start and end apart: 4, of which 3 were waited for; matrix products, arithmetic and copies ran while one was open for 0% of the time, Pallas kernels for 11%

profile of v4, /device:TPU:0, one launch (start us, length us, event | category | flops | bytes accessed | tf_op | source)
XLA Modules:
  0.0 34.8 jit_solution(14338680814083956431)
XLA Ops:
  0.6 1.5 %edge_kernel.1 = (f32[4,7,8,256]{3,2,1,0:T(8,128)S(1)}, f32[4,7,8,256]{3,2,1,0:T(8,128)S(1)}, f32[2,4,128,128]{3,2,1,0:T(8,128)S(1)}, f32[2,128,128]{2,1,0:T(8,1...) custom-call(f32[4,128,256]{2,1,0:T(8,128)} %bitcast.7, ...), custom_call_target="tpu_custom_call" | custom-call | bytes 1048576 | tf_op jit(solution)/shard_map/edge_kernel/pallas_call | solution.py:323
  2.2 2.4 %collective-permute-start = (f32[4,7,8,256]{3,2,1,0:T(8,128)S(1)}, f32[4,7,8,256]{3,2,1,0:T(8,128)S(1)}, u32[]{:S(2)}, u32[]{:S(2)}) collective-permute-start(f32[4,7,8,256]{3,2,1,0:T(8,128)S(1)} %get-tuple-element.31), channel_id=1, source_target_pairs={{0,4},{4,8},{8,12},{12,16},{16,20},{20,24},{24,28},{1,5},{5,9},{9,... | collective-permute-start | bytes 688136 | tf_op jit(solution)/shard_map/ppermute | solution.py:359
  4.6 1.3 %collective-permute-start.1 = (f32[4,7,8,256]{3,2,1,0:T(8,128)S(1)}, f32[4,7,8,256]{3,2,1,0:T(8,128)S(1)}, u32[]{:S(2)}, u32[]{:S(2)}) collective-permute-start(f32[4,7,8,256]{3,2,1,0:T(8,128)S(1)} %get-tuple-element.32), channel_id=1, source_target_pairs={{4,0},{8,4},{12,8},{16,12},{20,16},{24,20},{28,24},{5,1},{9,5},{13... | collective-permute-start | bytes 688136 | tf_op jit(solution)/shard_map/ppermute | solution.py:358
  5.9 1.6 %own_kernel.1 = (f32[16,4,8,256]{3,2,1,0:T(8,128)S(1)}, f32[16,4,8,256]{3,2,1,0:T(8,128)S(1)}, f32[2,8,8,128]{3,2,1,0:T(8,128)S(1)}, f32[16,8,128]{2,1,0:T(8,128)S(1)}, f32[16,3,8,128]{3,2,1,0:T(8,128)S(1)}) custom-call(f32[2,4,128,128]{3,2,1,0:T(8,128)S(1)} %get-tuple-element.24.n_ref, f32[2,128,128]{2,1,0:T(8,128)S(1)} %get-tuple-element.25.a_ref, ...), custom_call_target="tpu_custom_call" | custom-call | flops 1000000 | bytes 1048576 | tf_op jit(solution)/shard_map/own_kernel/pallas_call | solution.py:323
  7.5 0.0 collective-permute-done.before_ref
  7.6 2.5 %collective-permute-done.1.after_ref = f32[4,7,8,256]{3,2,1,0:T(8,128)S(1)} collective-permute-done((f32[4,7,8,256]{3,2,1,0:T(8,128)S(1)}, f32[4,7,8,256]{3,2,1,0:T(8,128)S(1)}, u32[]{:S(2)}, u32[]{:S(2)}) %collective-permute-start.1) | collective-permute-done | bytes 229408 | tf_op jit(solution)/shard_map/ppermute | solution.py:358
  10.1 0.3 join_kernel.1
  10.4 1.6 %collective-permute-start.2 = (f32[12,8,128]{2,1,0:T(8,128)S(1)}, f32[12,8,128]{2,1,0:T(8,128)S(1)}, u32[]{:S(2)}, u32[]{:S(2)}) collective-permute-start(f32[12,8,128]{2,1,0:T(8,128)S(1)} %get-tuple-element.39), channel_id=1, source_target_pairs={{0,1},{1,2},{2,3},{3,0},{4,5},{5,6},{6,7},{7,4},{8,9},{9,10},{10,1... | collective-permute-start | bytes 147464 | tf_op jit(solution)/shard_map/ppermute | solution.py:368
  12.0 2.2 %collective-permute-start.3 = (f32[12,8,128]{2,1,0:T(8,128)S(1)}, f32[12,8,128]{2,1,0:T(8,128)S(1)}, u32[]{:S(2)}, u32[]{:S(2)}) collective-permute-start(f32[12,8,128]{2,1,0:T(8,128)S(1)} %get-tuple-element.40), channel_id=1, source_target_pairs={{1,0},{2,1},{3,2},{0,3},{5,4},{6,5},{7,6},{4,7},{9,8},{10,9},{11,1... | collective-permute-start | bytes 147464 | tf_op jit(solution)/shard_map/ppermute | solution.py:369
  14.3 2.0 %main_kernel.1 = (f32[16,4,8,256]{3,2,1,0:T(8,128)S(1)}, f32[8,8,128]{2,1,0:T(8,128)S(1)}, f32[8,3,8,128]{3,2,1,0:T(8,128)S(1)}) custom-call(f32[16,4,8,256]{3,2,1,0:T(8,128)S(1)} %get-tuple-element.29.y_ref, f32[16,4,8,256]{3,2,1,0:T(8,128)S(1)} %get-tuple-element.30.w_ref, f32[4,7,8,256]{3,2,1,0:T(8,128)S(1)} %collective-permute-done.before_ref, ...), custom_call_target="tpu_custom_call" | custom-call | flops 10000000 | bytes 1507328 | tf_op jit(solution)/shard_map/main_kernel/pallas_call | solution.py:323
  16.3 0.1 collective-permute-done.2.left_ref
  16.4 0.2 collective-permute-done.3.right_ref
  16.6 0.7 %strip_kernel.1 = (f32[16,4,8,256]{3,2,1,0:T(8,128)S(1)}, f32[16,8,256]{2,1,0:T(8,128)S(1)}, f32[2,128]{1,0:T(2,128)S(1)}) custom-call(f32[16,4,8,256]{3,2,1,0:T(8,128)S(1)} %get-tuple-element.33.x_ref, f32[16,4,8,256]{3,2,1,0:T(8,128)S(1)} %get-tuple-element.30.w_ref, f32[16,8,128]{2,1,0:T(8,128)S(1)} %get-tuple-element.34.sy_ref, ...), custom_call_target="tpu_custom_call" | custom-call | bytes 1540096 | tf_op jit(solution)/shard_map/strip_kernel/pallas_call | solution.py:323
  17.4 15.8 %all_to_all.5.all_ref = f32[32,2,128]{2,1,0:T(2,128)S(1)} all-to-all(f32[32,2,128]{2,1,0:T(2,128)S(1)} %broadcast_in_dim.3), channel_id=1, replica_groups=mesh['lat'=8,'lon'=4] {'lat','lon'}, dimensions={0} | all-to-all | bytes 65536 | tf_op jit(solution)/shard_map/all_to_all | solution.py:385
  33.2 1.6 %scale_kernel.1 = (f32[4,128,256]{2,1,0:T(8,128)}, f32[1,1]{1,0:T(1,128)}) custom-call(f32[16,4,8,256]{3,2,1,0:T(8,128)S(1)} %get-tuple-element.41.x_ref, f32[16,4,8,256]{3,2,1,0:T(8,128)S(1)} %get-tuple-element.30.w_ref, f32[16,8,256]{2,1,0:T(8,128)S(1)} %get-tuple-element.42.var_ref, f32[32,2,128]{2,1,0:T(2,128)S(1)} %all_to_all.5.all_ref), custom_call_target="tpu_custom_call" | custom-call | bytes 1212416 | tf_op jit(solution)/shard_map/scale_kernel/pallas_call | solution.py:323
  (1 shorter events, 0.0 us)
Async XLA Ops:
  2.2 5.4 %collective-permute-start = (f32[4,7,8,256]{3,2,1,0:T(8,128)S(1)}, f32[4,7,8,256]{3,2,1,0:T(8,128)S(1)}, u32[]{:S(2)}, u32[]{:S(2)}) collective-permute-start(f32[4,7,8,256]{3,2,1,0:T(8,128)S(1)} %get-tuple-element.31), channel_id=1, source_target_pairs={{0,4},{4,8},{8,12},{12,16},{16,20},{20,24},{24,28},{1,5},{5,9},{9,... | collective-permute-start | bytes 688136 | tf_op jit(solution)/shard_map/ppermute | solution.py:359
  4.6 5.5 %collective-permute-start.1 = (f32[4,7,8,256]{3,2,1,0:T(8,128)S(1)}, f32[4,7,8,256]{3,2,1,0:T(8,128)S(1)}, u32[]{:S(2)}, u32[]{:S(2)}) collective-permute-start(f32[4,7,8,256]{3,2,1,0:T(8,128)S(1)} %get-tuple-element.32), channel_id=1, source_target_pairs={{4,0},{8,4},{12,8},{16,12},{20,16},{24,20},{28,24},{5,1},{9,5},{13... | collective-permute-start | bytes 688136 | tf_op jit(solution)/shard_map/ppermute | solution.py:358
  10.4 6.0 %collective-permute-start.2 = (f32[12,8,128]{2,1,0:T(8,128)S(1)}, f32[12,8,128]{2,1,0:T(8,128)S(1)}, u32[]{:S(2)}, u32[]{:S(2)}) collective-permute-start(f32[12,8,128]{2,1,0:T(8,128)S(1)} %get-tuple-element.39), channel_id=1, source_target_pairs={{0,1},{1,2},{2,3},{3,0},{4,5},{5,6},{6,7},{7,4},{8,9},{9,10},{10,1... | collective-permute-start | bytes 147464 | tf_op jit(solution)/shard_map/ppermute | solution.py:368
  12.0 4.6 %collective-permute-start.3 = (f32[12,8,128]{2,1,0:T(8,128)S(1)}, f32[12,8,128]{2,1,0:T(8,128)S(1)}, u32[]{:S(2)}, u32[]{:S(2)}) collective-permute-start(f32[12,8,128]{2,1,0:T(8,128)S(1)} %get-tuple-element.40), channel_id=1, source_target_pairs={{1,0},{2,1},{3,2},{0,3},{5,4},{6,5},{7,6},{4,7},{9,8},{10,9},{11,1... | collective-permute-start | bytes 147464 | tf_op jit(solution)/shard_map/ppermute | solution.py:369

commit v5 on v4

--- a/solution.py
+++ b/solution.py
@@ -48,8 +48,17 @@
         prev, here = here, after
 
 
-def edge_kernel(n_ref, a_ref, b_ref, s_ref, m_ref, top_ref, bot_ref, n_to, a_to, b_to, s_to, m_to, sem):
-    samples, levels, tiles = n_ref.shape[0], top_ref.shape[2], n_to.shape[0]
+def odd_row_block():
+    return lax.rem(lax.axis_index("lat"), 2)
+
+
+def halo_slots():
+    odd = odd_row_block()
+    return (1 - odd) * ITERS, odd * ITERS
+
+
+def edge_kernel(n_ref, a_ref, b_ref, s_ref, m_ref, near_ref, far_ref, n_to, a_to, b_to, s_to, m_to, sem):
+    samples, levels, tiles = n_ref.shape[0], near_ref.shape[2], n_to.shape[0]
     rows = n_ref.shape[1] // levels
     copies = []
     for c in range(tiles):
@@ -61,8 +70,9 @@
         copy.start()
     for copy in copies:
         copy.wait()
+    near_first = (1 - odd_row_block()) * (rows - ITERS)
     for i in range(ITERS):
-        for out, r in ((top_ref, i), (bot_ref, rows - ITERS + i)):
+        for out, r in ((near_ref, near_first + i), (far_ref, rows - ITERS - near_first + i)):
             at = pl.ds(r, levels, stride=rows)
             for c in range(tiles):
                 lanes = pl.ds(c * LANES, LANES)
@@ -169,53 +179,52 @@
     return [lambda g, side, i=i: ref[i, g, :, pl.ds(side * last, LANES)] for i in range(ITERS)]
 
 
-def join_kernel(own_ref, before_ref, after_ref, east_ref, west_ref):
+def join_kernel(own_ref, near_ref, far_ref, east_ref, west_ref):
     pairs, half = own_ref.shape[1], ITERS // 2
-    samples = before_ref.shape[1] - 3
+    samples = near_ref.shape[1] - 3
     parts = lane_parts(own_ref.shape[2:])
-    sent = messages(halo_gets(before_ref) + halo_gets(after_ref), samples, parts)
+    sent = messages(halo_gets(near_ref) + halo_gets(far_ref), samples, parts)
     for d, ref in enumerate((east_ref, west_ref)):
         ref[half : half + pairs] = own_ref[d]
-        for i in range(half):
-            ref[i] = sent[d][i]
-            ref[half + pairs + i] = sent[d][half + i]
-
-
-def main_kernel(y_ref, w_ref, before_ref, after_ref, x_ref, hy_ref, hw_ref, wh_ref, p_ref, q_ref):
+        for n, slot in enumerate(halo_slots()):
+            at = lax.div(slot, ITERS) * (half + pairs)
+            for i in range(half):
+                ref[at + i] = sent[d][n * half + i]
+
+
+def main_kernel(y_ref, w_ref, near_ref, far_ref, x_ref, hy_ref, hw_ref, yh_ref, wh_ref, p_ref, q_ref):
     rows, samples, levels, cols = y_ref.shape
     high = rows + 2 * ITERS
     parts = lane_parts((levels, LANES))
 
-    def halo(r):
-        return (before_ref, r) if r < ITERS else (after_ref, r - ITERS - rows)
-
     def own(r):
         return ITERS <= r < ITERS + rows
 
-    for r in range(high):
-        if not own(r):
-            ref, i = halo(r)
-            slot = r if r < ITERS else r - rows
-            w = [ref[i, samples + k] for k in range(3)]
-            wh_ref[slot, 0] = centre_weight(w[0], w[1])
-            for k in range(3):
-                wh_ref[slot, 1 + k] = w[k]
-
-    def get_w(r):
+    def pick(r, own_ref, halo_ref):
         if own(r):
-            return [w_ref[r - ITERS, k] for k in range(4)]
-        return [wh_ref[r if r < ITERS else r - rows, k] for k in range(4)]
-
-    for side, ref in enumerate((before_ref, after_ref)):
+            return own_ref, r - ITERS
+        return halo_ref, r if r < ITERS else r - rows
+
+    for ref, slot in zip((near_ref, far_ref), halo_slots()):
         lines, weights = strips(halo_gets(ref), samples, parts)
         for i in range(ITERS):
-            hy_ref[side * ITERS + i] = lines[i]
+            hy_ref[slot + i] = lines[i]
             for k in range(3):
-                hw_ref[side * ITERS + i, k] = weights[i][k]
+                hw_ref[slot + i, k] = weights[i][k]
+            for s in range(samples):
+                yh_ref[slot + i, s] = ref[i, s]
+            w = [ref[i, samples + k] for k in range(3)]
+            wh_ref[slot + i, 0] = centre_weight(w[0], w[1])
+            for k in range(3):
+                wh_ref[slot + i, 1 + k] = w[k]
+
+    def get_w(r):
+        ref, i = pick(r, w_ref, wh_ref)
+        return [ref[i, k] for k in range(4)]
 
     def sample(s, carry):
         def first_y(r):
-            ref, i = (y_ref, r - ITERS) if own(r) else halo(r)
+            ref, i = pick(r, y_ref, yh_ref)
             return ref[i, s]
 
         source = first_y
@@ -339,8 +348,8 @@
         a.reshape(levels * rows, cols) for a in (diff_lat, diff_lon, shear, sea_mask)
     ]
     n_lat, n_lon = lax.axis_size("lat"), lax.axis_size("lon")
-    up = [(i, i + 1) for i in range(n_lat - 1)]
-    down = [(j, i) for i, j in up]
+    pair = [(i, i ^ 1) for i in range(n_lat)]
+    across = [(i, i - 1 if i % 2 == 0 else i + 1) for i in range(1, n_lat - 1)]
     east = [(i, (i + 1) % n_lon) for i in range(n_lon)]
     west = [(j, i) for i, j in east]
 
@@ -348,15 +357,15 @@
     tiles = cols // LANES
     plane = (tiles, levels * rows, LANES)
     flat = [pltpu.with_memory_space_constraint(a, pltpu.HBM) for a in flat]
-    top, bottom, *staged = call(
+    to_near, to_far, *staged = call(
         edge_kernel,
         [halo, halo, (tiles, samples, levels * rows, LANES)] + [plane] * 3 + [jax.ShapeDtypeStruct(plane, sea_mask.dtype)],
         *flat,
         scratch=[pltpu.SemaphoreType.DMA((tiles, 5))],
         in_space=pltpu.HBM,
     )
-    after = lax.ppermute(top, "lat", down)
-    before = lax.ppermute(bottom, "lat", up)
+    far = lax.ppermute(to_far, "lat", across)
+    near = lax.ppermute(to_near, "lat", pair)
     y, w, own_msg, sy, sw = call(
         own_kernel,
         [(rows, samples, levels, cols), (rows, 4, levels, cols), (2, rows // 2, levels, LANES), (rows, levels, LANES), (rows, 3, levels, LANES)],
@@ -364,7 +373,7 @@
         flops=10**6,
     )
     message = (high // 2, levels, LANES)
-    to_east, to_west = call(join_kernel, [message, message], own_msg, before, after)
+    to_east, to_west = call(join_kernel, [message, message], own_msg, near, far)
     left = lax.ppermute(to_east, "lon", east)
     right = lax.ppermute(to_west, "lon", west)
     buffer = (high, samples, levels, cols)
@@ -373,9 +382,9 @@
         [y.shape, (2 * ITERS, levels, LANES), (2 * ITERS, 3, levels, LANES)],
         y,
         w,
-        before,
-        after,
-        scratch=[(2 * ITERS, 4, levels, cols), buffer, buffer],
+        near,
+        far,
+        scratch=[(2 * ITERS, samples, levels, cols), (2 * ITERS, 4, levels, cols), buffer, buffer],
         flops=10**7,
     )
     x, var, part = call(

time: 35 us -> 35 us (level)
  blocking collectives: 15.8 us -> 19.8 us
  waiting for transfers between devices: 2.82 us -> 0.44 us
  starting transfers between devices: 7.58 us -> 5.95 us
    all_to_all x1, blocking collectives: 15.8 us -> 19.8 us  [shards(): every = lax.all_to_all(spread, ('lat', 'lon'), 0, 0, tiled=True)]
    ppermute x2, waiting for transfers between devices: 2.51 us -> 0.01 us  [the longest x1 0.01 us: shards(): far = lax.ppermute(to_far, 'lat', across)]
    ppermute x2, starting transfers between devices: 3.7 us -> 1.22 us  [the longest x1 0.66 us: shards(): far = lax.ppermute(to_far, 'lat', across)]
    ppermute x1, starting transfers between devices: 1.63 us -> 2.64 us  [shards(): left = lax.ppermute(to_east, 'lon', east)]
  transfers between devices with their start and end apart: 4 -> 4, of which waited for: 3 -> 1; matrix products, arithmetic and copies ran while one was open for 0% -> 0% of each run, Pallas kernels for 11% -> 11%
where the time goes in v5:
time: 35 us; the launch traced here: 34.8 us
  blocking collectives  19.8 us (57%)
  Pallas kernels  7.91 us (23%)
  starting transfers between devices  5.95 us (17%)
  between operations  0.69 us (2%)
  waiting for transfers between devices  0.44 us (1%)
    all_to_all x1, blocking collectives, shards(): every = lax.all_to_all(spread, ('lat', 'lon'), 0, 0, tiled=True)  19.8 us
    pallas_call x6, Pallas kernels, call(): pl.pallas_call(kernel, out_shape=out, in_specs=[pl.BlockSpec(memory_space...  7.91 us
    ppermute x1, starting transfers between devices, shards(): left = lax.ppermute(to_east, 'lon', east)  2.64 us
    ppermute x1, starting transfers between devices, shards(): right = lax.ppermute(to_west, 'lon', west)  2.09 us
  transfers between devices with their start and end apart: 4, of which 1 were waited for; matrix products, arithmetic and copies ran while one was open for 0% of the time, Pallas kernels for 11%

profile of v5, /device:TPU:0, one launch (start us, length us, event | category | flops | bytes accessed | tf_op | source)
XLA Modules:
  0.0 34.8 jit_solution(3440897972996627607)
XLA Ops:
  0.6 1.6 %edge_kernel.1 = (f32[4,7,8,256]{3,2,1,0:T(8,128)S(1)}, f32[4,7,8,256]{3,2,1,0:T(8,128)S(1)}, f32[2,4,128,128]{3,2,1,0:T(8,128)S(1)}, f32[2,128,128]{2,1,0:T(8,1...) custom-call(f32[4,128,256]{2,1,0:T(8,128)} %bitcast.7, ...), custom_call_target="tpu_custom_call" | custom-call | bytes 1048576 | tf_op jit(solution)/shard_map/edge_kernel/pallas_call | solution.py:332
  2.2 0.6 %collective-permute-start = (f32[4,7,8,256]{3,2,1,0:T(8,128)S(1)}, f32[4,7,8,256]{3,2,1,0:T(8,128)S(1)}, u32[]{:S(2)}, u32[]{:S(2)}) collective-permute-start(f32[4,7,8,256]{3,2,1,0:T(8,128)S(1)} %get-tuple-element.31), channel_id=1, source_target_pairs={{0,4},{4,0},{8,12},{12,8},{16,20},{20,16},{24,28},{28,24},{1,5},{5... | collective-permute-start | bytes 688136 | tf_op jit(solution)/shard_map/ppermute | solution.py:368
  2.8 0.7 %collective-permute-start.1 = (f32[4,7,8,256]{3,2,1,0:T(8,128)S(1)}, f32[4,7,8,256]{3,2,1,0:T(8,128)S(1)}, u32[]{:S(2)}, u32[]{:S(2)}) collective-permute-start(f32[4,7,8,256]{3,2,1,0:T(8,128)S(1)} %get-tuple-element.32), channel_id=1, source_target_pairs={{4,8},{8,4},{12,16},{16,12},{20,24},{24,20},{5,9},{9,5},{13,17},{1... | collective-permute-start | bytes 688136 | tf_op jit(solution)/shard_map/ppermute | solution.py:367
  3.4 1.6 %own_kernel.1 = (f32[16,4,8,256]{3,2,1,0:T(8,128)S(1)}, f32[16,4,8,256]{3,2,1,0:T(8,128)S(1)}, f32[2,8,8,128]{3,2,1,0:T(8,128)S(1)}, f32[16,8,128]{2,1,0:T(8,128)S(1)}, f32[16,3,8,128]{3,2,1,0:T(8,128)S(1)}) custom-call(f32[2,4,128,128]{3,2,1,0:T(8,128)S(1)} %get-tuple-element.24.n_ref, f32[2,128,128]{2,1,0:T(8,128)S(1)} %get-tuple-element.25.a_ref, ...), custom_call_target="tpu_custom_call" | custom-call | flops 1000000 | bytes 1048576 | tf_op jit(solution)/shard_map/own_kernel/pallas_call | solution.py:332
  5.1 0.0 collective-permute-done.near_ref
  5.1 0.0 collective-permute-done.1.far_ref
  5.1 0.3 join_kernel.1
  5.4 2.6 %collective-permute-start.2 = (f32[12,8,128]{2,1,0:T(8,128)S(1)}, f32[12,8,128]{2,1,0:T(8,128)S(1)}, u32[]{:S(2)}, u32[]{:S(2)}) collective-permute-start(f32[12,8,128]{2,1,0:T(8,128)S(1)} %get-tuple-element.39), channel_id=1, source_target_pairs={{0,1},{1,2},{2,3},{3,0},{4,5},{5,6},{6,7},{7,4},{8,9},{9,10},{10,1... | collective-permute-start | bytes 147464 | tf_op jit(solution)/shard_map/ppermute | solution.py:377
  8.1 2.1 %collective-permute-start.3 = (f32[12,8,128]{2,1,0:T(8,128)S(1)}, f32[12,8,128]{2,1,0:T(8,128)S(1)}, u32[]{:S(2)}, u32[]{:S(2)}) collective-permute-start(f32[12,8,128]{2,1,0:T(8,128)S(1)} %get-tuple-element.40), channel_id=1, source_target_pairs={{1,0},{2,1},{3,2},{0,3},{5,4},{6,5},{7,6},{4,7},{9,8},{10,9},{11,1... | collective-permute-start | bytes 147464 | tf_op jit(solution)/shard_map/ppermute | solution.py:378
  10.1 2.1 %main_kernel.1 = (f32[16,4,8,256]{3,2,1,0:T(8,128)S(1)}, f32[8,8,128]{2,1,0:T(8,128)S(1)}, f32[8,3,8,128]{3,2,1,0:T(8,128)S(1)}) custom-call(f32[16,4,8,256]{3,2,1,0:T(8,128)S(1)} %get-tuple-element.29.y_ref, f32[16,4,8,256]{3,2,1,0:T(8,128)S(1)} %get-tuple-element.30.w_ref, f32[4,7,8,256]{3,2,1,0:T(8,128)S(1)} %collective-permute-done.near_ref, ...), custom_call_target="tpu_custom_call" | custom-call | flops 10000000 | bytes 1507328 | tf_op jit(solution)/shard_map/main_kernel/pallas_call | solution.py:332
  12.2 0.0 collective-permute-done.2.left_ref
  12.3 0.4 %collective-permute-done.3.right_ref = f32[12,8,128]{2,1,0:T(8,128)S(1)} collective-permute-done((f32[12,8,128]{2,1,0:T(8,128)S(1)}, f32[12,8,128]{2,1,0:T(8,128)S(1)}, u32[]{:S(2)}, u32[]{:S(2)}) %collective-permute-start.3) | collective-permute-done | bytes 49184 | tf_op jit(solution)/shard_map/ppermute | solution.py:378
  12.7 0.7 %strip_kernel.1 = (f32[16,4,8,256]{3,2,1,0:T(8,128)S(1)}, f32[16,8,256]{2,1,0:T(8,128)S(1)}, f32[2,128]{1,0:T(2,128)S(1)}) custom-call(f32[16,4,8,256]{3,2,1,0:T(8,128)S(1)} %get-tuple-element.33.x_ref, f32[16,4,8,256]{3,2,1,0:T(8,128)S(1)} %get-tuple-element.30.w_ref, f32[16,8,128]{2,1,0:T(8,128)S(1)} %get-tuple-element.34.sy_ref, ...), custom_call_target="tpu_custom_call" | custom-call | bytes 1540096 | tf_op jit(solution)/shard_map/strip_kernel/pallas_call | solution.py:332
  13.4 19.8 %all_to_all.5.all_ref = f32[32,2,128]{2,1,0:T(2,128)S(1)} all-to-all(f32[32,2,128]{2,1,0:T(2,128)S(1)} %broadcast_in_dim.3), channel_id=1, replica_groups=mesh['lat'=8,'lon'=4] {'lat','lon'}, dimensions={0} | all-to-all | bytes 65536 | tf_op jit(solution)/shard_map/all_to_all | solution.py:394
  33.3 1.6 %scale_kernel.1 = (f32[4,128,256]{2,1,0:T(8,128)}, f32[1,1]{1,0:T(1,128)}) custom-call(f32[16,4,8,256]{3,2,1,0:T(8,128)S(1)} %get-tuple-element.41.x_ref, f32[16,4,8,256]{3,2,1,0:T(8,128)S(1)} %get-tuple-element.30.w_ref, f32[16,8,256]{2,1,0:T(8,128)S(1)} %get-tuple-element.42.var_ref, f32[32,2,128]{2,1,0:T(2,128)S(1)} %all_to_all.5.all_ref), custom_call_target="tpu_custom_call" | custom-call | bytes 1212416 | tf_op jit(solution)/shard_map/scale_kernel/pallas_call | solution.py:332
  (1 shorter events, 0.0 us)
Async XLA Ops:
  2.2 2.9 %collective-permute-start = (f32[4,7,8,256]{3,2,1,0:T(8,128)S(1)}, f32[4,7,8,256]{3,2,1,0:T(8,128)S(1)}, u32[]{:S(2)}, u32[]{:S(2)}) collective-permute-start(f32[4,7,8,256]{3,2,1,0:T(8,128)S(1)} %get-tuple-element.31), channel_id=1, source_target_pairs={{0,4},{4,0},{8,12},{12,8},{16,20},{20,16},{24,28},{28,24},{1,5},{5... | collective-permute-start | bytes 688136 | tf_op jit(solution)/shard_map/ppermute | solution.py:368
  2.8 2.3 %collective-permute-start.1 = (f32[4,7,8,256]{3,2,1,0:T(8,128)S(1)}, f32[4,7,8,256]{3,2,1,0:T(8,128)S(1)}, u32[]{:S(2)}, u32[]{:S(2)}) collective-permute-start(f32[4,7,8,256]{3,2,1,0:T(8,128)S(1)} %get-tuple-element.32), channel_id=1, source_target_pairs={{4,8},{8,4},{12,16},{16,12},{20,24},{24,20},{5,9},{9,5},{13,17},{1... | collective-permute-start | bytes 688136 | tf_op jit(solution)/shard_map/ppermute | solution.py:367
  5.4 6.8 %collective-permute-start.2 = (f32[12,8,128]{2,1,0:T(8,128)S(1)}, f32[12,8,128]{2,1,0:T(8,128)S(1)}, u32[]{:S(2)}, u32[]{:S(2)}) collective-permute-start(f32[12,8,128]{2,1,0:T(8,128)S(1)} %get-tuple-element.39), channel_id=1, source_target_pairs={{0,1},{1,2},{2,3},{3,0},{4,5},{5,6},{6,7},{7,4},{8,9},{9,10},{10,1... | collective-permute-start | bytes 147464 | tf_op jit(solution)/shard_map/ppermute | solution.py:377
  8.1 4.6 %collective-permute-start.3 = (f32[12,8,128]{2,1,0:T(8,128)S(1)}, f32[12,8,128]{2,1,0:T(8,128)S(1)}, u32[]{:S(2)}, u32[]{:S(2)}) collective-permute-start(f32[12,8,128]{2,1,0:T(8,128)S(1)} %get-tuple-element.40), channel_id=1, source_target_pairs={{1,0},{2,1},{3,2},{0,3},{5,4},{6,5},{7,6},{4,7},{9,8},{10,9},{11,1... | collective-permute-start | bytes 147464 | tf_op jit(solution)/shard_map/ppermute | solution.py:378

commit v6 on v5

--- a/solution.py
+++ b/solution.py
@@ -33,7 +33,7 @@
     return lane, lane // SEG, lane % SEG
 
 
-def stencil(rows, get_y, get_w, first, last, put):
+def stencil(get_y, get_w, first, last, put):
     def products(r):
         y = get_y(r)
         w0, wa, wb, wc = get_w(r)
@@ -57,7 +57,7 @@
     return (1 - odd) * ITERS, odd * ITERS
 
 
-def edge_kernel(n_ref, a_ref, b_ref, s_ref, m_ref, near_ref, far_ref, n_to, a_to, b_to, s_to, m_to, sem):
+def edge_kernel(n_ref, a_ref, b_ref, s_ref, m_ref, near_ref, far_ref, corner_ref, n_to, a_to, b_to, s_to, m_to, sem):
     samples, levels, tiles = n_ref.shape[0], near_ref.shape[2], n_to.shape[0]
     rows = n_ref.shape[1] // levels
     copies = []
@@ -81,6 +81,10 @@
                 w = cell_weights(a_to[c, at], b_to[c, at], s_to[c, at], m_to[c, at])
                 for k in range(3):
                     out[i, samples + k, :, lanes] = w[k]
+    sent = messages(halo_gets(far_ref), samples, lane_parts((levels, LANES)))
+    for d in range(2):
+        for i in range(ITERS // 2):
+            corner_ref[d, i] = sent[d][i]
 
 
 BATCH = 4
@@ -138,32 +142,43 @@
     return lines, [weights[3 * i : 3 * i + 3] for i in range(len(gets))]
 
 
-def own_kernel(n_ref, a_ref, b_ref, s_ref, m_ref, y_ref, w_ref, msg_ref, sy_ref, sw_ref):
-    rows, samples, levels, cols = y_ref.shape
+def own_row(refs, r, rows, levels):
+    n_ref, a_ref, b_ref, s_ref, m_ref = refs
+    at = pl.ds(r, levels, stride=rows)
+    return [
+        [n_ref[c, s, at] for s in range(n_ref.shape[1])]
+        + list(cell_weights(a_ref[c, at], b_ref[c, at], s_ref[c, at], m_ref[c, at]))
+        for c in range(n_ref.shape[0])
+    ]
+
+
+def own_gets(data):
+    return [lambda g, side, row=row: row[-side][g] for row in data]
+
+
+def message_kernel(*refs):
+    refs, msg_ref = refs[:-1], refs[-1]
+    levels = msg_ref.shape[2]
+    rows, samples = refs[0].shape[2] // levels, refs[0].shape[1]
     parts = lane_parts((levels, LANES))
-    tiles = cols // LANES
-
-    def read(r):
-        at = pl.ds(r, levels, stride=rows)
-        return [
-            [n_ref[c, s, at] for s in range(samples)]
-            + list(cell_weights(a_ref[c, at], b_ref[c, at], s_ref[c, at], m_ref[c, at]))
-            for c in range(tiles)
-        ]
-
+    for first in range(0, rows, BATCH):
+        data = [own_row(refs, r, rows, levels) for r in range(first, first + BATCH)]
+        sent = messages(own_gets(data), samples, parts)
+        for d in range(2):
+            for i in range(BATCH // 2):
+                msg_ref[d, first // 2 + i] = sent[d][i]
+
+
+def own_kernel(n_ref, a_ref, b_ref, s_ref, m_ref, y_ref, w_ref, sy_ref, sw_ref):
+    rows, samples, levels, _ = y_ref.shape
+    parts = lane_parts((levels, LANES))
     for first in range(0, rows, BATCH):
         batch = range(first, first + BATCH)
-        data = [read(r) for r in batch]
-        gets = [lambda g, side, row=row: row[side * (tiles - 1)][g] for row in data]
-        east, west = messages(gets, samples, parts)
-        for i in range(BATCH // 2):
-            msg_ref[0, first // 2 + i] = east[i]
-            msg_ref[1, first // 2 + i] = west[i]
-        lines, weights = strips(gets, samples, parts)
+        data = [own_row((n_ref, a_ref, b_ref, s_ref, m_ref), r, rows, levels) for r in batch]
+        lines, weights = strips(own_gets(data), samples, parts)
         for i, r in enumerate(batch):
-            for c in range(tiles):
+            for c, values in enumerate(data[i]):
                 lanes = pl.ds(c * LANES, LANES)
-                values = data[i][c]
                 for s in range(samples):
                     y_ref[r, s, :, lanes] = values[s]
                 w_ref[r, 0, :, lanes] = centre_weight(values[samples], values[samples + 1])
@@ -179,21 +194,19 @@
     return [lambda g, side, i=i: ref[i, g, :, pl.ds(side * last, LANES)] for i in range(ITERS)]
 
 
-def join_kernel(own_ref, near_ref, far_ref, east_ref, west_ref):
+def join_kernel(own_ref, near_ref, corner_ref, east_ref, west_ref):
     pairs, half = own_ref.shape[1], ITERS // 2
-    samples = near_ref.shape[1] - 3
-    parts = lane_parts(own_ref.shape[2:])
-    sent = messages(halo_gets(near_ref) + halo_gets(far_ref), samples, parts)
+    sent = messages(halo_gets(near_ref), near_ref.shape[1] - 3, lane_parts(own_ref.shape[2:]))
+    near, far = [lax.div(slot, ITERS) * (half + pairs) for slot in halo_slots()]
     for d, ref in enumerate((east_ref, west_ref)):
         ref[half : half + pairs] = own_ref[d]
-        for n, slot in enumerate(halo_slots()):
-            at = lax.div(slot, ITERS) * (half + pairs)
-            for i in range(half):
-                ref[at + i] = sent[d][n * half + i]
+        for i in range(half):
+            ref[near + i] = sent[d][i]
+            ref[far + i] = corner_ref[d, i]
 
 
 def main_kernel(y_ref, w_ref, near_ref, far_ref, x_ref, hy_ref, hw_ref, yh_ref, wh_ref, p_ref, q_ref):
-    rows, samples, levels, cols = y_ref.shape
+    rows, samples, levels, _ = y_ref.shape
     high = rows + 2 * ITERS
     parts = lane_parts((levels, LANES))
 
@@ -237,7 +250,7 @@
                 else:
                     target[r, s] = v
 
-            stencil(high, source, get_w, step + 1, high - 1 - step, put)
+            stencil(source, get_w, step + 1, high - 1 - step, put)
             source = functools.partial(lambda r, target: target[r, s], target=target)
         return carry
 
@@ -247,7 +260,7 @@
 def strip_kernel(x_ref, w_ref, sy_ref, sw_ref, hy_ref, hw_ref, left_ref, right_ref, out_ref, var_ref, sum_ref):
     rows, samples, levels, cols = x_ref.shape
     high = rows + 2 * ITERS
-    lane, seg, l32 = lane_parts((levels, LANES))
+    lane, _, l32 = lane_parts((levels, LANES))
     from_left, from_right = l32 < 4, l32 >= 28
 
     def strip_at(r):
@@ -278,7 +291,7 @@
     field = {r: get_y(r) for r in range(high)}
     for step in range(ITERS):
         new = {}
-        stencil(high, field.__getitem__, weights.__getitem__, step + 1, high - 1 - step, new.__setitem__)
+        stencil(field.__getitem__, weights.__getitem__, step + 1, high - 1 - step, new.__setitem__)
         field = new
 
     total, count = None, None
@@ -337,7 +350,6 @@
         scratch_shapes=scratch,
         cost_estimate=pl.CostEstimate(flops=flops, bytes_accessed=sum(a.size * 4 for a in args), transcendentals=0),
         compiler_params=pltpu.CompilerParams(vmem_limit_bytes=12 << 20),
-        name=kernel.__name__,
     )(*args)
 
 
@@ -357,25 +369,28 @@
     tiles = cols // LANES
     plane = (tiles, levels * rows, LANES)
     flat = [pltpu.with_memory_space_constraint(a, pltpu.HBM) for a in flat]
-    to_near, to_far, *staged = call(
+    to_near, to_far, to_corner, *staged = call(
         edge_kernel,
-        [halo, halo, (tiles, samples, levels * rows, LANES)] + [plane] * 3 + [jax.ShapeDtypeStruct(plane, sea_mask.dtype)],
+        [halo, halo, (2, ITERS // 2, levels, LANES), (tiles, samples, levels * rows, LANES)] + [plane] * 3 + [jax.ShapeDtypeStruct(plane, sea_mask.dtype)],
         *flat,
         scratch=[pltpu.SemaphoreType.DMA((tiles, 5))],
         in_space=pltpu.HBM,
     )
+    near = lax.ppermute(to_near, "lat", pair)
+    corner = lax.ppermute(to_corner, "lat", across)
     far = lax.ppermute(to_far, "lat", across)
-    near = lax.ppermute(to_near, "lat", pair)
-    y, w, own_msg, sy, sw = call(
+    (own_msg,) = call(message_kernel, [(2, rows // 2, levels, LANES)], *staged, flops=10**6)
+    message = (high // 2, levels, LANES)
+    to_east, to_west = call(join_kernel, [message, message], own_msg, near, corner)
+    left = lax.ppermute(to_east, "lon", east)
+    right = lax.ppermute(to_west, "lon", west)
+    strip = (rows, levels, LANES)
+    y, w, sy, sw = call(
         own_kernel,
-        [(rows, samples, levels, cols), (rows, 4, levels, cols), (2, rows // 2, levels, LANES), (rows, levels, LANES), (rows, 3, levels, LANES)],
+        [(rows, samples, levels, cols), (rows, 4, levels, cols), strip, (rows, 3, levels, LANES)],
         *staged,
         flops=10**6,
     )
-    message = (high // 2, levels, LANES)
-    to_east, to_west = call(join_kernel, [message, message], own_msg, near, far)
-    left = lax.ppermute(to_east, "lon", east)
-    right = lax.ppermute(to_west, "lon", west)
     buffer = (high, samples, levels, cols)
     x, hy, hw = call(
         main_kernel,

time: 35 us -> 35.5 us (1.014)
  starting transfers between devices: 5.95 us -> 6.58 us
  waiting for transfers between devices: 0.44 us -> 0.01 us
  blocking collectives: 19.8 us -> 20.2 us
    ppermute x0 -> x1, starting transfers between devices: none -> 0.66 us  [shards(): corner = lax.ppermute(to_corner, 'lat', across)]
    ppermute x1, waiting for transfers between devices: 0.42 us -> 0.01 us  [shards(): right = lax.ppermute(to_west, 'lon', west)]
    all_to_all x1, blocking collectives: 19.8 us -> 20.2 us  [shards(): every = lax.all_to_all(spread, ('lat', 'lon'), 0, 0, tiled=True)]
    pallas_call x6 -> x7, Pallas kernels: 7.91 us -> 7.82 us  [call(): pl.pallas_call(kernel, out_shape=out, in_specs=[pl.BlockSpec(memory_space...]
  transfers between devices with their start and end apart: 4 -> 5, of which waited for: 1 -> 0; matrix products, arithmetic and copies ran while one was open for 0% -> 0% of each run, Pallas kernels for 11% -> 11%
where the time goes in v6:
time: 35.5 us; the launch traced here: 35.4 us
  blocking collectives  20.2 us (57%)
  Pallas kernels  7.82 us (22%)
  starting transfers between devices  6.58 us (19%)
  between operations  0.71 us (2%)
    all_to_all x1, blocking collectives, shards(): every = lax.all_to_all(spread, ('lat', 'lon'), 0, 0, tiled=True)  20.2 us
    pallas_call x7, Pallas kernels, call(): pl.pallas_call(kernel, out_shape=out, in_specs=[pl.BlockSpec(memory_space...  7.82 us
    ppermute x1, starting transfers between devices, shards(): left = lax.ppermute(to_east, 'lon', east)  2.61 us
    ppermute x1, starting transfers between devices, shards(): right = lax.ppermute(to_west, 'lon', west)  2.09 us
  transfers between devices with their start and end apart: 5, of which 0 were waited for; matrix products, arithmetic and copies ran while one was open for 0% of the time, Pallas kernels for 11%

profile of v6, /device:TPU:0, one launch (start us, length us, event | category | flops | bytes accessed | tf_op | source)
XLA Modules:
  0.0 35.4 jit_solution(5603810967393859131)
XLA Ops:
  0.6 1.8 %shard_map.68 = (f32[4,7,8,256]{3,2,1,0:T(8,128)S(1)}, f32[4,7,8,256]{3,2,1,0:T(8,128)S(1)}, f32[2,2,8,128]{3,2,1,0:T(8,128)S(1)}, f32[2,4,128,128]{3,2,1,0:T(8,...) custom-call(f32[4,128,256]{2,1,0:T(8,128)} %bitcast.7, ...), custom_call_target="tpu_custom_call" | custom-call | bytes 1048576 | tf_op jit(solution)/shard_map/pallas_call | solution.py:345
  2.4 0.6 %collective-permute-start = (f32[4,7,8,256]{3,2,1,0:T(8,128)S(1)}, f32[4,7,8,256]{3,2,1,0:T(8,128)S(1)}, u32[]{:S(2)}, u32[]{:S(2)}) collective-permute-start(f32[4,7,8,256]{3,2,1,0:T(8,128)S(1)} %get-tuple-element.31), channel_id=1, source_target_pairs={{0,4},{4,0},{8,12},{12,8},{16,20},{20,16},{24,28},{28,24},{1,5},{5... | collective-permute-start | bytes 688136 | tf_op jit(solution)/shard_map/ppermute | solution.py:379
  3.0 0.7 %collective-permute-start.1 = (f32[4,7,8,256]{3,2,1,0:T(8,128)S(1)}, f32[4,7,8,256]{3,2,1,0:T(8,128)S(1)}, u32[]{:S(2)}, u32[]{:S(2)}) collective-permute-start(f32[4,7,8,256]{3,2,1,0:T(8,128)S(1)} %get-tuple-element.32), channel_id=1, source_target_pairs={{4,8},{8,4},{12,16},{16,12},{20,24},{24,20},{5,9},{9,5},{13,17},{1... | collective-permute-start | bytes 688136 | tf_op jit(solution)/shard_map/ppermute | solution.py:381
  3.7 0.7 %collective-permute-start.2 = (f32[2,2,8,128]{3,2,1,0:T(8,128)S(1)}, f32[2,2,8,128]{3,2,1,0:T(8,128)S(1)}, u32[]{:S(2)}, u32[]{:S(2)}) collective-permute-start(f32[2,2,8,128]{3,2,1,0:T(8,128)S(1)} %get-tuple-element.38), channel_id=1, source_target_pairs={{4,8},{8,4},{12,16},{16,12},{20,24},{24,20},{5,9},{9,5},{13,17},{1... | collective-permute-start | bytes 49160 | tf_op jit(solution)/shard_map/ppermute | solution.py:380
  4.3 0.6 %shard_map.71.own_ref = f32[2,8,8,128]{3,2,1,0:T(8,128)S(1)} custom-call(f32[2,4,128,128]{3,2,1,0:T(8,128)S(1)} %get-tuple-element.24.n_ref.refs_0_, f32[2,128,128]{2,1,0:T(8,128)S(1)} %get-tuple-element.25.a_ref.refs_1_, f32[2,128,128]{2,1,0:T(8,128)S(1)} %get-tuple-element.26.b_ref.refs_2_, f32[2,128,128]{2,1,0:T(8,128)S(1)} %get-tuple-element.27.s_ref.refs_3_, ...), custom_call_target="tpu_custom_call" | custom-call | flops 1000000 | bytes 1048576 | tf_op jit(solution)/shard_map/pallas_call | solution.py:345
  5.0 0.0 collective-permute-done.2.corner_ref
  5.0 0.0 collective-permute-done.near_ref
  5.0 0.3 shard_map.72
  5.3 2.6 %collective-permute-start.3 = (f32[12,8,128]{2,1,0:T(8,128)S(1)}, f32[12,8,128]{2,1,0:T(8,128)S(1)}, u32[]{:S(2)}, u32[]{:S(2)}) collective-permute-start(f32[12,8,128]{2,1,0:T(8,128)S(1)} %get-tuple-element.39), channel_id=1, source_target_pairs={{0,1},{1,2},{2,3},{3,0},{4,5},{5,6},{6,7},{7,4},{8,9},{9,10},{10,1... | collective-permute-start | bytes 147464 | tf_op jit(solution)/shard_map/ppermute | solution.py:385
  7.9 2.1 %collective-permute-start.4 = (f32[12,8,128]{2,1,0:T(8,128)S(1)}, f32[12,8,128]{2,1,0:T(8,128)S(1)}, u32[]{:S(2)}, u32[]{:S(2)}) collective-permute-start(f32[12,8,128]{2,1,0:T(8,128)S(1)} %get-tuple-element.40), channel_id=1, source_target_pairs={{1,0},{2,1},{3,2},{0,3},{5,4},{6,5},{7,6},{4,7},{9,8},{10,9},{11,1... | collective-permute-start | bytes 147464 | tf_op jit(solution)/shard_map/ppermute | solution.py:386
  10.0 0.7 %shard_map.69 = (f32[16,4,8,256]{3,2,1,0:T(8,128)S(1)}, f32[16,4,8,256]{3,2,1,0:T(8,128)S(1)}, f32[16,8,128]{2,1,0:T(8,128)S(1)}, f32[16,3,8,128]{3,2,1,0:T(8,128)S(1)}) custom-call(f32[2,4,128,128]{3,2,1,0:T(8,128)S(1)} %get-tuple-element.24.n_ref.refs_0_, f32[2,128,128]{2,1,0:T(8,128)S(1)} %get-tuple-element.25.a_ref.refs_1_, ...), custom_call_target="tpu_custom_call" | custom-call | flops 1000000 | bytes 1048576 | tf_op jit(solution)/shard_map/pallas_call | solution.py:345
  10.7 0.0 collective-permute-done.1.far_ref
  10.7 2.1 %shard_map.70 = (f32[16,4,8,256]{3,2,1,0:T(8,128)S(1)}, f32[8,8,128]{2,1,0:T(8,128)S(1)}, f32[8,3,8,128]{3,2,1,0:T(8,128)S(1)}) custom-call(f32[16,4,8,256]{3,2,1,0:T(8,128)S(1)} %get-tuple-element.29.y_ref, f32[16,4,8,256]{3,2,1,0:T(8,128)S(1)} %get-tuple-element.30.w_ref, f32[4,7,8,256]{3,2,1,0:T(8,128)S(1)} %collective-permute-done.near_ref, ...), custom_call_target="tpu_custom_call" | custom-call | flops 10000000 | bytes 1507328 | tf_op jit(solution)/shard_map/pallas_call | solution.py:345
  12.8 0.0 collective-permute-done.3.left_ref
  12.8 0.0 collective-permute-done.4.right_ref
  12.8 0.7 %shard_map.73 = (f32[16,4,8,256]{3,2,1,0:T(8,128)S(1)}, f32[16,8,256]{2,1,0:T(8,128)S(1)}, f32[2,128]{1,0:T(2,128)S(1)}) custom-call(f32[16,4,8,256]{3,2,1,0:T(8,128)S(1)} %get-tuple-element.33.x_ref, f32[16,4,8,256]{3,2,1,0:T(8,128)S(1)} %get-tuple-element.30.w_ref, f32[16,8,128]{2,1,0:T(8,128)S(1)} %get-tuple-element.34.sy_ref, ...), custom_call_target="tpu_custom_call" | custom-call | bytes 1540096 | tf_op jit(solution)/shard_map/pallas_call | solution.py:345
  13.6 20.2 %all_to_all.5.all_ref = f32[32,2,128]{2,1,0:T(2,128)S(1)} all-to-all(f32[32,2,128]{2,1,0:T(2,128)S(1)} %broadcast_in_dim.3), channel_id=1, replica_groups=mesh['lat'=8,'lon'=4] {'lat','lon'}, dimensions={0} | all-to-all | bytes 65536 | tf_op jit(solution)/shard_map/all_to_all | solution.py:409
  33.8 1.6 %shard_map.74 = (f32[4,128,256]{2,1,0:T(8,128)}, f32[1,1]{1,0:T(1,128)}) custom-call(f32[16,4,8,256]{3,2,1,0:T(8,128)S(1)} %get-tuple-element.41.x_ref, f32[16,4,8,256]{3,2,1,0:T(8,128)S(1)} %get-tuple-element.30.w_ref, f32[16,8,256]{2,1,0:T(8,128)S(1)} %get-tuple-element.42.var_ref, f32[32,2,128]{2,1,0:T(2,128)S(1)} %all_to_all.5.all_ref), custom_call_target="tpu_custom_call" | custom-call | bytes 1212416 | tf_op jit(solution)/shard_map/pallas_call | solution.py:345
  (1 shorter events, 0.0 us)
Async XLA Ops:
  2.4 2.6 %collective-permute-start = (f32[4,7,8,256]{3,2,1,0:T(8,128)S(1)}, f32[4,7,8,256]{3,2,1,0:T(8,128)S(1)}, u32[]{:S(2)}, u32[]{:S(2)}) collective-permute-start(f32[4,7,8,256]{3,2,1,0:T(8,128)S(1)} %get-tuple-element.31), channel_id=1, source_target_pairs={{0,4},{4,0},{8,12},{12,8},{16,20},{20,16},{24,28},{28,24},{1,5},{5... | collective-permute-start | bytes 688136 | tf_op jit(solution)/shard_map/ppermute | solution.py:379
  3.0 7.7 %collective-permute-start.1 = (f32[4,7,8,256]{3,2,1,0:T(8,128)S(1)}, f32[4,7,8,256]{3,2,1,0:T(8,128)S(1)}, u32[]{:S(2)}, u32[]{:S(2)}) collective-permute-start(f32[4,7,8,256]{3,2,1,0:T(8,128)S(1)} %get-tuple-element.32), channel_id=1, source_target_pairs={{4,8},{8,4},{12,16},{16,12},{20,24},{24,20},{5,9},{9,5},{13,17},{1... | collective-permute-start | bytes 688136 | tf_op jit(solution)/shard_map/ppermute | solution.py:381
  3.7 1.3 %collective-permute-start.2 = (f32[2,2,8,128]{3,2,1,0:T(8,128)S(1)}, f32[2,2,8,128]{3,2,1,0:T(8,128)S(1)}, u32[]{:S(2)}, u32[]{:S(2)}) collective-permute-start(f32[2,2,8,128]{3,2,1,0:T(8,128)S(1)} %get-tuple-element.38), channel_id=1, source_target_pairs={{4,8},{8,4},{12,16},{16,12},{20,24},{24,20},{5,9},{9,5},{13,17},{1... | collective-permute-start | bytes 49160 | tf_op jit(solution)/shard_map/ppermute | solution.py:380
  5.3 7.5 %collective-permute-start.3 = (f32[12,8,128]{2,1,0:T(8,128)S(1)}, f32[12,8,128]{2,1,0:T(8,128)S(1)}, u32[]{:S(2)}, u32[]{:S(2)}) collective-permute-start(f32[12,8,128]{2,1,0:T(8,128)S(1)} %get-tuple-element.39), channel_id=1, source_target_pairs={{0,1},{1,2},{2,3},{3,0},{4,5},{5,6},{6,7},{7,4},{8,9},{9,10},{10,1... | collective-permute-start | bytes 147464 | tf_op jit(solution)/shard_map/ppermute | solution.py:385
  7.9 4.9 %collective-permute-start.4 = (f32[12,8,128]{2,1,0:T(8,128)S(1)}, f32[12,8,128]{2,1,0:T(8,128)S(1)}, u32[]{:S(2)}, u32[]{:S(2)}) collective-permute-start(f32[12,8,128]{2,1,0:T(8,128)S(1)} %get-tuple-element.40), channel_id=1, source_target_pairs={{1,0},{2,1},{3,2},{0,3},{5,4},{6,5},{7,6},{4,7},{9,8},{10,9},{11,1... | collective-permute-start | bytes 147464 | tf_op jit(solution)/shard_map/ppermute | solution.py:386

commit v7 on v6

--- a/solution.py
+++ b/solution.py
@@ -20,6 +20,10 @@
 
 def centre_weight(wa, wb):
     return jnp.where(wa > 0, 1.0, 0.0) - 2.0 * (wa + wb)
+
+
+def all_weights(w, sign):
+    return centre_weight(w[0], w[1]), w[0], w[1], sign * w[2]
 
 
 def roll(x, shift):
@@ -48,13 +52,10 @@
         prev, here = here, after
 
 
-def odd_row_block():
-    return lax.rem(lax.axis_index("lat"), 2)
-
-
-def halo_slots():
-    odd = odd_row_block()
-    return (1 - odd) * ITERS, odd * ITERS
+def row_order(rows):
+    odd = lax.rem(lax.axis_index("lat"), 2)
+    step = 2 * odd - 1
+    return lambda d: (1 - odd) * (rows - 1) + step * d, step.astype(F32)
 
 
 def edge_kernel(n_ref, a_ref, b_ref, s_ref, m_ref, near_ref, far_ref, corner_ref, n_to, a_to, b_to, s_to, m_to, sem):
@@ -70,10 +71,10 @@
         copy.start()
     for copy in copies:
         copy.wait()
-    near_first = (1 - odd_row_block()) * (rows - ITERS)
+    row_at, _ = row_order(rows)
     for i in range(ITERS):
-        for out, r in ((near_ref, near_first + i), (far_ref, rows - ITERS - near_first + i)):
-            at = pl.ds(r, levels, stride=rows)
+        for out, d in ((near_ref, ITERS - 1 - i), (far_ref, rows - 1 - i)):
+            at = pl.ds(row_at(d), levels, stride=rows)
             for c in range(tiles):
                 lanes = pl.ds(c * LANES, LANES)
                 for s in range(samples):
@@ -113,24 +114,22 @@
 
 
 def messages(gets, samples, parts):
-    _, seg, l32 = parts
-    lines = line_up(gets, samples, parts, 1, 0)
-    turned = [
-        [(roll(get(samples + k, 1), 4 * k + 8), roll(get(samples + k, 0), 24 - 4 * k)) for k in range(3)] for get in gets
-    ]
-    packed = []
-    for row in turned:
-        line = None
-        for k, (a, b) in enumerate(row):
-            v = jnp.where(l32 < SEG // 2, a, b)
-            line = v if line is None else jnp.where((l32 // 4 == k + 1) | (l32 // 4 == 6 - k), v, line)
-        packed.append(line)
-    packed = replicate(packed, seg)
-    both = [jnp.where((l32 < 4) | (l32 >= 28), a, b) for a, b in zip(lines, packed)]
-    east, west = [], []
-    for a, b in zip(both[0::2], both[1::2]):
-        east.append(jnp.where(l32 < SEG // 2, a, roll(b, SEG // 2)))
-        west.append(jnp.where(l32 < SEG // 2, roll(a, -SEG // 2), b))
+    lane, seg, l32 = parts
+    left = lane < LANES // 2
+    both = [[jnp.where(left, get(g, 0), get(g, 1)) for g in range(samples + 3)] for get in gets]
+    lines = [[roll(row[s], SEG * s + 4) for s in range(samples)] for row in both]
+    packed = [[roll(row[samples + k], 8 * k + 12) for k in range(3)] for row in both]
+    packed = replicate([jnp.where(l32 < 16, a, jnp.where(l32 < 24, b, c)) for a, b, c in packed], seg)
+    full = []
+    for line, weights in zip(lines, packed):
+        v = line[0]
+        for s in range(1, samples):
+            v = jnp.where(seg == s, line[s], v)
+        full.append(jnp.where(l32 < 8, v, weights))
+    low = lane % 8 < 4
+    pairs = list(zip(full[0::2], full[1::2]))
+    east = [jnp.where(low, a, roll(b, 4)) for a, b in pairs]
+    west = [jnp.where(low, roll(a, -4), b) for a, b in pairs]
     return east, west
 
 
@@ -144,7 +143,7 @@
 
 def own_row(refs, r, rows, levels):
     n_ref, a_ref, b_ref, s_ref, m_ref = refs
-    at = pl.ds(r, levels, stride=rows)
+    at = pl.ds(row_order(rows)[0](r), levels, stride=rows)
     return [
         [n_ref[c, s, at] for s in range(n_ref.shape[1])]
         + list(cell_weights(a_ref[c, at], b_ref[c, at], s_ref[c, at], m_ref[c, at]))
@@ -172,6 +171,7 @@
 def own_kernel(n_ref, a_ref, b_ref, s_ref, m_ref, y_ref, w_ref, sy_ref, sw_ref):
     rows, samples, levels, _ = y_ref.shape
     parts = lane_parts((levels, LANES))
+    _, sign = row_order(rows)
     for first in range(0, rows, BATCH):
         batch = range(first, first + BATCH)
         data = [own_row((n_ref, a_ref, b_ref, s_ref, m_ref), r, rows, levels) for r in batch]
@@ -181,9 +181,8 @@
                 lanes = pl.ds(c * LANES, LANES)
                 for s in range(samples):
                     y_ref[r, s, :, lanes] = values[s]
-                w_ref[r, 0, :, lanes] = centre_weight(values[samples], values[samples + 1])
-                for k in range(3):
-                    w_ref[r, 1 + k, :, lanes] = values[samples + k]
+                for k, v in enumerate(all_weights(values[samples:], sign)):
+                    w_ref[r, k, :, lanes] = v
             sy_ref[r] = lines[i]
             for k in range(3):
                 sw_ref[r, k] = weights[i][k]
@@ -197,58 +196,42 @@
 def join_kernel(own_ref, near_ref, corner_ref, east_ref, west_ref):
     pairs, half = own_ref.shape[1], ITERS // 2
     sent = messages(halo_gets(near_ref), near_ref.shape[1] - 3, lane_parts(own_ref.shape[2:]))
-    near, far = [lax.div(slot, ITERS) * (half + pairs) for slot in halo_slots()]
     for d, ref in enumerate((east_ref, west_ref)):
+        for i in range(half):
+            ref[i] = sent[d][i]
         ref[half : half + pairs] = own_ref[d]
-        for i in range(half):
-            ref[near + i] = sent[d][i]
-            ref[far + i] = corner_ref[d, i]
-
-
-def main_kernel(y_ref, w_ref, near_ref, far_ref, x_ref, hy_ref, hw_ref, yh_ref, wh_ref, p_ref, q_ref):
+        ref[half + pairs :] = corner_ref[d]
+
+
+def near_kernel(y_ref, w_ref, near_ref, x_ref, keep_ref, hy_ref, hw_ref, wh_ref, p_ref, q_ref):
     rows, samples, levels, _ = y_ref.shape
-    high = rows + 2 * ITERS
-    parts = lane_parts((levels, LANES))
-
-    def own(r):
-        return ITERS <= r < ITERS + rows
-
-    def pick(r, own_ref, halo_ref):
-        if own(r):
-            return own_ref, r - ITERS
-        return halo_ref, r if r < ITERS else r - rows
-
-    for ref, slot in zip((near_ref, far_ref), halo_slots()):
-        lines, weights = strips(halo_gets(ref), samples, parts)
-        for i in range(ITERS):
-            hy_ref[slot + i] = lines[i]
-            for k in range(3):
-                hw_ref[slot + i, k] = weights[i][k]
-            for s in range(samples):
-                yh_ref[slot + i, s] = ref[i, s]
-            w = [ref[i, samples + k] for k in range(3)]
-            wh_ref[slot + i, 0] = centre_weight(w[0], w[1])
-            for k in range(3):
-                wh_ref[slot + i, 1 + k] = w[k]
+    high = rows + ITERS
+    _, sign = row_order(rows)
+    lines, weights = strips(halo_gets(near_ref), samples, lane_parts((levels, LANES)))
+    for i in range(ITERS):
+        hy_ref[i] = lines[i]
+        for k in range(3):
+            hw_ref[i, k] = weights[i][k]
+        for k, v in enumerate(all_weights([near_ref[i, samples + k] for k in range(3)], sign)):
+            wh_ref[i, k] = v
 
     def get_w(r):
-        ref, i = pick(r, w_ref, wh_ref)
+        ref, i = (wh_ref, r) if r < ITERS else (w_ref, r - ITERS)
         return [ref[i, k] for k in range(4)]
 
     def sample(s, carry):
-        def first_y(r):
-            ref, i = pick(r, y_ref, yh_ref)
-            return ref[i, s]
-
-        source = first_y
+        source = lambda r: near_ref[r, s] if r < ITERS else y_ref[r - ITERS, s]
         for step in range(ITERS):
             target = (p_ref, q_ref)[step % 2]
 
             def put(r, v, target=target, step=step):
                 if step == ITERS - 1:
                     x_ref[r - ITERS, s] = v
-                else:
-                    target[r, s] = v
+                    return
+                target[r, s] = v
+                kept = r - (high - 3 - step)
+                if kept >= 0:
+                    keep_ref[step, kept, s] = v
 
             stencil(source, get_w, step + 1, high - 1 - step, put)
             source = functools.partial(lambda r, target: target[r, s], target=target)
@@ -257,42 +240,67 @@
     lax.fori_loop(0, samples, sample, 0)
 
 
-def strip_kernel(x_ref, w_ref, sy_ref, sw_ref, hy_ref, hw_ref, left_ref, right_ref, out_ref, var_ref, sum_ref):
+def far_rows(y_ref, w_ref, far_ref, keep_ref, wh_ref, s):
+    rows = y_ref.shape[0]
+    high = rows + ITERS
+
+    def get_w(r):
+        ref, i = (wh_ref, r - high) if r >= high else (w_ref, r - ITERS)
+        return [ref[i, k] for k in range(4)]
+
+    source = lambda r: far_ref[r - high, s] if r >= high else y_ref[r - ITERS, s]
+    for step in range(ITERS):
+        new = {}
+        stencil(source, get_w, high - 1 - step, high - 1 - step + ITERS, new.__setitem__)
+        if step < ITERS - 1:
+            new[high - 3 - step], new[high - 2 - step] = keep_ref[step, 0, s], keep_ref[step, 1, s]
+        source = new.__getitem__
+    return new
+
+
+def finish_kernel(
+    x_ref, y_ref, w_ref, keep_ref, far_ref, sy_ref, sw_ref, hy_ref, hw_ref, left_ref, right_ref,
+    out_ref, var_ref, sum_ref, wh_ref,
+):
     rows, samples, levels, cols = x_ref.shape
     high = rows + 2 * ITERS
-    lane, _, l32 = lane_parts((levels, LANES))
+    parts = lane_parts((levels, LANES))
+    lane, _, l32 = parts
     from_left, from_right = l32 < 4, l32 >= 28
+    _, sign = row_order(rows)
+
+    for i in range(ITERS):
+        for k, v in enumerate(all_weights([far_ref[i, samples + k] for k in range(3)], sign)):
+            wh_ref[i, k] = v
+    far_lines, far_weights = strips(halo_gets(far_ref), samples, parts)
 
     def strip_at(r):
-        if ITERS <= r < ITERS + rows:
-            return sy_ref, sw_ref, r - ITERS
-        return hy_ref, hw_ref, r if r < ITERS else r - rows
-
-    def get_y(r):
-        ref, _, i = strip_at(r)
-        a, b = (left_ref[r // 2], roll(right_ref[r // 2], 16)) if r % 2 == 0 else (roll(left_ref[r // 2], -16), right_ref[r // 2])
-        return jnp.where(from_left, a, jnp.where(from_right, b, ref[i]))
-
-    def get_w(r):
-        _, ref, i = strip_at(r)
-        a, b = left_ref[r // 2], right_ref[r // 2]
-        skip = (0, 16) if r % 2 == 0 else (16, 0)
-        w = [
+        if r < ITERS:
+            return hy_ref[r], [hw_ref[r, k] for k in range(3)]
+        if r < ITERS + rows:
+            return sy_ref[r - ITERS], [sw_ref[r - ITERS, k] for k in range(3)]
+        return far_lines[r - ITERS - rows], far_weights[r - ITERS - rows]
+
+    field, weights = {}, {}
+    for r in range(high):
+        skip = 4 * (r % 2)
+        values = [
             jnp.where(
                 from_left,
-                roll(a, -4 * (k + 1) - skip[0]),
-                jnp.where(from_right, roll(b, 4 * (k + 1) + skip[1]), ref[i, k]),
+                roll(left_ref[r // 2], -8 * g - skip),
+                jnp.where(from_right, roll(right_ref[r // 2], 28 - 8 * g - skip), v),
             )
-            for k in range(3)
+            for g, v in enumerate([strip_at(r)[0], *strip_at(r)[1]])
         ]
-        return (centre_weight(w[0], w[1]), *w)
-
-    weights = [get_w(r) for r in range(high)]
-    field = {r: get_y(r) for r in range(high)}
+        field[r], weights[r] = values[0], all_weights(values[1:], sign)
     for step in range(ITERS):
         new = {}
         stencil(field.__getitem__, weights.__getitem__, step + 1, high - 1 - step, new.__setitem__)
         field = new
+
+    for s in range(samples):
+        for r, v in far_rows(y_ref, w_ref, far_ref, keep_ref, wh_ref, s).items():
+            out_ref[r - ITERS, s] = v
 
     total, count = None, None
     for r in range(rows):
@@ -301,7 +309,7 @@
             lanes = pl.ds(c, LANES)
             square = None
             for s in range(samples):
-                v = x_ref[r, s, :, lanes]
+                v = (x_ref if r < rows - ITERS else out_ref)[r, s, :, lanes]
                 if c == 0:
                     v = jnp.where(lane < 4, roll(strip, -(SEG * s + 4)), v)
                 if c == cols - LANES:
@@ -322,6 +330,7 @@
     sums = jnp.sum(jnp.sum(all_ref[...], axis=0), axis=1, keepdims=True)
     mean = sums[0:1] / sums[1:2]
     mean_ref[...] = mean
+    row_at, _ = row_order(rows)
     copies = []
     for c in range(cols // LANES):
         lanes = pl.ds(c * LANES, LANES)
@@ -332,7 +341,7 @@
             factors.append(jnp.where(wet, jnp.sqrt(mean / (safe + 1e-06)), 0.0))
         for s in range(samples):
             for r in range(rows):
-                stage[c, s, pl.ds(r, levels, stride=rows)] = x_ref[r, s, :, lanes] * factors[r]
+                stage[c, s, pl.ds(row_at(r), levels, stride=rows)] = x_ref[r, s, :, lanes] * factors[r]
             copies.append(pltpu.make_async_copy(stage.at[c, s], out_ref.at[s, :, lanes], sem.at[c, s]))
             copies[-1].start()
     for copy in copies:
@@ -391,19 +400,32 @@
         *staged,
         flops=10**6,
     )
-    buffer = (high, samples, levels, cols)
-    x, hy, hw = call(
-        main_kernel,
-        [y.shape, (2 * ITERS, levels, LANES), (2 * ITERS, 3, levels, LANES)],
+    buffer = (rows + ITERS, samples, levels, cols)
+    side = [(ITERS, levels, LANES), (ITERS, 3, levels, LANES)]
+    x, keep, hy, hw = call(
+        near_kernel,
+        [y.shape, (ITERS - 1, 2, samples, levels, cols), *side],
         y,
         w,
         near,
+        scratch=[(ITERS, 4, levels, cols), buffer, buffer],
+        flops=10**7,
+    )
+    x, var, part = call(
+        finish_kernel,
+        [y.shape, (rows, levels, cols), (2, LANES)],
+        x,
+        y,
+        w,
+        keep,
         far,
-        scratch=[(2 * ITERS, samples, levels, cols), (2 * ITERS, 4, levels, cols), buffer, buffer],
-        flops=10**7,
-    )
-    x, var, part = call(
-        strip_kernel, [y.shape, (rows, levels, cols), (2, LANES)], x, w, sy, sw, hy, hw, left, right
+        sy,
+        sw,
+        hy,
+        hw,
+        left,
+        right,
+        scratch=[(ITERS, 4, levels, cols)],
     )
     spread = jnp.broadcast_to(part, (n_lat * n_lon, 2, LANES))
     every = lax.all_to_all(spread, ("lat", "lon"), 0, 0, tiled=True)

time: 35.5 us -> 36.5 us (1.028)
  Pallas kernels: 7.82 us -> 8.85 us
    pallas_call x7, Pallas kernels: 7.82 us -> 8.85 us  [call(): pl.pallas_call(kernel, out_shape=out, in_specs=[pl.BlockSpec(memory_space...]
  transfers between devices with their start and end apart: 5 -> 5, of which waited for: 0 -> 0; matrix products, arithmetic and copies ran while one was open for 0% -> 0% of each run, Pallas kernels for 11% -> 10%
where the time goes in v7:
time: 36.5 us; the launch traced here: 36.4 us
  blocking collectives  20.2 us (55%)
  Pallas kernels  8.85 us (24%)
  starting transfers between devices  6.55 us (18%)
  between operations  0.72 us (2%)
    all_to_all x1, blocking collectives, shards(): every = lax.all_to_all(spread, ('lat', 'lon'), 0, 0, tiled=True)  20.2 us
    pallas_call x7, Pallas kernels, call(): pl.pallas_call(kernel, out_shape=out, in_specs=[pl.BlockSpec(memory_space...  8.85 us
    ppermute x1, starting transfers between devices, shards(): left = lax.ppermute(to_east, 'lon', east)  2.6 us
    ppermute x1, starting transfers between devices, shards(): right = lax.ppermute(to_west, 'lon', west)  2.07 us
  transfers between devices with their start and end apart: 5, of which 0 were waited for; matrix products, arithmetic and copies ran while one was open for 0% of the time, Pallas kernels for 10%

profile of v7, /device:TPU:0, one launch (start us, length us, event | category | flops | bytes accessed | tf_op | source)
XLA Modules:
  0.0 36.4 jit_solution(13918095026759371987)
XLA Ops:
  0.6 1.8 %shard_map.68 = (f32[4,7,8,256]{3,2,1,0:T(8,128)S(1)}, f32[4,7,8,256]{3,2,1,0:T(8,128)S(1)}, f32[2,2,8,128]{3,2,1,0:T(8,128)S(1)}, f32[2,4,128,128]{3,2,1,0:T(8,...) custom-call(f32[4,128,256]{2,1,0:T(8,128)} %bitcast.7, ...), custom_call_target="tpu_custom_call" | custom-call | bytes 1048576 | tf_op jit(solution)/shard_map/pallas_call | solution.py:354
  2.5 0.6 %collective-permute-start = (f32[4,7,8,256]{3,2,1,0:T(8,128)S(1)}, f32[4,7,8,256]{3,2,1,0:T(8,128)S(1)}, u32[]{:S(2)}, u32[]{:S(2)}) collective-permute-start(f32[4,7,8,256]{3,2,1,0:T(8,128)S(1)} %get-tuple-element.32), channel_id=1, source_target_pairs={{0,4},{4,0},{8,12},{12,8},{16,20},{20,16},{24,28},{28,24},{1,5},{5... | collective-permute-start | bytes 688136 | tf_op jit(solution)/shard_map/ppermute | solution.py:388
  3.0 0.7 %collective-permute-start.1 = (f32[4,7,8,256]{3,2,1,0:T(8,128)S(1)}, f32[4,7,8,256]{3,2,1,0:T(8,128)S(1)}, u32[]{:S(2)}, u32[]{:S(2)}) collective-permute-start(f32[4,7,8,256]{3,2,1,0:T(8,128)S(1)} %get-tuple-element.35), channel_id=1, source_target_pairs={{4,8},{8,4},{12,16},{16,12},{20,24},{24,20},{5,9},{9,5},{13,17},{1... | collective-permute-start | bytes 688136 | tf_op jit(solution)/shard_map/ppermute | solution.py:390
  3.7 0.7 %collective-permute-start.2 = (f32[2,2,8,128]{3,2,1,0:T(8,128)S(1)}, f32[2,2,8,128]{3,2,1,0:T(8,128)S(1)}, u32[]{:S(2)}, u32[]{:S(2)}) collective-permute-start(f32[2,2,8,128]{3,2,1,0:T(8,128)S(1)} %get-tuple-element.40), channel_id=1, source_target_pairs={{4,8},{8,4},{12,16},{16,12},{20,24},{24,20},{5,9},{9,5},{13,17},{1... | collective-permute-start | bytes 49160 | tf_op jit(solution)/shard_map/ppermute | solution.py:389
  4.4 0.7 %shard_map.71.own_ref = f32[2,8,8,128]{3,2,1,0:T(8,128)S(1)} custom-call(f32[2,4,128,128]{3,2,1,0:T(8,128)S(1)} %get-tuple-element.25.n_ref.refs_0_, f32[2,128,128]{2,1,0:T(8,128)S(1)} %get-tuple-element.26.a_ref.refs_1_, f32[2,128,128]{2,1,0:T(8,128)S(1)} %get-tuple-element.27.b_ref.refs_2_, f32[2,128,128]{2,1,0:T(8,128)S(1)} %get-tuple-element.28.s_ref.refs_3_, ...), custom_call_target="tpu_custom_call" | custom-call | flops 1000000 | bytes 1048576 | tf_op jit(solution)/shard_map/pallas_call | solution.py:354
  5.1 0.0 collective-permute-done.2.corner_ref
  5.1 0.0 collective-permute-done.near_ref
  5.1 0.3 shard_map.72
  5.4 2.6 %collective-permute-start.3 = (f32[12,8,128]{2,1,0:T(8,128)S(1)}, f32[12,8,128]{2,1,0:T(8,128)S(1)}, u32[]{:S(2)}, u32[]{:S(2)}) collective-permute-start(f32[12,8,128]{2,1,0:T(8,128)S(1)} %get-tuple-element.41), channel_id=1, source_target_pairs={{0,1},{1,2},{2,3},{3,0},{4,5},{5,6},{6,7},{7,4},{8,9},{9,10},{10,1... | collective-permute-start | bytes 147464 | tf_op jit(solution)/shard_map/ppermute | solution.py:394
  8.0 2.1 %collective-permute-start.4 = (f32[12,8,128]{2,1,0:T(8,128)S(1)}, f32[12,8,128]{2,1,0:T(8,128)S(1)}, u32[]{:S(2)}, u32[]{:S(2)}) collective-permute-start(f32[12,8,128]{2,1,0:T(8,128)S(1)} %get-tuple-element.42), channel_id=1, source_target_pairs={{1,0},{2,1},{3,2},{0,3},{5,4},{6,5},{7,6},{4,7},{9,8},{10,9},{11,1... | collective-permute-start | bytes 147464 | tf_op jit(solution)/shard_map/ppermute | solution.py:395
  10.1 0.8 %shard_map.69 = (f32[16,4,8,256]{3,2,1,0:T(8,128)S(1)}, f32[16,4,8,256]{3,2,1,0:T(8,128)S(1)}, f32[16,8,128]{2,1,0:T(8,128)S(1)}, f32[16,3,8,128]{3,2,1,0:T(8,128)S(1)}) custom-call(f32[2,4,128,128]{3,2,1,0:T(8,128)S(1)} %get-tuple-element.25.n_ref.refs_0_, f32[2,128,128]{2,1,0:T(8,128)S(1)} %get-tuple-element.26.a_ref.refs_1_, ...), custom_call_target="tpu_custom_call" | custom-call | flops 1000000 | bytes 1048576 | tf_op jit(solution)/shard_map/pallas_call | solution.py:354
  10.9 1.9 %shard_map.70 = (f32[16,4,8,256]{3,2,1,0:T(8,128)S(1)}, f32[3,2,4,8,256]{4,3,2,1,0:T(8,128)S(1)}, f32[4,8,128]{2,1,0:T(8,128)S(1)}, f32[4,3,8,128]{3,2,1,0:T(8,128)S(1)}) custom-call(f32[16,4,8,256]{3,2,1,0:T(8,128)S(1)} %get-tuple-element.30.y_ref, f32[16,4,8,256]{3,2,1,0:T(8,128)S(1)} %get-tuple-element.31.w_ref, ...), custom_call_target="tpu_custom_call" | custom-call | flops 10000000 | bytes 1277952 | tf_op jit(solution)/shard_map/pallas_call | solution.py:354
  12.8 0.0 collective-permute-done.1.far_ref
  12.8 0.0 collective-permute-done.3.left_ref
  12.8 0.0 collective-permute-done.4.right_ref
  12.8 1.8 %shard_map.73 = (f32[16,4,8,256]{3,2,1,0:T(8,128)S(1)}, f32[16,8,256]{2,1,0:T(8,128)S(1)}, f32[2,128]{1,0:T(2,128)S(1)}) custom-call(f32[16,4,8,256]{3,2,1,0:T(8,128)S(1)} %get-tuple-element.33.x_ref, f32[16,4,8,256]{3,2,1,0:T(8,128)S(1)} %get-tuple-element.30.y_ref, f32[16,4,8,256]{3,2,1,0:T(8,128)S(1)} %get-tuple-element.31.w_ref, ...), custom_call_target="tpu_custom_call" | custom-call | bytes 2424832 | tf_op jit(solution)/shard_map/pallas_call | solution.py:354
  14.6 20.2 %all_to_all.5.all_ref = f32[32,2,128]{2,1,0:T(2,128)S(1)} all-to-all(f32[32,2,128]{2,1,0:T(2,128)S(1)} %broadcast_in_dim.3), channel_id=1, replica_groups=mesh['lat'=8,'lon'=4] {'lat','lon'}, dimensions={0} | all-to-all | bytes 65536 | tf_op jit(solution)/shard_map/all_to_all | solution.py:431
  34.8 1.5 %shard_map.74 = (f32[4,128,256]{2,1,0:T(8,128)}, f32[1,1]{1,0:T(1,128)}) custom-call(f32[16,4,8,256]{3,2,1,0:T(8,128)S(1)} %get-tuple-element.43.x_ref, f32[16,4,8,256]{3,2,1,0:T(8,128)S(1)} %get-tuple-element.31.w_ref, f32[16,8,256]{2,1,0:T(8,128)S(1)} %get-tuple-element.44.var_ref, f32[32,2,128]{2,1,0:T(2,128)S(1)} %all_to_all.5.all_ref), custom_call_target="tpu_custom_call" | custom-call | bytes 1212416 | tf_op jit(solution)/shard_map/pallas_call | solution.py:354
  (1 shorter events, 0.0 us)
Async XLA Ops:
  2.5 2.6 %collective-permute-start = (f32[4,7,8,256]{3,2,1,0:T(8,128)S(1)}, f32[4,7,8,256]{3,2,1,0:T(8,128)S(1)}, u32[]{:S(2)}, u32[]{:S(2)}) collective-permute-start(f32[4,7,8,256]{3,2,1,0:T(8,128)S(1)} %get-tuple-element.32), channel_id=1, source_target_pairs={{0,4},{4,0},{8,12},{12,8},{16,20},{20,16},{24,28},{28,24},{1,5},{5... | collective-permute-start | bytes 688136 | tf_op jit(solution)/shard_map/ppermute | solution.py:388
  3.0 9.8 %collective-permute-start.1 = (f32[4,7,8,256]{3,2,1,0:T(8,128)S(1)}, f32[4,7,8,256]{3,2,1,0:T(8,128)S(1)}, u32[]{:S(2)}, u32[]{:S(2)}) collective-permute-start(f32[4,7,8,256]{3,2,1,0:T(8,128)S(1)} %get-tuple-element.35), channel_id=1, source_target_pairs={{4,8},{8,4},{12,16},{16,12},{20,24},{24,20},{5,9},{9,5},{13,17},{1... | collective-permute-start | bytes 688136 | tf_op jit(solution)/shard_map/ppermute | solution.py:390
  3.7 1.4 %collective-permute-start.2 = (f32[2,2,8,128]{3,2,1,0:T(8,128)S(1)}, f32[2,2,8,128]{3,2,1,0:T(8,128)S(1)}, u32[]{:S(2)}, u32[]{:S(2)}) collective-permute-start(f32[2,2,8,128]{3,2,1,0:T(8,128)S(1)} %get-tuple-element.40), channel_id=1, source_target_pairs={{4,8},{8,4},{12,16},{16,12},{20,24},{24,20},{5,9},{9,5},{13,17},{1... | collective-permute-start | bytes 49160 | tf_op jit(solution)/shard_map/ppermute | solution.py:389
  5.4 7.4 %collective-permute-start.3 = (f32[12,8,128]{2,1,0:T(8,128)S(1)}, f32[12,8,128]{2,1,0:T(8,128)S(1)}, u32[]{:S(2)}, u32[]{:S(2)}) collective-permute-start(f32[12,8,128]{2,1,0:T(8,128)S(1)} %get-tuple-element.41), channel_id=1, source_target_pairs={{0,1},{1,2},{2,3},{3,0},{4,5},{5,6},{6,7},{7,4},{8,9},{9,10},{10,1... | collective-permute-start | bytes 147464 | tf_op jit(solution)/shard_map/ppermute | solution.py:394
  8.0 4.8 %collective-permute-start.4 = (f32[12,8,128]{2,1,0:T(8,128)S(1)}, f32[12,8,128]{2,1,0:T(8,128)S(1)}, u32[]{:S(2)}, u32[]{:S(2)}) collective-permute-start(f32[12,8,128]{2,1,0:T(8,128)S(1)} %get-tuple-element.42), channel_id=1, source_target_pairs={{1,0},{2,1},{3,2},{0,3},{5,4},{6,5},{7,6},{4,7},{9,8},{10,9},{11,1... | collective-permute-start | bytes 147464 | tf_op jit(solution)/shard_map/ppermute | solution.py:395

commit v8 on v7

--- a/solution.py
+++ b/solution.py
@@ -58,7 +58,7 @@
     return lambda d: (1 - odd) * (rows - 1) + step * d, step.astype(F32)
 
 
-def edge_kernel(n_ref, a_ref, b_ref, s_ref, m_ref, near_ref, far_ref, corner_ref, n_to, a_to, b_to, s_to, m_to, sem):
+def edge_kernel(n_ref, a_ref, b_ref, s_ref, m_ref, near_ref, head_ref, tail_ref, n_to, a_to, b_to, s_to, m_to, sem):
     samples, levels, tiles = n_ref.shape[0], near_ref.shape[2], n_to.shape[0]
     rows = n_ref.shape[1] // levels
     copies = []
@@ -72,20 +72,30 @@
     for copy in copies:
         copy.wait()
     row_at, _ = row_order(rows)
+    parts = lane_parts((levels, LANES))
+    edges = []
     for i in range(ITERS):
-        for out, d in ((near_ref, ITERS - 1 - i), (far_ref, rows - 1 - i)):
+        for far, d in ((False, ITERS - 1 - i), (True, rows - 1 - i)):
             at = pl.ds(row_at(d), levels, stride=rows)
+            data = [
+                [n_to[c, s, at] for s in range(samples)]
+                + list(cell_weights(a_to[c, at], b_to[c, at], s_to[c, at], m_to[c, at]))
+                for c in range(tiles)
+            ]
             for c in range(tiles):
-                lanes = pl.ds(c * LANES, LANES)
-                for s in range(samples):
-                    out[i, s, :, lanes] = n_to[c, s, at]
-                w = cell_weights(a_to[c, at], b_to[c, at], s_to[c, at], m_to[c, at])
-                for k in range(3):
-                    out[i, samples + k, :, lanes] = w[k]
-    sent = messages(halo_gets(far_ref), samples, lane_parts((levels, LANES)))
+                for g, v in enumerate(data[c]):
+                    if not far:
+                        near_ref[i, g, :, pl.ds(c * LANES, LANES)] = v
+                    elif i == 0:
+                        head_ref[ITERS + g * tiles + c] = v
+                    else:
+                        tail_ref[i - 1, g, :, pl.ds(c * LANES, LANES)] = v
+            if far:
+                edges.append(both_edges(lambda g, side: data[-side][g], samples + 3, parts))
+    sent = messages(edges, parts)
     for d in range(2):
         for i in range(ITERS // 2):
-            corner_ref[d, i] = sent[d][i]
+            head_ref[d * (ITERS // 2) + i] = sent[d][i]
 
 
 BATCH = 4
@@ -113,10 +123,13 @@
     return lines
 
 
-def messages(gets, samples, parts):
+def both_edges(get, groups, parts):
+    return [jnp.where(parts[0] < LANES // 2, get(g, 0), get(g, 1)) for g in range(groups)]
+
+
+def messages(both, parts):
     lane, seg, l32 = parts
-    left = lane < LANES // 2
-    both = [[jnp.where(left, get(g, 0), get(g, 1)) for g in range(samples + 3)] for get in gets]
+    samples = len(both[0]) - 3
     lines = [[roll(row[s], SEG * s + 4) for s in range(samples)] for row in both]
     packed = [[roll(row[samples + k], 8 * k + 12) for k in range(3)] for row in both]
     packed = replicate([jnp.where(l32 < 16, a, jnp.where(l32 < 24, b, c)) for a, b, c in packed], seg)
@@ -155,14 +168,22 @@
     return [lambda g, side, row=row: row[-side][g] for row in data]
 
 
-def message_kernel(*refs):
-    refs, msg_ref = refs[:-1], refs[-1]
+def message_kernel(n_ref, a_ref, b_ref, s_ref, m_ref, msg_ref, n_to, a_to, b_to, s_to, m_to):
     levels = msg_ref.shape[2]
-    rows, samples = refs[0].shape[2] // levels, refs[0].shape[1]
+    rows, samples, last = n_ref.shape[2] // levels, n_ref.shape[1], n_ref.shape[0] - 1
     parts = lane_parts((levels, LANES))
+    left = lax.broadcasted_iota(jnp.int32, a_to.shape, 1) < LANES // 2
+    for ref, to in ((a_ref, a_to), (b_ref, b_to), (s_ref, s_to), (m_ref, m_to)):
+        to[...] = jnp.where(left, ref[0], ref[last])
+    for s in range(samples):
+        n_to[s] = jnp.where(left, n_ref[0, s], n_ref[last, s])
+    row_at, _ = row_order(rows)
     for first in range(0, rows, BATCH):
-        data = [own_row(refs, r, rows, levels) for r in range(first, first + BATCH)]
-        sent = messages(own_gets(data), samples, parts)
+        both = []
+        for d in range(first, first + BATCH):
+            at = pl.ds(row_at(d), levels, stride=rows)
+            both.append([n_to[s, at] for s in range(samples)] + list(cell_weights(a_to[at], b_to[at], s_to[at], m_to[at])))
+        sent = messages(both, parts)
         for d in range(2):
             for i in range(BATCH // 2):
                 msg_ref[d, first // 2 + i] = sent[d][i]
@@ -193,14 +214,15 @@
     return [lambda g, side, i=i: ref[i, g, :, pl.ds(side * last, LANES)] for i in range(ITERS)]
 
 
-def join_kernel(own_ref, near_ref, corner_ref, east_ref, west_ref):
+def join_kernel(own_ref, near_ref, head_ref, east_ref, west_ref):
     pairs, half = own_ref.shape[1], ITERS // 2
-    sent = messages(halo_gets(near_ref), near_ref.shape[1] - 3, lane_parts(own_ref.shape[2:]))
+    parts = lane_parts(own_ref.shape[2:])
+    sent = messages([both_edges(get, near_ref.shape[1], parts) for get in halo_gets(near_ref)], parts)
     for d, ref in enumerate((east_ref, west_ref)):
         for i in range(half):
             ref[i] = sent[d][i]
+            ref[half + pairs + i] = head_ref[d * half + i]
         ref[half : half + pairs] = own_ref[d]
-        ref[half + pairs :] = corner_ref[d]
 
 
 def near_kernel(y_ref, w_ref, near_ref, x_ref, keep_ref, hy_ref, hw_ref, wh_ref, p_ref, q_ref):
@@ -240,27 +262,53 @@
     lax.fori_loop(0, samples, sample, 0)
 
 
-def far_rows(y_ref, w_ref, far_ref, keep_ref, wh_ref, s):
-    rows = y_ref.shape[0]
+def far_kernel(y_ref, w_ref, keep_ref, head_ref, tail_ref, x_ref, hy_ref, hw_ref, wh_ref, yh_ref):
+    rows, samples, levels, cols = y_ref.shape
     high = rows + ITERS
+    tiles = cols // LANES
+    _, sign = row_order(rows)
+
+    def tile(i, g, c):
+        return head_ref[ITERS + g * tiles + c] if i == 0 else tail_ref[i - 1, g, :, pl.ds(c * LANES, LANES)]
+
+    for i in range(ITERS):
+        for c in range(tiles):
+            lanes = pl.ds(c * LANES, LANES)
+            for k, v in enumerate(all_weights([tile(i, samples + k, c) for k in range(3)], sign)):
+                wh_ref[i, k, :, lanes] = v
+    for c in range(tiles):
+        for s in range(samples):
+            yh_ref[s, :, pl.ds(c * LANES, LANES)] = tile(0, s, c)
+    gets = [lambda g, side, i=i: tile(i, g, side * (tiles - 1)) for i in range(ITERS)]
+    lines, weights = strips(gets, samples, lane_parts((levels, LANES)))
+    for i in range(ITERS):
+        hy_ref[i] = lines[i]
+        for k in range(3):
+            hw_ref[i, k] = weights[i][k]
 
     def get_w(r):
         ref, i = (wh_ref, r - high) if r >= high else (w_ref, r - ITERS)
         return [ref[i, k] for k in range(4)]
 
-    source = lambda r: far_ref[r - high, s] if r >= high else y_ref[r - ITERS, s]
-    for step in range(ITERS):
-        new = {}
-        stencil(source, get_w, high - 1 - step, high - 1 - step + ITERS, new.__setitem__)
-        if step < ITERS - 1:
-            new[high - 3 - step], new[high - 2 - step] = keep_ref[step, 0, s], keep_ref[step, 1, s]
-        source = new.__getitem__
-    return new
+    for s in range(samples):
+
+        def source(r, s=s):
+            if r < high:
+                return y_ref[r - ITERS, s]
+            return yh_ref[s] if r == high else tail_ref[r - high - 1, s]
+
+        for step in range(ITERS):
+            new = {}
+            stencil(source, get_w, high - 1 - step, high - 1 - step + ITERS, new.__setitem__)
+            if step < ITERS - 1:
+                new[high - 3 - step], new[high - 2 - step] = keep_ref[step, 0, s], keep_ref[step, 1, s]
+            source = new.__getitem__
+        for r, v in new.items():
+            x_ref[r - rows, s] = v
 
 
 def finish_kernel(
-    x_ref, y_ref, w_ref, keep_ref, far_ref, sy_ref, sw_ref, hy_ref, hw_ref, left_ref, right_ref,
-    out_ref, var_ref, sum_ref, wh_ref,
+    x_ref, xf_ref, w_ref, sy_ref, sw_ref, hy_ref, hw_ref, fy_ref, fw_ref, left_ref, right_ref, out_ref, var_ref, sum_ref
 ):
     rows, samples, levels, cols = x_ref.shape
     high = rows + 2 * ITERS
@@ -269,17 +317,12 @@
     from_left, from_right = l32 < 4, l32 >= 28
     _, sign = row_order(rows)
 
-    for i in range(ITERS):
-        for k, v in enumerate(all_weights([far_ref[i, samples + k] for k in range(3)], sign)):
-            wh_ref[i, k] = v
-    far_lines, far_weights = strips(halo_gets(far_ref), samples, parts)
-
     def strip_at(r):
         if r < ITERS:
             return hy_ref[r], [hw_ref[r, k] for k in range(3)]
         if r < ITERS + rows:
             return sy_ref[r - ITERS], [sw_ref[r - ITERS, k] for k in range(3)]
-        return far_lines[r - ITERS - rows], far_weights[r - ITERS - rows]
+        return fy_ref[r - ITERS - rows], [fw_ref[r - ITERS - rows, k] for k in range(3)]
 
     field, weights = {}, {}
     for r in range(high):
@@ -298,10 +341,6 @@
         stencil(field.__getitem__, weights.__getitem__, step + 1, high - 1 - step, new.__setitem__)
         field = new
 
-    for s in range(samples):
-        for r, v in far_rows(y_ref, w_ref, far_ref, keep_ref, wh_ref, s).items():
-            out_ref[r - ITERS, s] = v
-
     total, count = None, None
     for r in range(rows):
         strip = field[ITERS + r]
@@ -309,7 +348,7 @@
             lanes = pl.ds(c, LANES)
             square = None
             for s in range(samples):
-                v = (x_ref if r < rows - ITERS else out_ref)[r, s, :, lanes]
+                v = x_ref[r, s, :, lanes] if r < rows - ITERS else xf_ref[r - rows + ITERS, s, :, lanes]
                 if c == 0:
                     v = jnp.where(lane < 4, roll(strip, -(SEG * s + 4)), v)
                 if c == cols - LANES:
@@ -378,19 +417,27 @@
     tiles = cols // LANES
     plane = (tiles, levels * rows, LANES)
     flat = [pltpu.with_memory_space_constraint(a, pltpu.HBM) for a in flat]
-    to_near, to_far, to_corner, *staged = call(
+    head = (ITERS + (samples + 3) * tiles, levels, LANES)
+    to_near, to_far, to_far_tail, *staged = call(
         edge_kernel,
-        [halo, halo, (2, ITERS // 2, levels, LANES), (tiles, samples, levels * rows, LANES)] + [plane] * 3 + [jax.ShapeDtypeStruct(plane, sea_mask.dtype)],
+        [halo, head, (ITERS - 1, *halo[1:]), (tiles, samples, levels * rows, LANES)] + [plane] * 3 + [jax.ShapeDtypeStruct(plane, sea_mask.dtype)],
         *flat,
         scratch=[pltpu.SemaphoreType.DMA((tiles, 5))],
         in_space=pltpu.HBM,
     )
     near = lax.ppermute(to_near, "lat", pair)
-    corner = lax.ppermute(to_corner, "lat", across)
     far = lax.ppermute(to_far, "lat", across)
-    (own_msg,) = call(message_kernel, [(2, rows // 2, levels, LANES)], *staged, flops=10**6)
+    far_tail = lax.ppermute(to_far_tail, "lat", across)
+    flat_plane = plane[1:]
+    (own_msg,) = call(
+        message_kernel,
+        [(2, rows // 2, levels, LANES)],
+        *staged,
+        scratch=[(samples, *flat_plane)] + [flat_plane] * 3 + [pltpu.VMEM(flat_plane, sea_mask.dtype)],
+        flops=10**6,
+    )
     message = (high // 2, levels, LANES)
-    to_east, to_west = call(join_kernel, [message, message], own_msg, near, corner)
+    to_east, to_west = call(join_kernel, [message, message], own_msg, near, far)
     left = lax.ppermute(to_east, "lon", east)
     right = lax.ppermute(to_west, "lon", west)
     strip = (rows, levels, LANES)
@@ -411,21 +458,31 @@
         scratch=[(ITERS, 4, levels, cols), buffer, buffer],
         flops=10**7,
     )
+    x_far, fy, fw = call(
+        far_kernel,
+        [(ITERS, samples, levels, cols), *side],
+        y,
+        w,
+        keep,
+        far,
+        far_tail,
+        scratch=[(ITERS, 4, levels, cols), (samples, levels, cols)],
+        flops=10**6,
+    )
     x, var, part = call(
         finish_kernel,
         [y.shape, (rows, levels, cols), (2, LANES)],
         x,
-        y,
+        x_far,
         w,
-        keep,
-        far,
         sy,
         sw,
         hy,
         hw,
+        fy,
+        fw,
         left,
         right,
-        scratch=[(ITERS, 4, levels, cols)],
     )
     spread = jnp.broadcast_to(part, (n_lat * n_lon, 2, LANES))
     every = lax.all_to_all(spread, ("lat", "lon"), 0, 0, tiled=True)

time: 36.5 us -> 35.5 us (0.973)
  blocking collectives: 20.2 us -> 19.6 us
  Pallas kernels: 8.85 us -> 8.38 us
    all_to_all x1, blocking collectives: 20.2 us -> 19.6 us  [shards(): every = lax.all_to_all(spread, ('lat', 'lon'), 0, 0, tiled=True)]
    pallas_call x7 -> x8, Pallas kernels: 8.85 us -> 8.38 us  [call(): pl.pallas_call(kernel, out_shape=out, in_specs=[pl.BlockSpec(memory_space...]
  transfers between devices with their start and end apart: 5 -> 5, of which waited for: 0 -> 0; matrix products, arithmetic and copies ran while one was open for 0% -> 0% of each run, Pallas kernels for 10% -> 12%
where the time goes in v8:
time: 35.5 us; the launch traced here: 35.3 us
  blocking collectives  19.6 us (55%)
  Pallas kernels  8.38 us (24%)
  starting transfers between devices  6.55 us (18%)
  between operations  0.73 us (2%)
    all_to_all x1, blocking collectives, shards(): every = lax.all_to_all(spread, ('lat', 'lon'), 0, 0, tiled=True)  19.6 us
    pallas_call x8, Pallas kernels, call(): pl.pallas_call(kernel, out_shape=out, in_specs=[pl.BlockSpec(memory_space...  8.38 us
    ppermute x1, starting transfers between devices, shards(): left = lax.ppermute(to_east, 'lon', east)  2.6 us
    ppermute x1, starting transfers between devices, shards(): right = lax.ppermute(to_west, 'lon', west)  2.07 us
  transfers between devices with their start and end apart: 5, of which 0 were waited for; matrix products, arithmetic and copies ran while one was open for 0% of the time, Pallas kernels for 12%

profile of v8, /device:TPU:0, one launch (start us, length us, event | category | flops | bytes accessed | tf_op | source)
XLA Modules:
  0.0 35.3 jit_solution(11544860214482352473)
XLA Ops:
  0.6 1.8 %shard_map.68 = (f32[4,7,8,256]{3,2,1,0:T(8,128)S(1)}, f32[18,8,128]{2,1,0:T(8,128)S(1)}, f32[3,7,8,256]{3,2,1,0:T(8,128)S(1)}, f32[2,4,128,128]{3,2,1,0:T(8,128...) custom-call(f32[4,128,256]{2,1,0:T(8,128)} %bitcast.7, ...), custom_call_target="tpu_custom_call" | custom-call | bytes 1048576 | tf_op jit(solution)/shard_map/pallas_call | solution.py:393
  2.5 0.6 %collective-permute-start = (f32[4,7,8,256]{3,2,1,0:T(8,128)S(1)}, f32[4,7,8,256]{3,2,1,0:T(8,128)S(1)}, u32[]{:S(2)}, u32[]{:S(2)}) collective-permute-start(f32[4,7,8,256]{3,2,1,0:T(8,128)S(1)} %get-tuple-element.35), channel_id=1, source_target_pairs={{0,4},{4,0},{8,12},{12,8},{16,20},{20,16},{24,28},{28,24},{1,5},{5... | collective-permute-start | bytes 688136 | tf_op jit(solution)/shard_map/ppermute | solution.py:428
  3.0 0.7 %collective-permute-start.2 = (f32[3,7,8,256]{3,2,1,0:T(8,128)S(1)}, f32[3,7,8,256]{3,2,1,0:T(8,128)S(1)}, u32[]{:S(2)}, u32[]{:S(2)}) collective-permute-start(f32[3,7,8,256]{3,2,1,0:T(8,128)S(1)} %get-tuple-element.39), channel_id=1, source_target_pairs={{4,8},{8,4},{12,16},{16,12},{20,24},{24,20},{5,9},{9,5},{13,17},{1... | collective-permute-start | bytes 516104 | tf_op jit(solution)/shard_map/ppermute | solution.py:430
  3.7 0.7 %collective-permute-start.1 = (f32[18,8,128]{2,1,0:T(8,128)S(1)}, f32[18,8,128]{2,1,0:T(8,128)S(1)}, u32[]{:S(2)}, u32[]{:S(2)}) collective-permute-start(f32[18,8,128]{2,1,0:T(8,128)S(1)} %get-tuple-element.38), channel_id=1, source_target_pairs={{4,8},{8,4},{12,16},{16,12},{20,24},{24,20},{5,9},{9,5},{13,17},{1... | collective-permute-start | bytes 221192 | tf_op jit(solution)/shard_map/ppermute | solution.py:429
  4.4 0.5 %shard_map.72.own_ref = f32[2,8,8,128]{3,2,1,0:T(8,128)S(1)} custom-call(f32[2,4,128,128]{3,2,1,0:T(8,128)S(1)} %get-tuple-element.28.n_ref, f32[2,128,128]{2,1,0:T(8,128)S(1)} %get-tuple-element.29.a_ref, f32[2,128,128]{2,1,0:T(8,128)S(1)} %get-tuple-element.30.b_ref, f32[2,128,128]{2,1,0:T(8,128)S(1)} %get-tuple-element.31.s_ref, ...), custom_call_target="tpu_custom_call" | custom-call | flops 1000000 | bytes 1048576 | tf_op jit(solution)/shard_map/pallas_call | solution.py:393
  4.9 0.0 collective-permute-done.1.head_ref
  4.9 0.0 collective-permute-done.near_ref
  4.9 0.3 shard_map.73
  5.2 2.6 %collective-permute-start.3 = (f32[12,8,128]{2,1,0:T(8,128)S(1)}, f32[12,8,128]{2,1,0:T(8,128)S(1)}, u32[]{:S(2)}, u32[]{:S(2)}) collective-permute-start(f32[12,8,128]{2,1,0:T(8,128)S(1)} %get-tuple-element.47), channel_id=1, source_target_pairs={{0,1},{1,2},{2,3},{3,0},{4,5},{5,6},{6,7},{7,4},{8,9},{9,10},{10,1... | collective-permute-start | bytes 147464 | tf_op jit(solution)/shard_map/ppermute | solution.py:441
  7.8 2.1 %collective-permute-start.4 = (f32[12,8,128]{2,1,0:T(8,128)S(1)}, f32[12,8,128]{2,1,0:T(8,128)S(1)}, u32[]{:S(2)}, u32[]{:S(2)}) collective-permute-start(f32[12,8,128]{2,1,0:T(8,128)S(1)} %get-tuple-element.48), channel_id=1, source_target_pairs={{1,0},{2,1},{3,2},{0,3},{5,4},{6,5},{7,6},{4,7},{9,8},{10,9},{11,1... | collective-permute-start | bytes 147464 | tf_op jit(solution)/shard_map/ppermute | solution.py:442
  9.9 0.8 %shard_map.69 = (f32[16,4,8,256]{3,2,1,0:T(8,128)S(1)}, f32[16,4,8,256]{3,2,1,0:T(8,128)S(1)}, f32[16,8,128]{2,1,0:T(8,128)S(1)}, f32[16,3,8,128]{3,2,1,0:T(8,128)S(1)}) custom-call(f32[2,4,128,128]{3,2,1,0:T(8,128)S(1)} %get-tuple-element.28.n_ref, f32[2,128,128]{2,1,0:T(8,128)S(1)} %get-tuple-element.29.a_ref, f32[2,128,128]{2,1,0:T(8,128)S(1)} %get-tuple-element.30.b_ref, ...), custom_call_target="tpu_custom_call" | custom-call | flops 1000000 | bytes 1048576 | tf_op jit(solution)/shard_map/pallas_call | solution.py:393
  10.7 1.9 %shard_map.70 = (f32[16,4,8,256]{3,2,1,0:T(8,128)S(1)}, f32[3,2,4,8,256]{4,3,2,1,0:T(8,128)S(1)}, f32[4,8,128]{2,1,0:T(8,128)S(1)}, f32[4,3,8,128]{3,2,1,0:T(8,128)S(1)}) custom-call(f32[16,4,8,256]{3,2,1,0:T(8,128)S(1)} %get-tuple-element.33.y_ref, f32[16,4,8,256]{3,2,1,0:T(8,128)S(1)} %get-tuple-element.34.w_ref, ...), custom_call_target="tpu_custom_call" | custom-call | flops 10000000 | bytes 1277952 | tf_op jit(solution)/shard_map/pallas_call | solution.py:393
  12.6 0.0 collective-permute-done.2.tail_ref
  12.6 0.8 %shard_map.71 = (f32[4,4,8,256]{3,2,1,0:T(8,128)S(1)}, f32[4,8,128]{2,1,0:T(8,128)S(1)}, f32[4,3,8,128]{3,2,1,0:T(8,128)S(1)}) custom-call(f32[16,4,8,256]{3,2,1,0:T(8,128)S(1)} %get-tuple-element.33.y_ref, f32[16,4,8,256]{3,2,1,0:T(8,128)S(1)} %get-tuple-element.34.w_ref, f32[3,2,4,8,256]{4,3,2,1,0:T(8,128)S(1)} %get-tuple-element.37.keep_ref, ...), custom_call_target="tpu_custom_call" | custom-call | flops 1000000 | bytes 1490944 | tf_op jit(solution)/shard_map/pallas_call | solution.py:393
  13.4 0.0 collective-permute-done.3.left_ref
  13.4 0.0 collective-permute-done.4.right_ref
  13.4 0.7 %shard_map.74 = (f32[16,4,8,256]{3,2,1,0:T(8,128)S(1)}, f32[16,8,256]{2,1,0:T(8,128)S(1)}, f32[2,128]{1,0:T(2,128)S(1)}) custom-call(f32[16,4,8,256]{3,2,1,0:T(8,128)S(1)} %get-tuple-element.36.x_ref, f32[4,4,8,256]{3,2,1,0:T(8,128)S(1)} %get-tuple-element.40.xf_ref, f32[16,4,8,256]{3,2,1,0:T(8,128)S(1)} %get-tuple-element.34.w_ref, ...), custom_call_target="tpu_custom_call" | custom-call | bytes 1671168 | tf_op jit(solution)/shard_map/pallas_call | solution.py:393
  14.1 19.6 %all_to_all.5.all_ref = f32[32,2,128]{2,1,0:T(2,128)S(1)} all-to-all(f32[32,2,128]{2,1,0:T(2,128)S(1)} %broadcast_in_dim.3), channel_id=1, replica_groups=mesh['lat'=8,'lon'=4] {'lat','lon'}, dimensions={0} | all-to-all | bytes 65536 | tf_op jit(solution)/shard_map/all_to_all | solution.py:488
  33.7 1.5 %shard_map.75 = (f32[4,128,256]{2,1,0:T(8,128)}, f32[1,1]{1,0:T(1,128)}) custom-call(f32[16,4,8,256]{3,2,1,0:T(8,128)S(1)} %get-tuple-element.49.x_ref, f32[16,4,8,256]{3,2,1,0:T(8,128)S(1)} %get-tuple-element.34.w_ref, f32[16,8,256]{2,1,0:T(8,128)S(1)} %get-tuple-element.50.var_ref, f32[32,2,128]{2,1,0:T(2,128)S(1)} %all_to_all.5.all_ref), custom_call_target="tpu_custom_call" | custom-call | bytes 1212416 | tf_op jit(solution)/shard_map/pallas_call | solution.py:393
  (1 shorter events, 0.0 us)
Async XLA Ops:
  2.5 2.5 %collective-permute-start = (f32[4,7,8,256]{3,2,1,0:T(8,128)S(1)}, f32[4,7,8,256]{3,2,1,0:T(8,128)S(1)}, u32[]{:S(2)}, u32[]{:S(2)}) collective-permute-start(f32[4,7,8,256]{3,2,1,0:T(8,128)S(1)} %get-tuple-element.35), channel_id=1, source_target_pairs={{0,4},{4,0},{8,12},{12,8},{16,20},{20,16},{24,28},{28,24},{1,5},{5... | collective-permute-start | bytes 688136 | tf_op jit(solution)/shard_map/ppermute | solution.py:428
  3.0 9.6 %collective-permute-start.2 = (f32[3,7,8,256]{3,2,1,0:T(8,128)S(1)}, f32[3,7,8,256]{3,2,1,0:T(8,128)S(1)}, u32[]{:S(2)}, u32[]{:S(2)}) collective-permute-start(f32[3,7,8,256]{3,2,1,0:T(8,128)S(1)} %get-tuple-element.39), channel_id=1, source_target_pairs={{4,8},{8,4},{12,16},{16,12},{20,24},{24,20},{5,9},{9,5},{13,17},{1... | collective-permute-start | bytes 516104 | tf_op jit(solution)/shard_map/ppermute | solution.py:430
  3.7 1.2 %collective-permute-start.1 = (f32[18,8,128]{2,1,0:T(8,128)S(1)}, f32[18,8,128]{2,1,0:T(8,128)S(1)}, u32[]{:S(2)}, u32[]{:S(2)}) collective-permute-start(f32[18,8,128]{2,1,0:T(8,128)S(1)} %get-tuple-element.38), channel_id=1, source_target_pairs={{4,8},{8,4},{12,16},{16,12},{20,24},{24,20},{5,9},{9,5},{13,17},{1... | collective-permute-start | bytes 221192 | tf_op jit(solution)/shard_map/ppermute | solution.py:429
  5.2 8.2 %collective-permute-start.3 = (f32[12,8,128]{2,1,0:T(8,128)S(1)}, f32[12,8,128]{2,1,0:T(8,128)S(1)}, u32[]{:S(2)}, u32[]{:S(2)}) collective-permute-start(f32[12,8,128]{2,1,0:T(8,128)S(1)} %get-tuple-element.47), channel_id=1, source_target_pairs={{0,1},{1,2},{2,3},{3,0},{4,5},{5,6},{6,7},{7,4},{8,9},{9,10},{10,1... | collective-permute-start | bytes 147464 | tf_op jit(solution)/shard_map/ppermute | solution.py:441
  7.8 5.6 %collective-permute-start.4 = (f32[12,8,128]{2,1,0:T(8,128)S(1)}, f32[12,8,128]{2,1,0:T(8,128)S(1)}, u32[]{:S(2)}, u32[]{:S(2)}) collective-permute-start(f32[12,8,128]{2,1,0:T(8,128)S(1)} %get-tuple-element.48), channel_id=1, source_target_pairs={{1,0},{2,1},{3,2},{0,3},{5,4},{6,5},{7,6},{4,7},{9,8},{10,9},{11,1... | collective-permute-start | bytes 147464 | tf_op jit(solution)/shard_map/ppermute | solution.py:442

commit v9 on v8

--- a/solution.py
+++ b/solution.py
@@ -37,6 +37,16 @@
     return lane, lane // SEG, lane % SEG
 
 
+def shift(x, by):
+    tiles = [roll(x[:, c : c + LANES], by) for c in range(0, x.shape[1], LANES)]
+    lane = lax.broadcasted_iota(jnp.int32, tiles[0].shape, 1)
+    if by > 0:
+        joined = tiles[:1] + [jnp.where(lane == 0, a, b) for a, b in zip(tiles, tiles[1:])]
+    else:
+        joined = [jnp.where(lane == LANES - 1, b, a) for a, b in zip(tiles, tiles[1:])] + tiles[-1:]
+    return jnp.concatenate(joined, axis=1) if len(joined) > 1 else joined[0]
+
+
 def stencil(get_y, get_w, first, last, put):
     def products(r):
         y = get_y(r)
@@ -48,7 +58,7 @@
         after = products(r + 1)
         d, _, b, _ = here
         g = prev[3] - after[3]
-        put(r, d + (prev[1] + after[1]) + roll(b + g, 1) + roll(b - g, -1))
+        put(r, d + (prev[1] + after[1]) + shift(b + g, 1) + shift(b - g, -1))
         prev, here = here, after
 
 
@@ -66,32 +76,43 @@
         lanes = pl.ds(c * LANES, LANES)
         for k, (ref, to) in enumerate(((a_ref, a_to), (b_ref, b_to), (s_ref, s_to), (m_ref, m_to))):
             copies.append(pltpu.make_async_copy(ref.at[:, lanes], to.at[c], sem.at[c, k]))
+    for c in range(tiles):
+        lanes = pl.ds(c * LANES, LANES)
         copies.append(pltpu.make_async_copy(n_ref.at[:, :, lanes], n_to.at[c], sem.at[c, 4]))
     for copy in copies:
         copy.start()
-    for copy in copies:
-        copy.wait()
     row_at, _ = row_order(rows)
     parts = lane_parts((levels, LANES))
-    edges = []
-    for i in range(ITERS):
-        for far, d in ((False, ITERS - 1 - i), (True, rows - 1 - i)):
-            at = pl.ds(row_at(d), levels, stride=rows)
-            data = [
-                [n_to[c, s, at] for s in range(samples)]
-                + list(cell_weights(a_to[c, at], b_to[c, at], s_to[c, at], m_to[c, at]))
-                for c in range(tiles)
-            ]
-            for c in range(tiles):
-                for g, v in enumerate(data[c]):
-                    if not far:
-                        near_ref[i, g, :, pl.ds(c * LANES, LANES)] = v
-                    elif i == 0:
-                        head_ref[ITERS + g * tiles + c] = v
-                    else:
-                        tail_ref[i - 1, g, :, pl.ds(c * LANES, LANES)] = v
-            if far:
-                edges.append(both_edges(lambda g, side: data[-side][g], samples + 3, parts))
+
+    def put(i, far, g, c, v):
+        if not far:
+            near_ref[i, g, :, pl.ds(c * LANES, LANES)] = v
+        elif i == 0:
+            head_ref[ITERS + g * tiles + c] = v
+        else:
+            tail_ref[i - 1, g, :, pl.ds(c * LANES, LANES)] = v
+
+    blocks = [(i, far, row_at(rows - 1 - i if far else ITERS - 1 - i)) for i in range(ITERS) for far in (False, True)]
+    data = {}
+    for copy in copies[: 4 * tiles]:
+        copy.wait()
+    for i, far, r in blocks:
+        at = pl.ds(r, levels, stride=rows)
+        for c in range(tiles):
+            for k, v in enumerate(cell_weights(a_to[c, at], b_to[c, at], s_to[c, at], m_to[c, at])):
+                put(i, far, samples + k, c, v)
+                data[i, far, samples + k, c] = v
+    for copy in copies[4 * tiles :]:
+        copy.wait()
+    for i, far, r in blocks:
+        for c in range(tiles):
+            for s in range(samples):
+                v = n_to[c, s, pl.ds(r, levels, stride=rows)]
+                put(i, far, s, c, v)
+                data[i, far, s, c] = v
+    edges = [
+        both_edges(lambda g, side: data[i, True, g, side * (tiles - 1)], samples + 3, parts) for i in range(ITERS)
+    ]
     sent = messages(edges, parts)
     for d in range(2):
         for i in range(ITERS // 2):
@@ -168,8 +189,8 @@
     return [lambda g, side, row=row: row[-side][g] for row in data]
 
 
-def message_kernel(n_ref, a_ref, b_ref, s_ref, m_ref, msg_ref, n_to, a_to, b_to, s_to, m_to):
-    levels = msg_ref.shape[2]
+def message_kernel(n_ref, a_ref, b_ref, s_ref, m_ref, near_ref, head_ref, east_ref, west_ref, n_to, a_to, b_to, s_to, m_to):
+    levels, half = east_ref.shape[1], ITERS // 2
     rows, samples, last = n_ref.shape[2] // levels, n_ref.shape[1], n_ref.shape[0] - 1
     parts = lane_parts((levels, LANES))
     left = lax.broadcasted_iota(jnp.int32, a_to.shape, 1) < LANES // 2
@@ -183,10 +204,14 @@
         for d in range(first, first + BATCH):
             at = pl.ds(row_at(d), levels, stride=rows)
             both.append([n_to[s, at] for s in range(samples)] + list(cell_weights(a_to[at], b_to[at], s_to[at], m_to[at])))
-        sent = messages(both, parts)
-        for d in range(2):
+        for ref, sent in zip((east_ref, west_ref), messages(both, parts)):
             for i in range(BATCH // 2):
-                msg_ref[d, first // 2 + i] = sent[d][i]
+                ref[half + first // 2 + i] = sent[i]
+    near = [both_edges(get, near_ref.shape[1], parts) for get in halo_gets(near_ref)]
+    for d, (ref, sent) in enumerate(zip((east_ref, west_ref), messages(near, parts))):
+        for i in range(half):
+            ref[i] = sent[i]
+            ref[half + rows // 2 + i] = head_ref[d * half + i]
 
 
 def own_kernel(n_ref, a_ref, b_ref, s_ref, m_ref, y_ref, w_ref, sy_ref, sw_ref):
@@ -214,17 +239,6 @@
     return [lambda g, side, i=i: ref[i, g, :, pl.ds(side * last, LANES)] for i in range(ITERS)]
 
 
-def join_kernel(own_ref, near_ref, head_ref, east_ref, west_ref):
-    pairs, half = own_ref.shape[1], ITERS // 2
-    parts = lane_parts(own_ref.shape[2:])
-    sent = messages([both_edges(get, near_ref.shape[1], parts) for get in halo_gets(near_ref)], parts)
-    for d, ref in enumerate((east_ref, west_ref)):
-        for i in range(half):
-            ref[i] = sent[d][i]
-            ref[half + pairs + i] = head_ref[d * half + i]
-        ref[half : half + pairs] = own_ref[d]
-
-
 def near_kernel(y_ref, w_ref, near_ref, x_ref, keep_ref, hy_ref, hw_ref, wh_ref, p_ref, q_ref):
     rows, samples, levels, _ = y_ref.shape
     high = rows + ITERS
@@ -308,7 +322,7 @@
 
 
 def finish_kernel(
-    x_ref, xf_ref, w_ref, sy_ref, sw_ref, hy_ref, hw_ref, fy_ref, fw_ref, left_ref, right_ref, out_ref, var_ref, sum_ref
+    x_ref, xf_ref, w_ref, sy_ref, sw_ref, hy_ref, hw_ref, fy_ref, fw_ref, left_ref, right_ref, out_ref, sum_ref
 ):
     rows, samples, levels, cols = x_ref.shape
     high = rows + 2 * ITERS
@@ -342,45 +356,43 @@
         field = new
 
     total, count = None, None
+    row_at, _ = row_order(rows)
     for r in range(rows):
         strip = field[ITERS + r]
-        for c in range(0, cols, LANES):
-            lanes = pl.ds(c, LANES)
-            square = None
+        for c in range(cols // LANES):
+            lanes = pl.ds(c * LANES, LANES)
+            values = []
             for s in range(samples):
                 v = x_ref[r, s, :, lanes] if r < rows - ITERS else xf_ref[r - rows + ITERS, s, :, lanes]
                 if c == 0:
                     v = jnp.where(lane < 4, roll(strip, -(SEG * s + 4)), v)
-                if c == cols - LANES:
+                if c == cols // LANES - 1:
                     v = jnp.where(lane >= LANES - 4, roll(strip, LANES - SEG * s - 28), v)
-                out_ref[r, s, :, lanes] = v
-                square = v * v if square is None else square + v * v
-            var = square / samples
-            var_ref[r, :, lanes] = var
-            m = jnp.where(w_ref[r, 1, :, lanes] > 0, 1.0, 0.0)
+                values.append(v)
+            var = sum(v * v for v in values[1:]) + values[0] * values[0]
+            var = var / samples
+            wet = w_ref[r, 1, :, lanes] > 0
+            m = jnp.where(wet, 1.0, 0.0)
             total = m * var if total is None else total + m * var
             count = m if count is None else count + m
+            factor = m * jnp.sqrt(1.0 / (jnp.where(wet, var, 1.0) + 1e-06))
+            for s in range(samples):
+                out_ref[c, s, pl.ds(row_at(r), levels, stride=rows)] = values[s] * factor
     sum_ref[0:1] = jnp.sum(total, axis=0, keepdims=True)
     sum_ref[1:2] = jnp.sum(count, axis=0, keepdims=True)
 
 
-def scale_kernel(x_ref, w_ref, var_ref, all_ref, out_ref, mean_ref, stage, sem):
-    rows, samples, levels, cols = x_ref.shape
+def scale_kernel(x_ref, all_ref, out_ref, mean_ref, stage, sem):
+    tiles, samples = x_ref.shape[:2]
     sums = jnp.sum(jnp.sum(all_ref[...], axis=0), axis=1, keepdims=True)
     mean = sums[0:1] / sums[1:2]
     mean_ref[...] = mean
-    row_at, _ = row_order(rows)
+    factor = jnp.sqrt(mean)
     copies = []
-    for c in range(cols // LANES):
-        lanes = pl.ds(c * LANES, LANES)
-        factors = []
-        for r in range(rows):
-            wet = w_ref[r, 1, :, lanes] > 0
-            safe = jnp.where(wet, var_ref[r, :, lanes], 1.0)
-            factors.append(jnp.where(wet, jnp.sqrt(mean / (safe + 1e-06)), 0.0))
+    for c in range(tiles):
         for s in range(samples):
-            for r in range(rows):
-                stage[c, s, pl.ds(row_at(r), levels, stride=rows)] = x_ref[r, s, :, lanes] * factors[r]
+            stage[c, s] = x_ref[c, s] * factor
+            lanes = pl.ds(c * LANES, LANES)
             copies.append(pltpu.make_async_copy(stage.at[c, s], out_ref.at[s, :, lanes], sem.at[c, s]))
             copies[-1].start()
     for copy in copies:
@@ -429,15 +441,16 @@
     far = lax.ppermute(to_far, "lat", across)
     far_tail = lax.ppermute(to_far_tail, "lat", across)
     flat_plane = plane[1:]
-    (own_msg,) = call(
+    message = (high // 2, levels, LANES)
+    to_east, to_west = call(
         message_kernel,
-        [(2, rows // 2, levels, LANES)],
+        [message, message],
         *staged,
+        near,
+        far,
         scratch=[(samples, *flat_plane)] + [flat_plane] * 3 + [pltpu.VMEM(flat_plane, sea_mask.dtype)],
         flops=10**6,
     )
-    message = (high // 2, levels, LANES)
-    to_east, to_west = call(join_kernel, [message, message], own_msg, near, far)
     left = lax.ppermute(to_east, "lon", east)
     right = lax.ppermute(to_west, "lon", west)
     strip = (rows, levels, LANES)
@@ -469,9 +482,10 @@
         scratch=[(ITERS, 4, levels, cols), (samples, levels, cols)],
         flops=10**6,
     )
-    x, var, part = call(
+    stage = (tiles, samples, levels * rows, LANES)
+    x, part = call(
         finish_kernel,
-        [y.shape, (rows, levels, cols), (2, LANES)],
+        [stage, (2, LANES)],
         x,
         x_far,
         w,
@@ -490,10 +504,8 @@
         scale_kernel,
         [(samples, levels * rows, cols), (1, 1)],
         x,
-        w,
-        var,
         every,
-        scratch=[(tiles, samples, levels * rows, LANES), pltpu.SemaphoreType.DMA((tiles, samples))],
+        scratch=[stage, pltpu.SemaphoreType.DMA((tiles, samples))],
         out_space=[pl.ANY, pltpu.VMEM],
     )
     return out.reshape(noise.shape), mean.reshape(())

time: 35.5 us -> 35.9 us (1.011)
  blocking collectives: 19.6 us -> 20.1 us
    all_to_all x1, blocking collectives: 19.6 us -> 20.1 us  [shards(): every = lax.all_to_all(spread, ('lat', 'lon'), 0, 0, tiled=True)]
    pallas_call x8 -> x7, Pallas kernels: 8.38 us -> 8.21 us  [call(): pl.pallas_call(kernel, out_shape=out, in_specs=[pl.BlockSpec(memory_space...]
  transfers between devices with their start and end apart: 5 -> 5, of which waited for: 0 -> 0; matrix products, arithmetic and copies ran while one was open for 0% -> 0% of each run, Pallas kernels for 12% -> 11%
where the time goes in v9:
time: 35.9 us; the launch traced here: 35.7 us
  blocking collectives  20.1 us (56%)
  Pallas kernels  8.21 us (23%)
  starting transfers between devices  6.71 us (19%)
  between operations  0.74 us (2%)
    all_to_all x1, blocking collectives, shards(): every = lax.all_to_all(spread, ('lat', 'lon'), 0, 0, tiled=True)  20.1 us
    pallas_call x7, Pallas kernels, call(): pl.pallas_call(kernel, out_shape=out, in_specs=[pl.BlockSpec(memory_space...  8.21 us
    ppermute x1, starting transfers between devices, shards(): left = lax.ppermute(to_east, 'lon', east)  2.74 us
    ppermute x1, starting transfers between devices, shards(): right = lax.ppermute(to_west, 'lon', west)  2.09 us
  transfers between devices with their start and end apart: 5, of which 0 were waited for; matrix products, arithmetic and copies ran while one was open for 0% of the time, Pallas kernels for 11%

profile of v9, /device:TPU:0, one launch (start us, length us, event | category | flops | bytes accessed | tf_op | source)
XLA Modules:
  0.0 35.7 jit_solution(5566048580299695700)
XLA Ops:
  0.6 1.7 %shard_map.68 = (f32[4,7,8,256]{3,2,1,0:T(8,128)S(1)}, f32[18,8,128]{2,1,0:T(8,128)S(1)}, f32[3,7,8,256]{3,2,1,0:T(8,128)S(1)}, f32[2,4,128,128]{3,2,1,0:T(8,128...) custom-call(f32[4,128,256]{2,1,0:T(8,128)} %bitcast.7, ...), custom_call_target="tpu_custom_call" | custom-call | bytes 1048576 | tf_op jit(solution)/shard_map/pallas_call | solution.py:405
  2.4 0.6 %collective-permute-start = (f32[4,7,8,256]{3,2,1,0:T(8,128)S(1)}, f32[4,7,8,256]{3,2,1,0:T(8,128)S(1)}, u32[]{:S(2)}, u32[]{:S(2)}) collective-permute-start(f32[4,7,8,256]{3,2,1,0:T(8,128)S(1)} %get-tuple-element.34), channel_id=1, source_target_pairs={{0,4},{4,0},{8,12},{12,8},{16,20},{20,16},{24,28},{28,24},{1,5},{5... | collective-permute-start | bytes 688136 | tf_op jit(solution)/shard_map/ppermute | solution.py:440
  2.9 0.7 %collective-permute-start.2 = (f32[3,7,8,256]{3,2,1,0:T(8,128)S(1)}, f32[3,7,8,256]{3,2,1,0:T(8,128)S(1)}, u32[]{:S(2)}, u32[]{:S(2)}) collective-permute-start(f32[3,7,8,256]{3,2,1,0:T(8,128)S(1)} %get-tuple-element.38), channel_id=1, source_target_pairs={{4,8},{8,4},{12,16},{16,12},{20,24},{24,20},{5,9},{9,5},{13,17},{1... | collective-permute-start | bytes 516104 | tf_op jit(solution)/shard_map/ppermute | solution.py:442
  3.6 0.7 %collective-permute-start.1 = (f32[18,8,128]{2,1,0:T(8,128)S(1)}, f32[18,8,128]{2,1,0:T(8,128)S(1)}, u32[]{:S(2)}, u32[]{:S(2)}) collective-permute-start(f32[18,8,128]{2,1,0:T(8,128)S(1)} %get-tuple-element.37), channel_id=1, source_target_pairs={{4,8},{8,4},{12,16},{16,12},{20,24},{24,20},{5,9},{9,5},{13,17},{1... | collective-permute-start | bytes 221192 | tf_op jit(solution)/shard_map/ppermute | solution.py:441
  4.3 0.0 collective-permute-done.1.head_ref
  4.3 0.0 collective-permute-done.near_ref
  4.3 0.6 %shard_map.72 = (f32[12,8,128]{2,1,0:T(8,128)S(1)}, f32[12,8,128]{2,1,0:T(8,128)S(1)}) custom-call(f32[2,4,128,128]{3,2,1,0:T(8,128)S(1)} %get-tuple-element.27.n_ref, f32[2,128,128]{2,1,0:T(8,128)S(1)} %get-tuple-element.28.a_ref, f32[2,128,128]{2,1,0:T(8,128)S(1)} %get-tuple-element.29.b_ref, f32[2,128,128]{2,1,0:T(8,128)S(1)} %get-tuple-element.30.s_ref, ...), custom_call_target="tpu_custom_call" | custom-call | flops 1000000 | bytes 1351680 | tf_op jit(solution)/shard_map/pallas_call | solution.py:405
  4.9 2.7 %collective-permute-start.3 = (f32[12,8,128]{2,1,0:T(8,128)S(1)}, f32[12,8,128]{2,1,0:T(8,128)S(1)}, u32[]{:S(2)}, u32[]{:S(2)}) collective-permute-start(f32[12,8,128]{2,1,0:T(8,128)S(1)} %get-tuple-element.46), channel_id=1, source_target_pairs={{0,1},{1,2},{2,3},{3,0},{4,5},{5,6},{6,7},{7,4},{8,9},{9,10},{10,1... | collective-permute-start | bytes 147464 | tf_op jit(solution)/shard_map/ppermute | solution.py:454
  7.6 2.1 %collective-permute-start.4 = (f32[12,8,128]{2,1,0:T(8,128)S(1)}, f32[12,8,128]{2,1,0:T(8,128)S(1)}, u32[]{:S(2)}, u32[]{:S(2)}) collective-permute-start(f32[12,8,128]{2,1,0:T(8,128)S(1)} %get-tuple-element.47), channel_id=1, source_target_pairs={{1,0},{2,1},{3,2},{0,3},{5,4},{6,5},{7,6},{4,7},{9,8},{10,9},{11,1... | collective-permute-start | bytes 147464 | tf_op jit(solution)/shard_map/ppermute | solution.py:455
  9.7 0.8 %shard_map.69 = (f32[16,4,8,256]{3,2,1,0:T(8,128)S(1)}, f32[16,4,8,256]{3,2,1,0:T(8,128)S(1)}, f32[16,8,128]{2,1,0:T(8,128)S(1)}, f32[16,3,8,128]{3,2,1,0:T(8,128)S(1)}) custom-call(f32[2,4,128,128]{3,2,1,0:T(8,128)S(1)} %get-tuple-element.27.n_ref, f32[2,128,128]{2,1,0:T(8,128)S(1)} %get-tuple-element.28.a_ref, f32[2,128,128]{2,1,0:T(8,128)S(1)} %get-tuple-element.29.b_ref, ...), custom_call_target="tpu_custom_call" | custom-call | flops 1000000 | bytes 1048576 | tf_op jit(solution)/shard_map/pallas_call | solution.py:405
  10.5 1.9 %shard_map.70 = (f32[16,4,8,256]{3,2,1,0:T(8,128)S(1)}, f32[3,2,4,8,256]{4,3,2,1,0:T(8,128)S(1)}, f32[4,8,128]{2,1,0:T(8,128)S(1)}, f32[4,3,8,128]{3,2,1,0:T(8,128)S(1)}) custom-call(f32[16,4,8,256]{3,2,1,0:T(8,128)S(1)} %get-tuple-element.32.y_ref, f32[16,4,8,256]{3,2,1,0:T(8,128)S(1)} %get-tuple-element.33.w_ref, ...), custom_call_target="tpu_custom_call" | custom-call | flops 10000000 | bytes 1277952 | tf_op jit(solution)/shard_map/pallas_call | solution.py:405
  12.4 0.0 collective-permute-done.2.tail_ref
  12.5 0.8 %shard_map.71 = (f32[4,4,8,256]{3,2,1,0:T(8,128)S(1)}, f32[4,8,128]{2,1,0:T(8,128)S(1)}, f32[4,3,8,128]{3,2,1,0:T(8,128)S(1)}) custom-call(f32[16,4,8,256]{3,2,1,0:T(8,128)S(1)} %get-tuple-element.32.y_ref, f32[16,4,8,256]{3,2,1,0:T(8,128)S(1)} %get-tuple-element.33.w_ref, f32[3,2,4,8,256]{4,3,2,1,0:T(8,128)S(1)} %get-tuple-element.36.keep_ref, ...), custom_call_target="tpu_custom_call" | custom-call | flops 1000000 | bytes 1490944 | tf_op jit(solution)/shard_map/pallas_call | solution.py:405
  13.2 0.0 collective-permute-done.3.left_ref
  13.3 0.0 collective-permute-done.4.right_ref
  13.3 0.9 %shard_map.73 = (f32[2,4,128,128]{3,2,1,0:T(8,128)S(1)}, f32[2,128]{1,0:T(2,128)S(1)}) custom-call(f32[16,4,8,256]{3,2,1,0:T(8,128)S(1)} %get-tuple-element.35.x_ref, f32[4,4,8,256]{3,2,1,0:T(8,128)S(1)} %get-tuple-element.39.xf_ref, f32[16,4,8,256]{3,2,1,0:T(8,128)S(1)} %get-tuple-element.33.w_ref, f32[16,8,128]{2,1,0:T(8,128)S(1)} %get-tuple-element.40.sy_ref, ...), custom_call_target="tpu_custom_call" | custom-call | bytes 1671168 | tf_op jit(solution)/shard_map/pallas_call | solution.py:405
  14.2 20.1 %all_to_all.5.all_ref = f32[32,2,128]{2,1,0:T(2,128)S(1)} all-to-all(f32[32,2,128]{2,1,0:T(2,128)S(1)} %broadcast_in_dim.3), channel_id=1, replica_groups=mesh['lat'=8,'lon'=4] {'lat','lon'}, dimensions={0} | all-to-all | bytes 65536 | tf_op jit(solution)/shard_map/all_to_all | solution.py:502
  34.2 1.5 %shard_map.74 = (f32[4,128,256]{2,1,0:T(8,128)}, f32[1,1]{1,0:T(1,128)}) custom-call(f32[2,4,128,128]{3,2,1,0:T(8,128)S(1)} %get-tuple-element.48.x_ref, f32[32,2,128]{2,1,0:T(2,128)S(1)} %all_to_all.5.all_ref), custom_call_target="tpu_custom_call" | custom-call | bytes 557056 | tf_op jit(solution)/shard_map/pallas_call | solution.py:405
  (1 shorter events, 0.0 us)
Async XLA Ops:
  2.4 1.9 %collective-permute-start = (f32[4,7,8,256]{3,2,1,0:T(8,128)S(1)}, f32[4,7,8,256]{3,2,1,0:T(8,128)S(1)}, u32[]{:S(2)}, u32[]{:S(2)}) collective-permute-start(f32[4,7,8,256]{3,2,1,0:T(8,128)S(1)} %get-tuple-element.34), channel_id=1, source_target_pairs={{0,4},{4,0},{8,12},{12,8},{16,20},{20,16},{24,28},{28,24},{1,5},{5... | collective-permute-start | bytes 688136 | tf_op jit(solution)/shard_map/ppermute | solution.py:440
  2.9 9.5 %collective-permute-start.2 = (f32[3,7,8,256]{3,2,1,0:T(8,128)S(1)}, f32[3,7,8,256]{3,2,1,0:T(8,128)S(1)}, u32[]{:S(2)}, u32[]{:S(2)}) collective-permute-start(f32[3,7,8,256]{3,2,1,0:T(8,128)S(1)} %get-tuple-element.38), channel_id=1, source_target_pairs={{4,8},{8,4},{12,16},{16,12},{20,24},{24,20},{5,9},{9,5},{13,17},{1... | collective-permute-start | bytes 516104 | tf_op jit(solution)/shard_map/ppermute | solution.py:442
  3.6 0.7 %collective-permute-start.1 = (f32[18,8,128]{2,1,0:T(8,128)S(1)}, f32[18,8,128]{2,1,0:T(8,128)S(1)}, u32[]{:S(2)}, u32[]{:S(2)}) collective-permute-start(f32[18,8,128]{2,1,0:T(8,128)S(1)} %get-tuple-element.37), channel_id=1, source_target_pairs={{4,8},{8,4},{12,16},{16,12},{20,24},{24,20},{5,9},{9,5},{13,17},{1... | collective-permute-start | bytes 221192 | tf_op jit(solution)/shard_map/ppermute | solution.py:441
  4.9 8.4 %collective-permute-start.3 = (f32[12,8,128]{2,1,0:T(8,128)S(1)}, f32[12,8,128]{2,1,0:T(8,128)S(1)}, u32[]{:S(2)}, u32[]{:S(2)}) collective-permute-start(f32[12,8,128]{2,1,0:T(8,128)S(1)} %get-tuple-element.46), channel_id=1, source_target_pairs={{0,1},{1,2},{2,3},{3,0},{4,5},{5,6},{6,7},{7,4},{8,9},{9,10},{10,1... | collective-permute-start | bytes 147464 | tf_op jit(solution)/shard_map/ppermute | solution.py:454
  7.6 5.6 %collective-permute-start.4 = (f32[12,8,128]{2,1,0:T(8,128)S(1)}, f32[12,8,128]{2,1,0:T(8,128)S(1)}, u32[]{:S(2)}, u32[]{:S(2)}) collective-permute-start(f32[12,8,128]{2,1,0:T(8,128)S(1)} %get-tuple-element.47), channel_id=1, source_target_pairs={{1,0},{2,1},{3,2},{0,3},{5,4},{6,5},{7,6},{4,7},{9,8},{10,9},{11,1... | collective-permute-start | bytes 147464 | tf_op jit(solution)/shard_map/ppermute | solution.py:455

commit v10 on v8

--- a/solution.py
+++ b/solution.py
@@ -66,32 +66,43 @@
         lanes = pl.ds(c * LANES, LANES)
         for k, (ref, to) in enumerate(((a_ref, a_to), (b_ref, b_to), (s_ref, s_to), (m_ref, m_to))):
             copies.append(pltpu.make_async_copy(ref.at[:, lanes], to.at[c], sem.at[c, k]))
+    for c in range(tiles):
+        lanes = pl.ds(c * LANES, LANES)
         copies.append(pltpu.make_async_copy(n_ref.at[:, :, lanes], n_to.at[c], sem.at[c, 4]))
     for copy in copies:
         copy.start()
-    for copy in copies:
-        copy.wait()
     row_at, _ = row_order(rows)
     parts = lane_parts((levels, LANES))
-    edges = []
-    for i in range(ITERS):
-        for far, d in ((False, ITERS - 1 - i), (True, rows - 1 - i)):
-            at = pl.ds(row_at(d), levels, stride=rows)
-            data = [
-                [n_to[c, s, at] for s in range(samples)]
-                + list(cell_weights(a_to[c, at], b_to[c, at], s_to[c, at], m_to[c, at]))
-                for c in range(tiles)
-            ]
-            for c in range(tiles):
-                for g, v in enumerate(data[c]):
-                    if not far:
-                        near_ref[i, g, :, pl.ds(c * LANES, LANES)] = v
-                    elif i == 0:
-                        head_ref[ITERS + g * tiles + c] = v
-                    else:
-                        tail_ref[i - 1, g, :, pl.ds(c * LANES, LANES)] = v
-            if far:
-                edges.append(both_edges(lambda g, side: data[-side][g], samples + 3, parts))
+
+    def put(i, far, g, c, v):
+        if not far:
+            near_ref[i, g, :, pl.ds(c * LANES, LANES)] = v
+        elif i == 0:
+            head_ref[ITERS + g * tiles + c] = v
+        else:
+            tail_ref[i - 1, g, :, pl.ds(c * LANES, LANES)] = v
+
+    blocks = [(i, far, row_at(rows - 1 - i if far else ITERS - 1 - i)) for i in range(ITERS) for far in (False, True)]
+    data = {}
+    for copy in copies[: 4 * tiles]:
+        copy.wait()
+    for i, far, r in blocks:
+        at = pl.ds(r, levels, stride=rows)
+        for c in range(tiles):
+            for k, v in enumerate(cell_weights(a_to[c, at], b_to[c, at], s_to[c, at], m_to[c, at])):
+                put(i, far, samples + k, c, v)
+                data[i, far, samples + k, c] = v
+    for copy in copies[4 * tiles :]:
+        copy.wait()
+    for i, far, r in blocks:
+        for c in range(tiles):
+            for s in range(samples):
+                v = n_to[c, s, pl.ds(r, levels, stride=rows)]
+                put(i, far, s, c, v)
+                data[i, far, s, c] = v
+    edges = [
+        both_edges(lambda g, side: data[i, True, g, side * (tiles - 1)], samples + 3, parts) for i in range(ITERS)
+    ]
     sent = messages(edges, parts)
     for d in range(2):
         for i in range(ITERS // 2):
@@ -364,13 +375,14 @@
     sum_ref[1:2] = jnp.sum(count, axis=0, keepdims=True)
 
 
-def scale_kernel(x_ref, w_ref, var_ref, all_ref, out_ref, mean_ref, stage, sem):
+def scale_kernel(x_ref, w_ref, var_ref, all_ref, out_ref, mean_ref, stage, mean_to, sem, mean_sem):
     rows, samples, levels, cols = x_ref.shape
     sums = jnp.sum(jnp.sum(all_ref[...], axis=0), axis=1, keepdims=True)
     mean = sums[0:1] / sums[1:2]
-    mean_ref[...] = mean
+    mean_to[...] = mean
+    copies = [pltpu.make_async_copy(mean_to, mean_ref, mean_sem)]
+    copies[0].start()
     row_at, _ = row_order(rows)
-    copies = []
     for c in range(cols // LANES):
         lanes = pl.ds(c * LANES, LANES)
         factors = []
@@ -493,8 +505,13 @@
         w,
         var,
         every,
-        scratch=[(tiles, samples, levels * rows, LANES), pltpu.SemaphoreType.DMA((tiles, samples))],
-        out_space=[pl.ANY, pltpu.VMEM],
+        scratch=[
+            (tiles, samples, levels * rows, LANES),
+            (1, 1),
+            pltpu.SemaphoreType.DMA((tiles, samples)),
+            pltpu.SemaphoreType.DMA,
+        ],
+        out_space=[pl.ANY, pl.ANY],
     )
     return out.reshape(noise.shape), mean.reshape(())
 

time: 35.5 us -> 34.9 us (0.983)
  Pallas kernels: 8.38 us -> 7.77 us
    pallas_call x8, Pallas kernels: 8.38 us -> 7.77 us  [call(): pl.pallas_call(kernel, out_shape=out, in_specs=[pl.BlockSpec(memory_space...]
where the time goes in v10:
time: 34.9 us; the launch traced here: 34.7 us
  blocking collectives  19.6 us (56%)
  Pallas kernels  7.77 us (22%)
  starting transfers between devices  6.55 us (19%)
  between operations  0.73 us (2%)
    all_to_all x1, blocking collectives, shards(): every = lax.all_to_all(spread, ('lat', 'lon'), 0, 0, tiled=True)  19.6 us
    pallas_call x8, Pallas kernels, call(): pl.pallas_call(kernel, out_shape=out, in_specs=[pl.BlockSpec(memory_space...  7.77 us
    ppermute x1, starting transfers between devices, shards(): left = lax.ppermute(to_east, 'lon', east)  2.6 us
    ppermute x1, starting transfers between devices, shards(): right = lax.ppermute(to_west, 'lon', west)  2.07 us
  transfers between devices with their start and end apart: 5, of which 0 were waited for; matrix products, arithmetic and copies ran while one was open for 0% of the time, Pallas kernels for 12%

profile of v10, /device:TPU:0, one launch (start us, length us, event | category | flops | bytes accessed | tf_op | source)
XLA Modules:
  0.0 34.7 jit_solution(15319076555755578926)
XLA Ops:
  0.6 1.7 %shard_map.68 = (f32[4,7,8,256]{3,2,1,0:T(8,128)S(1)}, f32[18,8,128]{2,1,0:T(8,128)S(1)}, f32[3,7,8,256]{3,2,1,0:T(8,128)S(1)}, f32[2,4,128,128]{3,2,1,0:T(8,128...) custom-call(f32[4,128,256]{2,1,0:T(8,128)} %bitcast.7, ...), custom_call_target="tpu_custom_call" | custom-call | bytes 1048576 | tf_op jit(solution)/shard_map/pallas_call | solution.py:405
  2.4 0.6 %collective-permute-start = (f32[4,7,8,256]{3,2,1,0:T(8,128)S(1)}, f32[4,7,8,256]{3,2,1,0:T(8,128)S(1)}, u32[]{:S(2)}, u32[]{:S(2)}) collective-permute-start(f32[4,7,8,256]{3,2,1,0:T(8,128)S(1)} %get-tuple-element.35), channel_id=1, source_target_pairs={{0,4},{4,0},{8,12},{12,8},{16,20},{20,16},{24,28},{28,24},{1,5},{5... | collective-permute-start | bytes 688136 | tf_op jit(solution)/shard_map/ppermute | solution.py:440
  2.9 0.7 %collective-permute-start.2 = (f32[3,7,8,256]{3,2,1,0:T(8,128)S(1)}, f32[3,7,8,256]{3,2,1,0:T(8,128)S(1)}, u32[]{:S(2)}, u32[]{:S(2)}) collective-permute-start(f32[3,7,8,256]{3,2,1,0:T(8,128)S(1)} %get-tuple-element.39), channel_id=1, source_target_pairs={{4,8},{8,4},{12,16},{16,12},{20,24},{24,20},{5,9},{9,5},{13,17},{1... | collective-permute-start | bytes 516104 | tf_op jit(solution)/shard_map/ppermute | solution.py:442
  3.6 0.7 %collective-permute-start.1 = (f32[18,8,128]{2,1,0:T(8,128)S(1)}, f32[18,8,128]{2,1,0:T(8,128)S(1)}, u32[]{:S(2)}, u32[]{:S(2)}) collective-permute-start(f32[18,8,128]{2,1,0:T(8,128)S(1)} %get-tuple-element.38), channel_id=1, source_target_pairs={{4,8},{8,4},{12,16},{16,12},{20,24},{24,20},{5,9},{9,5},{13,17},{1... | collective-permute-start | bytes 221192 | tf_op jit(solution)/shard_map/ppermute | solution.py:441
  4.3 0.5 %shard_map.72.own_ref = f32[2,8,8,128]{3,2,1,0:T(8,128)S(1)} custom-call(f32[2,4,128,128]{3,2,1,0:T(8,128)S(1)} %get-tuple-element.28.n_ref, f32[2,128,128]{2,1,0:T(8,128)S(1)} %get-tuple-element.29.a_ref, f32[2,128,128]{2,1,0:T(8,128)S(1)} %get-tuple-element.30.b_ref, f32[2,128,128]{2,1,0:T(8,128)S(1)} %get-tuple-element.31.s_ref, ...), custom_call_target="tpu_custom_call" | custom-call | flops 1000000 | bytes 1048576 | tf_op jit(solution)/shard_map/pallas_call | solution.py:405
  4.8 0.0 collective-permute-done.1.head_ref
  4.8 0.0 collective-permute-done.near_ref
  4.8 0.3 shard_map.73
  5.1 2.6 %collective-permute-start.3 = (f32[12,8,128]{2,1,0:T(8,128)S(1)}, f32[12,8,128]{2,1,0:T(8,128)S(1)}, u32[]{:S(2)}, u32[]{:S(2)}) collective-permute-start(f32[12,8,128]{2,1,0:T(8,128)S(1)} %get-tuple-element.47), channel_id=1, source_target_pairs={{0,1},{1,2},{2,3},{3,0},{4,5},{5,6},{6,7},{7,4},{8,9},{9,10},{10,1... | collective-permute-start | bytes 147464 | tf_op jit(solution)/shard_map/ppermute | solution.py:453
  7.7 2.1 %collective-permute-start.4 = (f32[12,8,128]{2,1,0:T(8,128)S(1)}, f32[12,8,128]{2,1,0:T(8,128)S(1)}, u32[]{:S(2)}, u32[]{:S(2)}) collective-permute-start(f32[12,8,128]{2,1,0:T(8,128)S(1)} %get-tuple-element.48), channel_id=1, source_target_pairs={{1,0},{2,1},{3,2},{0,3},{5,4},{6,5},{7,6},{4,7},{9,8},{10,9},{11,1... | collective-permute-start | bytes 147464 | tf_op jit(solution)/shard_map/ppermute | solution.py:454
  9.8 0.8 %shard_map.69 = (f32[16,4,8,256]{3,2,1,0:T(8,128)S(1)}, f32[16,4,8,256]{3,2,1,0:T(8,128)S(1)}, f32[16,8,128]{2,1,0:T(8,128)S(1)}, f32[16,3,8,128]{3,2,1,0:T(8,128)S(1)}) custom-call(f32[2,4,128,128]{3,2,1,0:T(8,128)S(1)} %get-tuple-element.28.n_ref, f32[2,128,128]{2,1,0:T(8,128)S(1)} %get-tuple-element.29.a_ref, f32[2,128,128]{2,1,0:T(8,128)S(1)} %get-tuple-element.30.b_ref, ...), custom_call_target="tpu_custom_call" | custom-call | flops 1000000 | bytes 1048576 | tf_op jit(solution)/shard_map/pallas_call | solution.py:405
  10.6 1.9 %shard_map.70 = (f32[16,4,8,256]{3,2,1,0:T(8,128)S(1)}, f32[3,2,4,8,256]{4,3,2,1,0:T(8,128)S(1)}, f32[4,8,128]{2,1,0:T(8,128)S(1)}, f32[4,3,8,128]{3,2,1,0:T(8,128)S(1)}) custom-call(f32[16,4,8,256]{3,2,1,0:T(8,128)S(1)} %get-tuple-element.33.y_ref, f32[16,4,8,256]{3,2,1,0:T(8,128)S(1)} %get-tuple-element.34.w_ref, ...), custom_call_target="tpu_custom_call" | custom-call | flops 10000000 | bytes 1277952 | tf_op jit(solution)/shard_map/pallas_call | solution.py:405
  12.5 0.0 collective-permute-done.2.tail_ref
  12.5 0.8 %shard_map.71 = (f32[4,4,8,256]{3,2,1,0:T(8,128)S(1)}, f32[4,8,128]{2,1,0:T(8,128)S(1)}, f32[4,3,8,128]{3,2,1,0:T(8,128)S(1)}) custom-call(f32[16,4,8,256]{3,2,1,0:T(8,128)S(1)} %get-tuple-element.33.y_ref, f32[16,4,8,256]{3,2,1,0:T(8,128)S(1)} %get-tuple-element.34.w_ref, f32[3,2,4,8,256]{4,3,2,1,0:T(8,128)S(1)} %get-tuple-element.37.keep_ref, ...), custom_call_target="tpu_custom_call" | custom-call | flops 1000000 | bytes 1490944 | tf_op jit(solution)/shard_map/pallas_call | solution.py:405
  13.3 0.0 collective-permute-done.3.left_ref
  13.3 0.0 collective-permute-done.4.right_ref
  13.3 0.7 %shard_map.74 = (f32[16,4,8,256]{3,2,1,0:T(8,128)S(1)}, f32[16,8,256]{2,1,0:T(8,128)S(1)}, f32[2,128]{1,0:T(2,128)S(1)}) custom-call(f32[16,4,8,256]{3,2,1,0:T(8,128)S(1)} %get-tuple-element.36.x_ref, f32[4,4,8,256]{3,2,1,0:T(8,128)S(1)} %get-tuple-element.40.xf_ref, f32[16,4,8,256]{3,2,1,0:T(8,128)S(1)} %get-tuple-element.34.w_ref, ...), custom_call_target="tpu_custom_call" | custom-call | bytes 1671168 | tf_op jit(solution)/shard_map/pallas_call | solution.py:405
  14.0 19.6 %all_to_all.5.all_ref = f32[32,2,128]{2,1,0:T(2,128)S(1)} all-to-all(f32[32,2,128]{2,1,0:T(2,128)S(1)} %broadcast_in_dim.3), channel_id=1, replica_groups=mesh['lat'=8,'lon'=4] {'lat','lon'}, dimensions={0} | all-to-all | bytes 65536 | tf_op jit(solution)/shard_map/all_to_all | solution.py:500
  33.6 1.0 %shard_map.75 = (f32[4,128,256]{2,1,0:T(8,128)}, f32[1,1]{1,0:T(1,128)}) custom-call(f32[16,4,8,256]{3,2,1,0:T(8,128)S(1)} %get-tuple-element.49.x_ref, f32[16,4,8,256]{3,2,1,0:T(8,128)S(1)} %get-tuple-element.34.w_ref, f32[16,8,256]{2,1,0:T(8,128)S(1)} %get-tuple-element.50.var_ref, f32[32,2,128]{2,1,0:T(2,128)S(1)} %all_to_all.5.all_ref), custom_call_target="tpu_custom_call" | custom-call | bytes 1212416 | tf_op jit(solution)/shard_map/pallas_call | solution.py:405
  (1 shorter events, 0.0 us)
Async XLA Ops:
  2.4 2.5 %collective-permute-start = (f32[4,7,8,256]{3,2,1,0:T(8,128)S(1)}, f32[4,7,8,256]{3,2,1,0:T(8,128)S(1)}, u32[]{:S(2)}, u32[]{:S(2)}) collective-permute-start(f32[4,7,8,256]{3,2,1,0:T(8,128)S(1)} %get-tuple-element.35), channel_id=1, source_target_pairs={{0,4},{4,0},{8,12},{12,8},{16,20},{20,16},{24,28},{28,24},{1,5},{5... | collective-permute-start | bytes 688136 | tf_op jit(solution)/shard_map/ppermute | solution.py:440
  2.9 9.6 %collective-permute-start.2 = (f32[3,7,8,256]{3,2,1,0:T(8,128)S(1)}, f32[3,7,8,256]{3,2,1,0:T(8,128)S(1)}, u32[]{:S(2)}, u32[]{:S(2)}) collective-permute-start(f32[3,7,8,256]{3,2,1,0:T(8,128)S(1)} %get-tuple-element.39), channel_id=1, source_target_pairs={{4,8},{8,4},{12,16},{16,12},{20,24},{24,20},{5,9},{9,5},{13,17},{1... | collective-permute-start | bytes 516104 | tf_op jit(solution)/shard_map/ppermute | solution.py:442
  3.6 1.2 %collective-permute-start.1 = (f32[18,8,128]{2,1,0:T(8,128)S(1)}, f32[18,8,128]{2,1,0:T(8,128)S(1)}, u32[]{:S(2)}, u32[]{:S(2)}) collective-permute-start(f32[18,8,128]{2,1,0:T(8,128)S(1)} %get-tuple-element.38), channel_id=1, source_target_pairs={{4,8},{8,4},{12,16},{16,12},{20,24},{24,20},{5,9},{9,5},{13,17},{1... | collective-permute-start | bytes 221192 | tf_op jit(solution)/shard_map/ppermute | solution.py:441
  5.1 8.2 %collective-permute-start.3 = (f32[12,8,128]{2,1,0:T(8,128)S(1)}, f32[12,8,128]{2,1,0:T(8,128)S(1)}, u32[]{:S(2)}, u32[]{:S(2)}) collective-permute-start(f32[12,8,128]{2,1,0:T(8,128)S(1)} %get-tuple-element.47), channel_id=1, source_target_pairs={{0,1},{1,2},{2,3},{3,0},{4,5},{5,6},{6,7},{7,4},{8,9},{9,10},{10,1... | collective-permute-start | bytes 147464 | tf_op jit(solution)/shard_map/ppermute | solution.py:453
  7.7 5.6 %collective-permute-start.4 = (f32[12,8,128]{2,1,0:T(8,128)S(1)}, f32[12,8,128]{2,1,0:T(8,128)S(1)}, u32[]{:S(2)}, u32[]{:S(2)}) collective-permute-start(f32[12,8,128]{2,1,0:T(8,128)S(1)} %get-tuple-element.48), channel_id=1, source_target_pairs={{1,0},{2,1},{3,2},{0,3},{5,4},{6,5},{7,6},{4,7},{9,8},{10,9},{11,1... | collective-permute-start | bytes 147464 | tf_op jit(solution)/shard_map/ppermute | solution.py:454

commit v11 on v10

--- a/solution.py
+++ b/solution.py
@@ -371,14 +371,17 @@
             m = jnp.where(w_ref[r, 1, :, lanes] > 0, 1.0, 0.0)
             total = m * var if total is None else total + m * var
             count = m if count is None else count + m
-    sum_ref[0:1] = jnp.sum(total, axis=0, keepdims=True)
-    sum_ref[1:2] = jnp.sum(count, axis=0, keepdims=True)
+    total, count = [jnp.sum(v, axis=0, keepdims=True) for v in (total, count)]
+    low = lax.broadcasted_iota(jnp.int32, total.shape, 1) < LANES // 2
+    sum_ref[...] = jnp.where(low, total + roll(total, LANES // 2), count + roll(count, LANES // 2))
 
 
 def scale_kernel(x_ref, w_ref, var_ref, all_ref, out_ref, mean_ref, stage, mean_to, sem, mean_sem):
     rows, samples, levels, cols = x_ref.shape
-    sums = jnp.sum(jnp.sum(all_ref[...], axis=0), axis=1, keepdims=True)
-    mean = sums[0:1] / sums[1:2]
+    sums = jnp.sum(all_ref[...], axis=0)
+    low = lax.broadcasted_iota(jnp.int32, sums.shape, 1) < LANES // 2
+    total, count = [jnp.sum(jnp.where(m, sums, 0.0), axis=1, keepdims=True) for m in (low, ~low)]
+    mean = total / count
     mean_to[...] = mean
     copies = [pltpu.make_async_copy(mean_to, mean_ref, mean_sem)]
     copies[0].start()
@@ -483,7 +486,7 @@
     )
     x, var, part = call(
         finish_kernel,
-        [y.shape, (rows, levels, cols), (2, LANES)],
+        [y.shape, (rows, levels, cols), (1, LANES)],
         x,
         x_far,
         w,
@@ -496,7 +499,7 @@
         left,
         right,
     )
-    spread = jnp.broadcast_to(part, (n_lat * n_lon, 2, LANES))
+    spread = jnp.broadcast_to(part, (n_lat * n_lon, 1, LANES))
     every = lax.all_to_all(spread, ("lat", "lon"), 0, 0, tiled=True)
     out, mean = call(
         scale_kernel,

time: 34.9 us -> 34.8 us (level)
  no operation moved by 1% of the time
where the time goes in v11:
time: 34.8 us; the launch traced here: 34.6 us
  blocking collectives  19.5 us (56%)
  Pallas kernels  7.81 us (22%)
  starting transfers between devices  6.55 us (19%)
  between operations  0.73 us (2%)
    all_to_all x1, blocking collectives, shards(): every = lax.all_to_all(spread, ('lat', 'lon'), 0, 0, tiled=True)  19.5 us
    pallas_call x8, Pallas kernels, call(): pl.pallas_call(kernel, out_shape=out, in_specs=[pl.BlockSpec(memory_space...  7.81 us
    ppermute x1, starting transfers between devices, shards(): left = lax.ppermute(to_east, 'lon', east)  2.6 us
    ppermute x1, starting transfers between devices, shards(): right = lax.ppermute(to_west, 'lon', west)  2.07 us
  transfers between devices with their start and end apart: 5, of which 0 were waited for; matrix products, arithmetic and copies ran while one was open for 0% of the time, Pallas kernels for 12%

profile of v11, /device:TPU:0, one launch (start us, length us, event | category | flops | bytes accessed | tf_op | source)
XLA Modules:
  0.0 34.6 jit_solution(1494261556522642441)
XLA Ops:
  0.6 1.7 %shard_map.68 = (f32[4,7,8,256]{3,2,1,0:T(8,128)S(1)}, f32[18,8,128]{2,1,0:T(8,128)S(1)}, f32[3,7,8,256]{3,2,1,0:T(8,128)S(1)}, f32[2,4,128,128]{3,2,1,0:T(8,128...) custom-call(f32[4,128,256]{2,1,0:T(8,128)} %bitcast.9, ...), custom_call_target="tpu_custom_call" | custom-call | bytes 1048576 | tf_op jit(solution)/shard_map/pallas_call | solution.py:408
  2.4 0.6 %collective-permute-start = (f32[4,7,8,256]{3,2,1,0:T(8,128)S(1)}, f32[4,7,8,256]{3,2,1,0:T(8,128)S(1)}, u32[]{:S(2)}, u32[]{:S(2)}) collective-permute-start(f32[4,7,8,256]{3,2,1,0:T(8,128)S(1)} %get-tuple-element.35), channel_id=1, source_target_pairs={{0,4},{4,0},{8,12},{12,8},{16,20},{20,16},{24,28},{28,24},{1,5},{5... | collective-permute-start | bytes 688136 | tf_op jit(solution)/shard_map/ppermute | solution.py:443
  2.9 0.7 %collective-permute-start.2 = (f32[3,7,8,256]{3,2,1,0:T(8,128)S(1)}, f32[3,7,8,256]{3,2,1,0:T(8,128)S(1)}, u32[]{:S(2)}, u32[]{:S(2)}) collective-permute-start(f32[3,7,8,256]{3,2,1,0:T(8,128)S(1)} %get-tuple-element.39), channel_id=1, source_target_pairs={{4,8},{8,4},{12,16},{16,12},{20,24},{24,20},{5,9},{9,5},{13,17},{1... | collective-permute-start | bytes 516104 | tf_op jit(solution)/shard_map/ppermute | solution.py:445
  3.6 0.7 %collective-permute-start.1 = (f32[18,8,128]{2,1,0:T(8,128)S(1)}, f32[18,8,128]{2,1,0:T(8,128)S(1)}, u32[]{:S(2)}, u32[]{:S(2)}) collective-permute-start(f32[18,8,128]{2,1,0:T(8,128)S(1)} %get-tuple-element.38), channel_id=1, source_target_pairs={{4,8},{8,4},{12,16},{16,12},{20,24},{24,20},{5,9},{9,5},{13,17},{1... | collective-permute-start | bytes 221192 | tf_op jit(solution)/shard_map/ppermute | solution.py:444
  4.3 0.5 %shard_map.72.own_ref = f32[2,8,8,128]{3,2,1,0:T(8,128)S(1)} custom-call(f32[2,4,128,128]{3,2,1,0:T(8,128)S(1)} %get-tuple-element.28.n_ref, f32[2,128,128]{2,1,0:T(8,128)S(1)} %get-tuple-element.29.a_ref, f32[2,128,128]{2,1,0:T(8,128)S(1)} %get-tuple-element.30.b_ref, f32[2,128,128]{2,1,0:T(8,128)S(1)} %get-tuple-element.31.s_ref, ...), custom_call_target="tpu_custom_call" | custom-call | flops 1000000 | bytes 1048576 | tf_op jit(solution)/shard_map/pallas_call | solution.py:408
  4.8 0.0 collective-permute-done.1.head_ref
  4.8 0.0 collective-permute-done.near_ref
  4.8 0.3 shard_map.73
  5.1 2.6 %collective-permute-start.3 = (f32[12,8,128]{2,1,0:T(8,128)S(1)}, f32[12,8,128]{2,1,0:T(8,128)S(1)}, u32[]{:S(2)}, u32[]{:S(2)}) collective-permute-start(f32[12,8,128]{2,1,0:T(8,128)S(1)} %get-tuple-element.47), channel_id=1, source_target_pairs={{0,1},{1,2},{2,3},{3,0},{4,5},{5,6},{6,7},{7,4},{8,9},{9,10},{10,1... | collective-permute-start | bytes 147464 | tf_op jit(solution)/shard_map/ppermute | solution.py:456
  7.7 2.1 %collective-permute-start.4 = (f32[12,8,128]{2,1,0:T(8,128)S(1)}, f32[12,8,128]{2,1,0:T(8,128)S(1)}, u32[]{:S(2)}, u32[]{:S(2)}) collective-permute-start(f32[12,8,128]{2,1,0:T(8,128)S(1)} %get-tuple-element.48), channel_id=1, source_target_pairs={{1,0},{2,1},{3,2},{0,3},{5,4},{6,5},{7,6},{4,7},{9,8},{10,9},{11,1... | collective-permute-start | bytes 147464 | tf_op jit(solution)/shard_map/ppermute | solution.py:457
  9.8 0.8 %shard_map.69 = (f32[16,4,8,256]{3,2,1,0:T(8,128)S(1)}, f32[16,4,8,256]{3,2,1,0:T(8,128)S(1)}, f32[16,8,128]{2,1,0:T(8,128)S(1)}, f32[16,3,8,128]{3,2,1,0:T(8,128)S(1)}) custom-call(f32[2,4,128,128]{3,2,1,0:T(8,128)S(1)} %get-tuple-element.28.n_ref, f32[2,128,128]{2,1,0:T(8,128)S(1)} %get-tuple-element.29.a_ref, f32[2,128,128]{2,1,0:T(8,128)S(1)} %get-tuple-element.30.b_ref, ...), custom_call_target="tpu_custom_call" | custom-call | flops 1000000 | bytes 1048576 | tf_op jit(solution)/shard_map/pallas_call | solution.py:408
  10.6 1.9 %shard_map.70 = (f32[16,4,8,256]{3,2,1,0:T(8,128)S(1)}, f32[3,2,4,8,256]{4,3,2,1,0:T(8,128)S(1)}, f32[4,8,128]{2,1,0:T(8,128)S(1)}, f32[4,3,8,128]{3,2,1,0:T(8,128)S(1)}) custom-call(f32[16,4,8,256]{3,2,1,0:T(8,128)S(1)} %get-tuple-element.33.y_ref, f32[16,4,8,256]{3,2,1,0:T(8,128)S(1)} %get-tuple-element.34.w_ref, ...), custom_call_target="tpu_custom_call" | custom-call | flops 10000000 | bytes 1277952 | tf_op jit(solution)/shard_map/pallas_call | solution.py:408
  12.5 0.0 collective-permute-done.2.tail_ref
  12.5 0.8 %shard_map.71 = (f32[4,4,8,256]{3,2,1,0:T(8,128)S(1)}, f32[4,8,128]{2,1,0:T(8,128)S(1)}, f32[4,3,8,128]{3,2,1,0:T(8,128)S(1)}) custom-call(f32[16,4,8,256]{3,2,1,0:T(8,128)S(1)} %get-tuple-element.33.y_ref, f32[16,4,8,256]{3,2,1,0:T(8,128)S(1)} %get-tuple-element.34.w_ref, f32[3,2,4,8,256]{4,3,2,1,0:T(8,128)S(1)} %get-tuple-element.37.keep_ref, ...), custom_call_target="tpu_custom_call" | custom-call | flops 1000000 | bytes 1490944 | tf_op jit(solution)/shard_map/pallas_call | solution.py:408
  13.3 0.0 collective-permute-done.3.left_ref
  13.3 0.0 collective-permute-done.4.right_ref
  13.3 0.8 %shard_map.74 = (f32[16,4,8,256]{3,2,1,0:T(8,128)S(1)}, f32[16,8,256]{2,1,0:T(8,128)S(1)}, f32[1,128]{1,0:T(1,128)S(1)}) custom-call(f32[16,4,8,256]{3,2,1,0:T(8,128)S(1)} %get-tuple-element.36.x_ref, f32[4,4,8,256]{3,2,1,0:T(8,128)S(1)} %get-tuple-element.40.xf_ref, f32[16,4,8,256]{3,2,1,0:T(8,128)S(1)} %get-tuple-element.34.w_ref, ...), custom_call_target="tpu_custom_call" | custom-call | bytes 1671168 | tf_op jit(solution)/shard_map/pallas_call | solution.py:408
  14.1 19.5 %all_to_all.5.all_ref = f32[32,1,128]{2,1,0:T(1,128)S(1)} all-to-all(f32[32,1,128]{2,1,0:T(1,128)S(1)} %broadcast_in_dim.3), channel_id=1, replica_groups=mesh['lat'=8,'lon'=4] {'lat','lon'}, dimensions={0} | all-to-all | bytes 32768 | tf_op jit(solution)/shard_map/all_to_all | solution.py:503
  33.6 1.0 %shard_map.75 = (f32[4,128,256]{2,1,0:T(8,128)}, f32[1,1]{1,0:T(1,128)}) custom-call(f32[16,4,8,256]{3,2,1,0:T(8,128)S(1)} %get-tuple-element.49.x_ref, f32[16,4,8,256]{3,2,1,0:T(8,128)S(1)} %get-tuple-element.34.w_ref, f32[16,8,256]{2,1,0:T(8,128)S(1)} %get-tuple-element.50.var_ref, f32[32,1,128]{2,1,0:T(1,128)S(1)} %all_to_all.5.all_ref), custom_call_target="tpu_custom_call" | custom-call | bytes 1196032 | tf_op jit(solution)/shard_map/pallas_call | solution.py:408
  (1 shorter events, 0.0 us)
Async XLA Ops:
  2.4 2.5 %collective-permute-start = (f32[4,7,8,256]{3,2,1,0:T(8,128)S(1)}, f32[4,7,8,256]{3,2,1,0:T(8,128)S(1)}, u32[]{:S(2)}, u32[]{:S(2)}) collective-permute-start(f32[4,7,8,256]{3,2,1,0:T(8,128)S(1)} %get-tuple-element.35), channel_id=1, source_target_pairs={{0,4},{4,0},{8,12},{12,8},{16,20},{20,16},{24,28},{28,24},{1,5},{5... | collective-permute-start | bytes 688136 | tf_op jit(solution)/shard_map/ppermute | solution.py:443
  2.9 9.6 %collective-permute-start.2 = (f32[3,7,8,256]{3,2,1,0:T(8,128)S(1)}, f32[3,7,8,256]{3,2,1,0:T(8,128)S(1)}, u32[]{:S(2)}, u32[]{:S(2)}) collective-permute-start(f32[3,7,8,256]{3,2,1,0:T(8,128)S(1)} %get-tuple-element.39), channel_id=1, source_target_pairs={{4,8},{8,4},{12,16},{16,12},{20,24},{24,20},{5,9},{9,5},{13,17},{1... | collective-permute-start | bytes 516104 | tf_op jit(solution)/shard_map/ppermute | solution.py:445
  3.6 1.2 %collective-permute-start.1 = (f32[18,8,128]{2,1,0:T(8,128)S(1)}, f32[18,8,128]{2,1,0:T(8,128)S(1)}, u32[]{:S(2)}, u32[]{:S(2)}) collective-permute-start(f32[18,8,128]{2,1,0:T(8,128)S(1)} %get-tuple-element.38), channel_id=1, source_target_pairs={{4,8},{8,4},{12,16},{16,12},{20,24},{24,20},{5,9},{9,5},{13,17},{1... | collective-permute-start | bytes 221192 | tf_op jit(solution)/shard_map/ppermute | solution.py:444
  5.1 8.2 %collective-permute-start.3 = (f32[12,8,128]{2,1,0:T(8,128)S(1)}, f32[12,8,128]{2,1,0:T(8,128)S(1)}, u32[]{:S(2)}, u32[]{:S(2)}) collective-permute-start(f32[12,8,128]{2,1,0:T(8,128)S(1)} %get-tuple-element.47), channel_id=1, source_target_pairs={{0,1},{1,2},{2,3},{3,0},{4,5},{5,6},{6,7},{7,4},{8,9},{9,10},{10,1... | collective-permute-start | bytes 147464 | tf_op jit(solution)/shard_map/ppermute | solution.py:456
  7.7 5.6 %collective-permute-start.4 = (f32[12,8,128]{2,1,0:T(8,128)S(1)}, f32[12,8,128]{2,1,0:T(8,128)S(1)}, u32[]{:S(2)}, u32[]{:S(2)}) collective-permute-start(f32[12,8,128]{2,1,0:T(8,128)S(1)} %get-tuple-element.48), channel_id=1, source_target_pairs={{1,0},{2,1},{3,2},{0,3},{5,4},{6,5},{7,6},{4,7},{9,8},{10,9},{11,1... | collective-permute-start | bytes 147464 | tf_op jit(solution)/shard_map/ppermute | solution.py:457

commit v12 on v11

--- a/solution.py
+++ b/solution.py
@@ -78,7 +78,7 @@
         if not far:
             near_ref[i, g, :, pl.ds(c * LANES, LANES)] = v
         elif i == 0:
-            head_ref[ITERS + g * tiles + c] = v
+            head_ref[2 + g * tiles + c] = v
         else:
             tail_ref[i - 1, g, :, pl.ds(c * LANES, LANES)] = v
 
@@ -103,10 +103,7 @@
     edges = [
         both_edges(lambda g, side: data[i, True, g, side * (tiles - 1)], samples + 3, parts) for i in range(ITERS)
     ]
-    sent = messages(edges, parts)
-    for d in range(2):
-        for i in range(ITERS // 2):
-            head_ref[d * (ITERS // 2) + i] = sent[d][i]
+    head_ref[0], head_ref[1] = messages(edges, parts)
 
 
 BATCH = 4
@@ -138,23 +135,45 @@
     return [jnp.where(parts[0] < LANES // 2, get(g, 0), get(g, 1)) for g in range(groups)]
 
 
+def by_segment(values, seg, first):
+    line = values[0]
+    for i, v in enumerate(values[1:]):
+        line = jnp.where(seg == first + 1 + i, v, line)
+    return line
+
+
 def messages(both, parts):
-    lane, seg, l32 = parts
+    _, seg, l32 = parts
     samples = len(both[0]) - 3
-    lines = [[roll(row[s], SEG * s + 4) for s in range(samples)] for row in both]
-    packed = [[roll(row[samples + k], 8 * k + 12) for k in range(3)] for row in both]
-    packed = replicate([jnp.where(l32 < 16, a, jnp.where(l32 < 24, b, c)) for a, b, c in packed], seg)
-    full = []
-    for line, weights in zip(lines, packed):
-        v = line[0]
-        for s in range(1, samples):
-            v = jnp.where(seg == s, line[s], v)
-        full.append(jnp.where(l32 < 8, v, weights))
-    low = lane % 8 < 4
-    pairs = list(zip(full[0::2], full[1::2]))
-    east = [jnp.where(low, a, roll(b, 4)) for a, b in pairs]
-    west = [jnp.where(low, roll(a, -4), b) for a, b in pairs]
+    slot = l32 // 4
+    east = west = None
+    for j, row in enumerate(both):
+        line = by_segment([roll(row[s], SEG * s + 4 * j + 4) for s in range(samples)], seg, 0)
+        turned = [roll(row[samples + k], SEG * k + 4 * j + 20) for k in range(3)]
+        weights = by_segment(turned, seg, 0)
+        east = line if east is None else jnp.where(slot == j, line, east)
+        west = line if west is None else jnp.where(slot == j + 1, line, west)
+        east = jnp.where(slot == 4 + j, weights, east)
+        if j < BATCH - 1:
+            west = jnp.where(slot == 5 + j, weights, west)
+        else:
+            west = jnp.where(slot == 0, by_segment(turned, seg, 1), west)
     return east, west
+
+
+def unpack(tile, parts, from_east):
+    _, seg, _ = parts
+    turned = [roll(tile, SEG * q) for q in range(4)]
+    every = [by_segment([turned[(q - k) % 4] for q in range(4)], seg, 0) for k in range(4 if from_east else 3)]
+    rows = []
+    for j in range(BATCH):
+        if not from_east:
+            rows.append([roll(tile, -4 * j)] + [roll(every[k], -16 - 4 * j) for k in range(3)])
+        elif j < BATCH - 1:
+            rows.append([roll(tile, 24 - 4 * j)] + [roll(every[k], 8 - 4 * j) for k in range(3)])
+        else:
+            rows.append([roll(tile, 24 - 4 * j)] + [roll(every[k + 1], 28) for k in range(3)])
+    return rows
 
 
 def strips(gets, samples, parts):
@@ -194,10 +213,7 @@
         for d in range(first, first + BATCH):
             at = pl.ds(row_at(d), levels, stride=rows)
             both.append([n_to[s, at] for s in range(samples)] + list(cell_weights(a_to[at], b_to[at], s_to[at], m_to[at])))
-        sent = messages(both, parts)
-        for d in range(2):
-            for i in range(BATCH // 2):
-                msg_ref[d, first // 2 + i] = sent[d][i]
+        msg_ref[0, first // BATCH], msg_ref[1, first // BATCH] = messages(both, parts)
 
 
 def own_kernel(n_ref, a_ref, b_ref, s_ref, m_ref, y_ref, w_ref, sy_ref, sw_ref):
@@ -226,14 +242,13 @@
 
 
 def join_kernel(own_ref, near_ref, head_ref, east_ref, west_ref):
-    pairs, half = own_ref.shape[1], ITERS // 2
+    tiles = own_ref.shape[1]
     parts = lane_parts(own_ref.shape[2:])
     sent = messages([both_edges(get, near_ref.shape[1], parts) for get in halo_gets(near_ref)], parts)
     for d, ref in enumerate((east_ref, west_ref)):
-        for i in range(half):
-            ref[i] = sent[d][i]
-            ref[half + pairs + i] = head_ref[d * half + i]
-        ref[half : half + pairs] = own_ref[d]
+        ref[0] = sent[d]
+        ref[1 : 1 + tiles] = own_ref[d]
+        ref[1 + tiles] = head_ref[d]
 
 
 def near_kernel(y_ref, w_ref, near_ref, x_ref, keep_ref, hy_ref, hw_ref, wh_ref, p_ref, q_ref):
@@ -280,7 +295,7 @@
     _, sign = row_order(rows)
 
     def tile(i, g, c):
-        return head_ref[ITERS + g * tiles + c] if i == 0 else tail_ref[i - 1, g, :, pl.ds(c * LANES, LANES)]
+        return head_ref[2 + g * tiles + c] if i == 0 else tail_ref[i - 1, g, :, pl.ds(c * LANES, LANES)]
 
     for i in range(ITERS):
         for c in range(tiles):
@@ -335,16 +350,13 @@
             return sy_ref[r - ITERS], [sw_ref[r - ITERS, k] for k in range(3)]
         return fy_ref[r - ITERS - rows], [fw_ref[r - ITERS - rows, k] for k in range(3)]
 
+    lefts = [row for q in range(high // BATCH) for row in unpack(left_ref[q], parts, False)]
+    rights = [row for q in range(high // BATCH) for row in unpack(right_ref[q], parts, True)]
     field, weights = {}, {}
     for r in range(high):
-        skip = 4 * (r % 2)
+        y, w = strip_at(r)
         values = [
-            jnp.where(
-                from_left,
-                roll(left_ref[r // 2], -8 * g - skip),
-                jnp.where(from_right, roll(right_ref[r // 2], 28 - 8 * g - skip), v),
-            )
-            for g, v in enumerate([strip_at(r)[0], *strip_at(r)[1]])
+            jnp.where(from_left, a, jnp.where(from_right, b, v)) for a, b, v in zip(lefts[r], rights[r], [y, *w])
         ]
         field[r], weights[r] = values[0], all_weights(values[1:], sign)
     for step in range(ITERS):
@@ -432,7 +444,7 @@
     tiles = cols // LANES
     plane = (tiles, levels * rows, LANES)
     flat = [pltpu.with_memory_space_constraint(a, pltpu.HBM) for a in flat]
-    head = (ITERS + (samples + 3) * tiles, levels, LANES)
+    head = (2 + (samples + 3) * tiles, levels, LANES)
     to_near, to_far, to_far_tail, *staged = call(
         edge_kernel,
         [halo, head, (ITERS - 1, *halo[1:]), (tiles, samples, levels * rows, LANES)] + [plane] * 3 + [jax.ShapeDtypeStruct(plane, sea_mask.dtype)],
@@ -446,12 +458,12 @@
     flat_plane = plane[1:]
     (own_msg,) = call(
         message_kernel,
-        [(2, rows // 2, levels, LANES)],
+        [(2, rows // BATCH, levels, LANES)],
         *staged,
         scratch=[(samples, *flat_plane)] + [flat_plane] * 3 + [pltpu.VMEM(flat_plane, sea_mask.dtype)],
         flops=10**6,
     )
-    message = (high // 2, levels, LANES)
+    message = (high // BATCH, levels, LANES)
     to_east, to_west = call(join_kernel, [message, message], own_msg, near, far)
     left = lax.ppermute(to_east, "lon", east)
     right = lax.ppermute(to_west, "lon", west)

time: 34.8 us -> 34.7 us (level)
  no operation moved by 1% of the time
where the time goes in v12:
time: 34.7 us; the launch traced here: 34.6 us
  blocking collectives  19.2 us (55%)
  Pallas kernels  8 us (23%)
  starting transfers between devices  6.61 us (19%)
  between operations  0.72 us (2%)
    all_to_all x1, blocking collectives, shards(): every = lax.all_to_all(spread, ('lat', 'lon'), 0, 0, tiled=True)  19.2 us
    pallas_call x8, Pallas kernels, call(): pl.pallas_call(kernel, out_shape=out, in_specs=[pl.BlockSpec(memory_space...  8 us
    ppermute x1, starting transfers between devices, shards(): left = lax.ppermute(to_east, 'lon', east)  2.64 us
    ppermute x1, starting transfers between devices, shards(): right = lax.ppermute(to_west, 'lon', west)  2.09 us
  transfers between devices with their start and end apart: 5, of which 0 were waited for; matrix products, arithmetic and copies ran while one was open for 0% of the time, Pallas kernels for 12%

profile of v12, /device:TPU:0, one launch (start us, length us, event | category | flops | bytes accessed | tf_op | source)
XLA Modules:
  0.0 34.6 jit_solution(1828557533936912208)
XLA Ops:
  0.6 1.6 %shard_map.68 = (f32[4,7,8,256]{3,2,1,0:T(8,128)S(1)}, f32[16,8,128]{2,1,0:T(8,128)S(1)}, f32[3,7,8,256]{3,2,1,0:T(8,128)S(1)}, f32[2,4,128,128]{3,2,1,0:T(8,128...) custom-call(f32[4,128,256]{2,1,0:T(8,128)} %bitcast.9, ...), custom_call_target="tpu_custom_call" | custom-call | bytes 1048576 | tf_op jit(solution)/shard_map/pallas_call | solution.py:420
  2.2 0.6 %collective-permute-start = (f32[4,7,8,256]{3,2,1,0:T(8,128)S(1)}, f32[4,7,8,256]{3,2,1,0:T(8,128)S(1)}, u32[]{:S(2)}, u32[]{:S(2)}) collective-permute-start(f32[4,7,8,256]{3,2,1,0:T(8,128)S(1)} %get-tuple-element.35), channel_id=1, source_target_pairs={{0,4},{4,0},{8,12},{12,8},{16,20},{20,16},{24,28},{28,24},{1,5},{5... | collective-permute-start | bytes 688136 | tf_op jit(solution)/shard_map/ppermute | solution.py:455
  2.8 0.7 %collective-permute-start.2 = (f32[3,7,8,256]{3,2,1,0:T(8,128)S(1)}, f32[3,7,8,256]{3,2,1,0:T(8,128)S(1)}, u32[]{:S(2)}, u32[]{:S(2)}) collective-permute-start(f32[3,7,8,256]{3,2,1,0:T(8,128)S(1)} %get-tuple-element.39), channel_id=1, source_target_pairs={{4,8},{8,4},{12,16},{16,12},{20,24},{24,20},{5,9},{9,5},{13,17},{1... | collective-permute-start | bytes 516104 | tf_op jit(solution)/shard_map/ppermute | solution.py:457
  3.5 0.7 %collective-permute-start.1 = (f32[16,8,128]{2,1,0:T(8,128)S(1)}, f32[16,8,128]{2,1,0:T(8,128)S(1)}, u32[]{:S(2)}, u32[]{:S(2)}) collective-permute-start(f32[16,8,128]{2,1,0:T(8,128)S(1)} %get-tuple-element.38), channel_id=1, source_target_pairs={{4,8},{8,4},{12,16},{16,12},{20,24},{24,20},{5,9},{9,5},{13,17},{1... | collective-permute-start | bytes 196616 | tf_op jit(solution)/shard_map/ppermute | solution.py:456
  4.1 0.4 %shard_map.72.own_ref = f32[2,4,8,128]{3,2,1,0:T(8,128)S(1)} custom-call(f32[2,4,128,128]{3,2,1,0:T(8,128)S(1)} %get-tuple-element.28.n_ref, f32[2,128,128]{2,1,0:T(8,128)S(1)} %get-tuple-element.29.a_ref, f32[2,128,128]{2,1,0:T(8,128)S(1)} %get-tuple-element.30.b_ref, f32[2,128,128]{2,1,0:T(8,128)S(1)} %get-tuple-element.31.s_ref, ...), custom_call_target="tpu_custom_call" | custom-call | flops 1000000 | bytes 1048576 | tf_op jit(solution)/shard_map/pallas_call | solution.py:420
  4.6 0.0 collective-permute-done.1.head_ref
  4.6 0.0 collective-permute-done.near_ref
  4.6 0.1 shard_map.73
  4.7 2.6 %collective-permute-start.3 = (f32[6,8,128]{2,1,0:T(8,128)S(1)}, f32[6,8,128]{2,1,0:T(8,128)S(1)}, u32[]{:S(2)}, u32[]{:S(2)}) collective-permute-start(f32[6,8,128]{2,1,0:T(8,128)S(1)} %get-tuple-element.47), channel_id=1, source_target_pairs={{0,1},{1,2},{2,3},{3,0},{4,5},{5,6},{6,7},{7,4},{8,9},{9,10},{10,1... | collective-permute-start | bytes 73736 | tf_op jit(solution)/shard_map/ppermute | solution.py:468
  7.3 2.1 %collective-permute-start.4 = (f32[6,8,128]{2,1,0:T(8,128)S(1)}, f32[6,8,128]{2,1,0:T(8,128)S(1)}, u32[]{:S(2)}, u32[]{:S(2)}) collective-permute-start(f32[6,8,128]{2,1,0:T(8,128)S(1)} %get-tuple-element.48), channel_id=1, source_target_pairs={{1,0},{2,1},{3,2},{0,3},{5,4},{6,5},{7,6},{4,7},{9,8},{10,9},{11,1... | collective-permute-start | bytes 73736 | tf_op jit(solution)/shard_map/ppermute | solution.py:469
  9.4 0.8 %shard_map.69 = (f32[16,4,8,256]{3,2,1,0:T(8,128)S(1)}, f32[16,4,8,256]{3,2,1,0:T(8,128)S(1)}, f32[16,8,128]{2,1,0:T(8,128)S(1)}, f32[16,3,8,128]{3,2,1,0:T(8,128)S(1)}) custom-call(f32[2,4,128,128]{3,2,1,0:T(8,128)S(1)} %get-tuple-element.28.n_ref, f32[2,128,128]{2,1,0:T(8,128)S(1)} %get-tuple-element.29.a_ref, f32[2,128,128]{2,1,0:T(8,128)S(1)} %get-tuple-element.30.b_ref, ...), custom_call_target="tpu_custom_call" | custom-call | flops 1000000 | bytes 1048576 | tf_op jit(solution)/shard_map/pallas_call | solution.py:420
  10.2 1.9 %shard_map.70 = (f32[16,4,8,256]{3,2,1,0:T(8,128)S(1)}, f32[3,2,4,8,256]{4,3,2,1,0:T(8,128)S(1)}, f32[4,8,128]{2,1,0:T(8,128)S(1)}, f32[4,3,8,128]{3,2,1,0:T(8,128)S(1)}) custom-call(f32[16,4,8,256]{3,2,1,0:T(8,128)S(1)} %get-tuple-element.33.y_ref, f32[16,4,8,256]{3,2,1,0:T(8,128)S(1)} %get-tuple-element.34.w_ref, ...), custom_call_target="tpu_custom_call" | custom-call | flops 10000000 | bytes 1277952 | tf_op jit(solution)/shard_map/pallas_call | solution.py:420
  12.1 0.0 collective-permute-done.2.tail_ref
  12.1 0.8 %shard_map.71 = (f32[4,4,8,256]{3,2,1,0:T(8,128)S(1)}, f32[4,8,128]{2,1,0:T(8,128)S(1)}, f32[4,3,8,128]{3,2,1,0:T(8,128)S(1)}) custom-call(f32[16,4,8,256]{3,2,1,0:T(8,128)S(1)} %get-tuple-element.33.y_ref, f32[16,4,8,256]{3,2,1,0:T(8,128)S(1)} %get-tuple-element.34.w_ref, f32[3,2,4,8,256]{4,3,2,1,0:T(8,128)S(1)} %get-tuple-element.37.keep_ref, ...), custom_call_target="tpu_custom_call" | custom-call | flops 1000000 | bytes 1482752 | tf_op jit(solution)/shard_map/pallas_call | solution.py:420
  12.9 0.0 collective-permute-done.3.left_ref
  12.9 0.0 collective-permute-done.4.right_ref
  12.9 1.4 %shard_map.74 = (f32[16,4,8,256]{3,2,1,0:T(8,128)S(1)}, f32[16,8,256]{2,1,0:T(8,128)S(1)}, f32[1,128]{1,0:T(1,128)S(1)}) custom-call(f32[16,4,8,256]{3,2,1,0:T(8,128)S(1)} %get-tuple-element.36.x_ref, f32[4,4,8,256]{3,2,1,0:T(8,128)S(1)} %get-tuple-element.40.xf_ref, f32[16,4,8,256]{3,2,1,0:T(8,128)S(1)} %get-tuple-element.34.w_ref, ...), custom_call_target="tpu_custom_call" | custom-call | bytes 1622016 | tf_op jit(solution)/shard_map/pallas_call | solution.py:420
  14.3 19.2 %all_to_all.5.all_ref = f32[32,1,128]{2,1,0:T(1,128)S(1)} all-to-all(f32[32,1,128]{2,1,0:T(1,128)S(1)} %broadcast_in_dim.3), channel_id=1, replica_groups=mesh['lat'=8,'lon'=4] {'lat','lon'}, dimensions={0} | all-to-all | bytes 32768 | tf_op jit(solution)/shard_map/all_to_all | solution.py:515
  33.5 1.0 %shard_map.75 = (f32[4,128,256]{2,1,0:T(8,128)}, f32[1,1]{1,0:T(1,128)}) custom-call(f32[16,4,8,256]{3,2,1,0:T(8,128)S(1)} %get-tuple-element.49.x_ref, f32[16,4,8,256]{3,2,1,0:T(8,128)S(1)} %get-tuple-element.34.w_ref, f32[16,8,256]{2,1,0:T(8,128)S(1)} %get-tuple-element.50.var_ref, f32[32,1,128]{2,1,0:T(1,128)S(1)} %all_to_all.5.all_ref), custom_call_target="tpu_custom_call" | custom-call | bytes 1196032 | tf_op jit(solution)/shard_map/pallas_call | solution.py:420
  (1 shorter events, 0.0 us)
Async XLA Ops:
  2.2 2.3 %collective-permute-start = (f32[4,7,8,256]{3,2,1,0:T(8,128)S(1)}, f32[4,7,8,256]{3,2,1,0:T(8,128)S(1)}, u32[]{:S(2)}, u32[]{:S(2)}) collective-permute-start(f32[4,7,8,256]{3,2,1,0:T(8,128)S(1)} %get-tuple-element.35), channel_id=1, source_target_pairs={{0,4},{4,0},{8,12},{12,8},{16,20},{20,16},{24,28},{28,24},{1,5},{5... | collective-permute-start | bytes 688136 | tf_op jit(solution)/shard_map/ppermute | solution.py:455
  2.8 9.3 %collective-permute-start.2 = (f32[3,7,8,256]{3,2,1,0:T(8,128)S(1)}, f32[3,7,8,256]{3,2,1,0:T(8,128)S(1)}, u32[]{:S(2)}, u32[]{:S(2)}) collective-permute-start(f32[3,7,8,256]{3,2,1,0:T(8,128)S(1)} %get-tuple-element.39), channel_id=1, source_target_pairs={{4,8},{8,4},{12,16},{16,12},{20,24},{24,20},{5,9},{9,5},{13,17},{1... | collective-permute-start | bytes 516104 | tf_op jit(solution)/shard_map/ppermute | solution.py:457
  3.5 1.1 %collective-permute-start.1 = (f32[16,8,128]{2,1,0:T(8,128)S(1)}, f32[16,8,128]{2,1,0:T(8,128)S(1)}, u32[]{:S(2)}, u32[]{:S(2)}) collective-permute-start(f32[16,8,128]{2,1,0:T(8,128)S(1)} %get-tuple-element.38), channel_id=1, source_target_pairs={{4,8},{8,4},{12,16},{16,12},{20,24},{24,20},{5,9},{9,5},{13,17},{1... | collective-permute-start | bytes 196616 | tf_op jit(solution)/shard_map/ppermute | solution.py:456
  4.7 8.3 %collective-permute-start.3 = (f32[6,8,128]{2,1,0:T(8,128)S(1)}, f32[6,8,128]{2,1,0:T(8,128)S(1)}, u32[]{:S(2)}, u32[]{:S(2)}) collective-permute-start(f32[6,8,128]{2,1,0:T(8,128)S(1)} %get-tuple-element.47), channel_id=1, source_target_pairs={{0,1},{1,2},{2,3},{3,0},{4,5},{5,6},{6,7},{7,4},{8,9},{9,10},{10,1... | collective-permute-start | bytes 73736 | tf_op jit(solution)/shard_map/ppermute | solution.py:468
  7.3 5.6 %collective-permute-start.4 = (f32[6,8,128]{2,1,0:T(8,128)S(1)}, f32[6,8,128]{2,1,0:T(8,128)S(1)}, u32[]{:S(2)}, u32[]{:S(2)}) collective-permute-start(f32[6,8,128]{2,1,0:T(8,128)S(1)} %get-tuple-element.48), channel_id=1, source_target_pairs={{1,0},{2,1},{3,2},{0,3},{5,4},{6,5},{7,6},{4,7},{9,8},{10,9},{11,1... | collective-permute-start | bytes 73736 | tf_op jit(solution)/shard_map/ppermute | solution.py:469

commit v13 on v12

--- a/solution.py
+++ b/solution.py
@@ -334,7 +334,8 @@
 
 
 def finish_kernel(
-    x_ref, xf_ref, w_ref, sy_ref, sw_ref, hy_ref, hw_ref, fy_ref, fw_ref, left_ref, right_ref, out_ref, var_ref, sum_ref
+    x_ref, xf_ref, w_ref, sy_ref, sw_ref, hy_ref, hw_ref, fy_ref, fw_ref, left_ref, right_ref, out_ref, var_ref, sum_ref,
+    line_ref,
 ):
     rows, samples, levels, cols = x_ref.shape
     high = rows + 2 * ITERS
@@ -350,18 +351,23 @@
             return sy_ref[r - ITERS], [sw_ref[r - ITERS, k] for k in range(3)]
         return fy_ref[r - ITERS - rows], [fw_ref[r - ITERS - rows, k] for k in range(3)]
 
-    lefts = [row for q in range(high // BATCH) for row in unpack(left_ref[q], parts, False)]
-    rights = [row for q in range(high // BATCH) for row in unpack(right_ref[q], parts, True)]
-    field, weights = {}, {}
-    for r in range(high):
-        y, w = strip_at(r)
-        values = [
-            jnp.where(from_left, a, jnp.where(from_right, b, v)) for a, b, v in zip(lefts[r], rights[r], [y, *w])
-        ]
-        field[r], weights[r] = values[0], all_weights(values[1:], sign)
+    for q in range(high // BATCH):
+        lefts, rights = unpack(left_ref[q], parts, False), unpack(right_ref[q], parts, True)
+        for j in range(BATCH):
+            y, w = strip_at(q * BATCH + j)
+            values = [
+                jnp.where(from_left, a, jnp.where(from_right, b, v)) for a, b, v in zip(lefts[j], rights[j], [y, *w])
+            ]
+            for k, v in enumerate([values[0], *all_weights(values[1:], sign)]):
+                line_ref[q * BATCH + j, k] = v
+
+    def get_w(r):
+        return [line_ref[r, 1 + k] for k in range(4)]
+
+    field = {r: line_ref[r, 0] for r in range(high)}
     for step in range(ITERS):
         new = {}
-        stencil(field.__getitem__, weights.__getitem__, step + 1, high - 1 - step, new.__setitem__)
+        stencil(field.__getitem__, get_w, step + 1, high - 1 - step, new.__setitem__)
         field = new
 
     total, count = None, None
@@ -510,6 +516,7 @@
         fw,
         left,
         right,
+        scratch=[(high, 5, levels, LANES)],
     )
     spread = jnp.broadcast_to(part, (n_lat * n_lon, 1, LANES))
     every = lax.all_to_all(spread, ("lat", "lon"), 0, 0, tiled=True)

time: 34.7 us -> 34.7 us (level)
  no operation moved by 1% of the time
where the time goes in v13:
time: 34.7 us; the launch traced here: 34.5 us
  blocking collectives  19.2 us (55%)
  Pallas kernels  7.98 us (23%)
  starting transfers between devices  6.61 us (19%)
  between operations  0.72 us (2%)
    all_to_all x1, blocking collectives, shards(): every = lax.all_to_all(spread, ('lat', 'lon'), 0, 0, tiled=True)  19.2 us
    pallas_call x8, Pallas kernels, call(): pl.pallas_call(kernel, out_shape=out, in_specs=[pl.BlockSpec(memory_space...  7.98 us
    ppermute x1, starting transfers between devices, shards(): left = lax.ppermute(to_east, 'lon', east)  2.64 us
    ppermute x1, starting transfers between devices, shards(): right = lax.ppermute(to_west, 'lon', west)  2.09 us
  transfers between devices with their start and end apart: 5, of which 0 were waited for; matrix products, arithmetic and copies ran while one was open for 0% of the time, Pallas kernels for 12%

profile of v13, /device:TPU:0, one launch (start us, length us, event | category | flops | bytes accessed | tf_op | source)
XLA Modules:
  0.0 34.5 jit_solution(6879957077728746386)
XLA Ops:
  0.6 1.6 %shard_map.68 = (f32[4,7,8,256]{3,2,1,0:T(8,128)S(1)}, f32[16,8,128]{2,1,0:T(8,128)S(1)}, f32[3,7,8,256]{3,2,1,0:T(8,128)S(1)}, f32[2,4,128,128]{3,2,1,0:T(8,128...) custom-call(f32[4,128,256]{2,1,0:T(8,128)} %bitcast.9, ...), custom_call_target="tpu_custom_call" | custom-call | bytes 1048576 | tf_op jit(solution)/shard_map/pallas_call | solution.py:426
  2.2 0.6 %collective-permute-start = (f32[4,7,8,256]{3,2,1,0:T(8,128)S(1)}, f32[4,7,8,256]{3,2,1,0:T(8,128)S(1)}, u32[]{:S(2)}, u32[]{:S(2)}) collective-permute-start(f32[4,7,8,256]{3,2,1,0:T(8,128)S(1)} %get-tuple-element.35), channel_id=1, source_target_pairs={{0,4},{4,0},{8,12},{12,8},{16,20},{20,16},{24,28},{28,24},{1,5},{5... | collective-permute-start | bytes 688136 | tf_op jit(solution)/shard_map/ppermute | solution.py:461
  2.8 0.7 %collective-permute-start.2 = (f32[3,7,8,256]{3,2,1,0:T(8,128)S(1)}, f32[3,7,8,256]{3,2,1,0:T(8,128)S(1)}, u32[]{:S(2)}, u32[]{:S(2)}) collective-permute-start(f32[3,7,8,256]{3,2,1,0:T(8,128)S(1)} %get-tuple-element.39), channel_id=1, source_target_pairs={{4,8},{8,4},{12,16},{16,12},{20,24},{24,20},{5,9},{9,5},{13,17},{1... | collective-permute-start | bytes 516104 | tf_op jit(solution)/shard_map/ppermute | solution.py:463
  3.5 0.7 %collective-permute-start.1 = (f32[16,8,128]{2,1,0:T(8,128)S(1)}, f32[16,8,128]{2,1,0:T(8,128)S(1)}, u32[]{:S(2)}, u32[]{:S(2)}) collective-permute-start(f32[16,8,128]{2,1,0:T(8,128)S(1)} %get-tuple-element.38), channel_id=1, source_target_pairs={{4,8},{8,4},{12,16},{16,12},{20,24},{24,20},{5,9},{9,5},{13,17},{1... | collective-permute-start | bytes 196616 | tf_op jit(solution)/shard_map/ppermute | solution.py:462
  4.1 0.4 %shard_map.72.own_ref = f32[2,4,8,128]{3,2,1,0:T(8,128)S(1)} custom-call(f32[2,4,128,128]{3,2,1,0:T(8,128)S(1)} %get-tuple-element.28.n_ref, f32[2,128,128]{2,1,0:T(8,128)S(1)} %get-tuple-element.29.a_ref, f32[2,128,128]{2,1,0:T(8,128)S(1)} %get-tuple-element.30.b_ref, f32[2,128,128]{2,1,0:T(8,128)S(1)} %get-tuple-element.31.s_ref, ...), custom_call_target="tpu_custom_call" | custom-call | flops 1000000 | bytes 1048576 | tf_op jit(solution)/shard_map/pallas_call | solution.py:426
  4.6 0.0 collective-permute-done.1.head_ref
  4.6 0.0 collective-permute-done.near_ref
  4.6 0.1 shard_map.73
  4.7 2.6 %collective-permute-start.3 = (f32[6,8,128]{2,1,0:T(8,128)S(1)}, f32[6,8,128]{2,1,0:T(8,128)S(1)}, u32[]{:S(2)}, u32[]{:S(2)}) collective-permute-start(f32[6,8,128]{2,1,0:T(8,128)S(1)} %get-tuple-element.47), channel_id=1, source_target_pairs={{0,1},{1,2},{2,3},{3,0},{4,5},{5,6},{6,7},{7,4},{8,9},{9,10},{10,1... | collective-permute-start | bytes 73736 | tf_op jit(solution)/shard_map/ppermute | solution.py:474
  7.3 2.1 %collective-permute-start.4 = (f32[6,8,128]{2,1,0:T(8,128)S(1)}, f32[6,8,128]{2,1,0:T(8,128)S(1)}, u32[]{:S(2)}, u32[]{:S(2)}) collective-permute-start(f32[6,8,128]{2,1,0:T(8,128)S(1)} %get-tuple-element.48), channel_id=1, source_target_pairs={{1,0},{2,1},{3,2},{0,3},{5,4},{6,5},{7,6},{4,7},{9,8},{10,9},{11,1... | collective-permute-start | bytes 73736 | tf_op jit(solution)/shard_map/ppermute | solution.py:475
  9.4 0.8 %shard_map.69 = (f32[16,4,8,256]{3,2,1,0:T(8,128)S(1)}, f32[16,4,8,256]{3,2,1,0:T(8,128)S(1)}, f32[16,8,128]{2,1,0:T(8,128)S(1)}, f32[16,3,8,128]{3,2,1,0:T(8,128)S(1)}) custom-call(f32[2,4,128,128]{3,2,1,0:T(8,128)S(1)} %get-tuple-element.28.n_ref, f32[2,128,128]{2,1,0:T(8,128)S(1)} %get-tuple-element.29.a_ref, f32[2,128,128]{2,1,0:T(8,128)S(1)} %get-tuple-element.30.b_ref, ...), custom_call_target="tpu_custom_call" | custom-call | flops 1000000 | bytes 1048576 | tf_op jit(solution)/shard_map/pallas_call | solution.py:426
  10.2 1.9 %shard_map.70 = (f32[16,4,8,256]{3,2,1,0:T(8,128)S(1)}, f32[3,2,4,8,256]{4,3,2,1,0:T(8,128)S(1)}, f32[4,8,128]{2,1,0:T(8,128)S(1)}, f32[4,3,8,128]{3,2,1,0:T(8,128)S(1)}) custom-call(f32[16,4,8,256]{3,2,1,0:T(8,128)S(1)} %get-tuple-element.33.y_ref, f32[16,4,8,256]{3,2,1,0:T(8,128)S(1)} %get-tuple-element.34.w_ref, ...), custom_call_target="tpu_custom_call" | custom-call | flops 10000000 | bytes 1277952 | tf_op jit(solution)/shard_map/pallas_call | solution.py:426
  12.1 0.0 collective-permute-done.2.tail_ref
  12.1 0.8 %shard_map.71 = (f32[4,4,8,256]{3,2,1,0:T(8,128)S(1)}, f32[4,8,128]{2,1,0:T(8,128)S(1)}, f32[4,3,8,128]{3,2,1,0:T(8,128)S(1)}) custom-call(f32[16,4,8,256]{3,2,1,0:T(8,128)S(1)} %get-tuple-element.33.y_ref, f32[16,4,8,256]{3,2,1,0:T(8,128)S(1)} %get-tuple-element.34.w_ref, f32[3,2,4,8,256]{4,3,2,1,0:T(8,128)S(1)} %get-tuple-element.37.keep_ref, ...), custom_call_target="tpu_custom_call" | custom-call | flops 1000000 | bytes 1482752 | tf_op jit(solution)/shard_map/pallas_call | solution.py:426
  12.9 0.0 collective-permute-done.3.left_ref
  12.9 0.0 collective-permute-done.4.right_ref
  12.9 1.4 %shard_map.74 = (f32[16,4,8,256]{3,2,1,0:T(8,128)S(1)}, f32[16,8,256]{2,1,0:T(8,128)S(1)}, f32[1,128]{1,0:T(1,128)S(1)}) custom-call(f32[16,4,8,256]{3,2,1,0:T(8,128)S(1)} %get-tuple-element.36.x_ref, f32[4,4,8,256]{3,2,1,0:T(8,128)S(1)} %get-tuple-element.40.xf_ref, f32[16,4,8,256]{3,2,1,0:T(8,128)S(1)} %get-tuple-element.34.w_ref, ...), custom_call_target="tpu_custom_call" | custom-call | bytes 1622016 | tf_op jit(solution)/shard_map/pallas_call | solution.py:426
  14.3 19.2 %all_to_all.5.all_ref = f32[32,1,128]{2,1,0:T(1,128)S(1)} all-to-all(f32[32,1,128]{2,1,0:T(1,128)S(1)} %broadcast_in_dim.3), channel_id=1, replica_groups=mesh['lat'=8,'lon'=4] {'lat','lon'}, dimensions={0} | all-to-all | bytes 32768 | tf_op jit(solution)/shard_map/all_to_all | solution.py:522
  33.5 1.0 %shard_map.75 = (f32[4,128,256]{2,1,0:T(8,128)}, f32[1,1]{1,0:T(1,128)}) custom-call(f32[16,4,8,256]{3,2,1,0:T(8,128)S(1)} %get-tuple-element.49.x_ref, f32[16,4,8,256]{3,2,1,0:T(8,128)S(1)} %get-tuple-element.34.w_ref, f32[16,8,256]{2,1,0:T(8,128)S(1)} %get-tuple-element.50.var_ref, f32[32,1,128]{2,1,0:T(1,128)S(1)} %all_to_all.5.all_ref), custom_call_target="tpu_custom_call" | custom-call | bytes 1196032 | tf_op jit(solution)/shard_map/pallas_call | solution.py:426
  (1 shorter events, 0.0 us)
Async XLA Ops:
  2.2 2.3 %collective-permute-start = (f32[4,7,8,256]{3,2,1,0:T(8,128)S(1)}, f32[4,7,8,256]{3,2,1,0:T(8,128)S(1)}, u32[]{:S(2)}, u32[]{:S(2)}) collective-permute-start(f32[4,7,8,256]{3,2,1,0:T(8,128)S(1)} %get-tuple-element.35), channel_id=1, source_target_pairs={{0,4},{4,0},{8,12},{12,8},{16,20},{20,16},{24,28},{28,24},{1,5},{5... | collective-permute-start | bytes 688136 | tf_op jit(solution)/shard_map/ppermute | solution.py:461
  2.8 9.3 %collective-permute-start.2 = (f32[3,7,8,256]{3,2,1,0:T(8,128)S(1)}, f32[3,7,8,256]{3,2,1,0:T(8,128)S(1)}, u32[]{:S(2)}, u32[]{:S(2)}) collective-permute-start(f32[3,7,8,256]{3,2,1,0:T(8,128)S(1)} %get-tuple-element.39), channel_id=1, source_target_pairs={{4,8},{8,4},{12,16},{16,12},{20,24},{24,20},{5,9},{9,5},{13,17},{1... | collective-permute-start | bytes 516104 | tf_op jit(solution)/shard_map/ppermute | solution.py:463
  3.5 1.1 %collective-permute-start.1 = (f32[16,8,128]{2,1,0:T(8,128)S(1)}, f32[16,8,128]{2,1,0:T(8,128)S(1)}, u32[]{:S(2)}, u32[]{:S(2)}) collective-permute-start(f32[16,8,128]{2,1,0:T(8,128)S(1)} %get-tuple-element.38), channel_id=1, source_target_pairs={{4,8},{8,4},{12,16},{16,12},{20,24},{24,20},{5,9},{9,5},{13,17},{1... | collective-permute-start | bytes 196616 | tf_op jit(solution)/shard_map/ppermute | solution.py:462
  4.7 8.3 %collective-permute-start.3 = (f32[6,8,128]{2,1,0:T(8,128)S(1)}, f32[6,8,128]{2,1,0:T(8,128)S(1)}, u32[]{:S(2)}, u32[]{:S(2)}) collective-permute-start(f32[6,8,128]{2,1,0:T(8,128)S(1)} %get-tuple-element.47), channel_id=1, source_target_pairs={{0,1},{1,2},{2,3},{3,0},{4,5},{5,6},{6,7},{7,4},{8,9},{9,10},{10,1... | collective-permute-start | bytes 73736 | tf_op jit(solution)/shard_map/ppermute | solution.py:474
  7.3 5.6 %collective-permute-start.4 = (f32[6,8,128]{2,1,0:T(8,128)S(1)}, f32[6,8,128]{2,1,0:T(8,128)S(1)}, u32[]{:S(2)}, u32[]{:S(2)}) collective-permute-start(f32[6,8,128]{2,1,0:T(8,128)S(1)} %get-tuple-element.48), channel_id=1, source_target_pairs={{1,0},{2,1},{3,2},{0,3},{5,4},{6,5},{7,6},{4,7},{9,8},{10,9},{11,1... | collective-permute-start | bytes 73736 | tf_op jit(solution)/shard_map/ppermute | solution.py:475

commit v14 on v13

--- a/solution.py
+++ b/solution.py
@@ -161,9 +161,13 @@
     return east, west
 
 
-def unpack(tile, parts, from_east):
+def turns(tile):
+    return [roll(tile, SEG * q) for q in range(4)]
+
+
+def unpack(turned, parts, from_east):
     _, seg, _ = parts
-    turned = [roll(tile, SEG * q) for q in range(4)]
+    tile = turned[0]
     every = [by_segment([turned[(q - k) % 4] for q in range(4)], seg, 0) for k in range(4 if from_east else 3)]
     rows = []
     for j in range(BATCH):
@@ -351,15 +355,26 @@
             return sy_ref[r - ITERS], [sw_ref[r - ITERS, k] for k in range(3)]
         return fy_ref[r - ITERS - rows], [fw_ref[r - ITERS - rows, k] for k in range(3)]
 
-    for q in range(high // BATCH):
-        lefts, rights = unpack(left_ref[q], parts, False), unpack(right_ref[q], parts, True)
-        for j in range(BATCH):
-            y, w = strip_at(q * BATCH + j)
-            values = [
-                jnp.where(from_left, a, jnp.where(from_right, b, v)) for a, b, v in zip(lefts[j], rights[j], [y, *w])
-            ]
-            for k, v in enumerate([values[0], *all_weights(values[1:], sign)]):
-                line_ref[q * BATCH + j, k] = v
+    tiles = high // BATCH
+    group = 2 if tiles % 2 == 0 else 1
+
+    def turn(first):
+        return [(turns(left_ref[q]), turns(right_ref[q])) for q in range(first, min(first + group, tiles))]
+
+    ahead = turn(0)
+    for first in range(0, tiles, group):
+        here, ahead = ahead, turn(first + group)
+        sides = [(unpack(a, parts, False), unpack(b, parts, True)) for a, b in here]
+        for i, (lefts, rights) in enumerate(sides):
+            for j in range(BATCH):
+                r = (first + i) * BATCH + j
+                y, w = strip_at(r)
+                values = [
+                    jnp.where(from_left, a, jnp.where(from_right, b, v))
+                    for a, b, v in zip(lefts[j], rights[j], [y, *w])
+                ]
+                for k, v in enumerate([values[0], *all_weights(values[1:], sign)]):
+                    line_ref[r, k] = v
 
     def get_w(r):
         return [line_ref[r, 1 + k] for k in range(4)]

time: 34.7 us -> 34.2 us (0.986)
  Pallas kernels: 7.98 us -> 7.45 us
    pallas_call x8, Pallas kernels: 7.98 us -> 7.45 us  [call(): pl.pallas_call(kernel, out_shape=out, in_specs=[pl.BlockSpec(memory_space...]
where the time goes in v14:
time: 34.2 us; the launch traced here: 34 us
  blocking collectives  19.2 us (56%)
  Pallas kernels  7.45 us (22%)
  starting transfers between devices  6.61 us (19%)
  between operations  0.72 us (2%)
    all_to_all x1, blocking collectives, shards(): every = lax.all_to_all(spread, ('lat', 'lon'), 0, 0, tiled=True)  19.2 us
    pallas_call x8, Pallas kernels, call(): pl.pallas_call(kernel, out_shape=out, in_specs=[pl.BlockSpec(memory_space...  7.45 us
    ppermute x1, starting transfers between devices, shards(): left = lax.ppermute(to_east, 'lon', east)  2.64 us
    ppermute x1, starting transfers between devices, shards(): right = lax.ppermute(to_west, 'lon', west)  2.09 us
  transfers between devices with their start and end apart: 5, of which 0 were waited for; matrix products, arithmetic and copies ran while one was open for 0% of the time, Pallas kernels for 12%

profile of v14, /device:TPU:0, one launch (start us, length us, event | category | flops | bytes accessed | tf_op | source)
XLA Modules:
  0.0 34.0 jit_solution(7245987844616806126)
XLA Ops:
  0.6 1.6 %shard_map.68 = (f32[4,7,8,256]{3,2,1,0:T(8,128)S(1)}, f32[16,8,128]{2,1,0:T(8,128)S(1)}, f32[3,7,8,256]{3,2,1,0:T(8,128)S(1)}, f32[2,4,128,128]{3,2,1,0:T(8,128...) custom-call(f32[4,128,256]{2,1,0:T(8,128)} %bitcast.9, ...), custom_call_target="tpu_custom_call" | custom-call | bytes 1048576 | tf_op jit(solution)/shard_map/pallas_call | solution.py:441
  2.2 0.6 %collective-permute-start = (f32[4,7,8,256]{3,2,1,0:T(8,128)S(1)}, f32[4,7,8,256]{3,2,1,0:T(8,128)S(1)}, u32[]{:S(2)}, u32[]{:S(2)}) collective-permute-start(f32[4,7,8,256]{3,2,1,0:T(8,128)S(1)} %get-tuple-element.35), channel_id=1, source_target_pairs={{0,4},{4,0},{8,12},{12,8},{16,20},{20,16},{24,28},{28,24},{1,5},{5... | collective-permute-start | bytes 688136 | tf_op jit(solution)/shard_map/ppermute | solution.py:476
  2.8 0.7 %collective-permute-start.2 = (f32[3,7,8,256]{3,2,1,0:T(8,128)S(1)}, f32[3,7,8,256]{3,2,1,0:T(8,128)S(1)}, u32[]{:S(2)}, u32[]{:S(2)}) collective-permute-start(f32[3,7,8,256]{3,2,1,0:T(8,128)S(1)} %get-tuple-element.39), channel_id=1, source_target_pairs={{4,8},{8,4},{12,16},{16,12},{20,24},{24,20},{5,9},{9,5},{13,17},{1... | collective-permute-start | bytes 516104 | tf_op jit(solution)/shard_map/ppermute | solution.py:478
  3.5 0.7 %collective-permute-start.1 = (f32[16,8,128]{2,1,0:T(8,128)S(1)}, f32[16,8,128]{2,1,0:T(8,128)S(1)}, u32[]{:S(2)}, u32[]{:S(2)}) collective-permute-start(f32[16,8,128]{2,1,0:T(8,128)S(1)} %get-tuple-element.38), channel_id=1, source_target_pairs={{4,8},{8,4},{12,16},{16,12},{20,24},{24,20},{5,9},{9,5},{13,17},{1... | collective-permute-start | bytes 196616 | tf_op jit(solution)/shard_map/ppermute | solution.py:477
  4.1 0.4 %shard_map.72.own_ref = f32[2,4,8,128]{3,2,1,0:T(8,128)S(1)} custom-call(f32[2,4,128,128]{3,2,1,0:T(8,128)S(1)} %get-tuple-element.28.n_ref, f32[2,128,128]{2,1,0:T(8,128)S(1)} %get-tuple-element.29.a_ref, f32[2,128,128]{2,1,0:T(8,128)S(1)} %get-tuple-element.30.b_ref, f32[2,128,128]{2,1,0:T(8,128)S(1)} %get-tuple-element.31.s_ref, ...), custom_call_target="tpu_custom_call" | custom-call | flops 1000000 | bytes 1048576 | tf_op jit(solution)/shard_map/pallas_call | solution.py:441
  4.6 0.0 collective-permute-done.1.head_ref
  4.6 0.0 collective-permute-done.near_ref
  4.6 0.1 shard_map.73
  4.7 2.6 %collective-permute-start.3 = (f32[6,8,128]{2,1,0:T(8,128)S(1)}, f32[6,8,128]{2,1,0:T(8,128)S(1)}, u32[]{:S(2)}, u32[]{:S(2)}) collective-permute-start(f32[6,8,128]{2,1,0:T(8,128)S(1)} %get-tuple-element.47), channel_id=1, source_target_pairs={{0,1},{1,2},{2,3},{3,0},{4,5},{5,6},{6,7},{7,4},{8,9},{9,10},{10,1... | collective-permute-start | bytes 73736 | tf_op jit(solution)/shard_map/ppermute | solution.py:489
  7.3 2.1 %collective-permute-start.4 = (f32[6,8,128]{2,1,0:T(8,128)S(1)}, f32[6,8,128]{2,1,0:T(8,128)S(1)}, u32[]{:S(2)}, u32[]{:S(2)}) collective-permute-start(f32[6,8,128]{2,1,0:T(8,128)S(1)} %get-tuple-element.48), channel_id=1, source_target_pairs={{1,0},{2,1},{3,2},{0,3},{5,4},{6,5},{7,6},{4,7},{9,8},{10,9},{11,1... | collective-permute-start | bytes 73736 | tf_op jit(solution)/shard_map/ppermute | solution.py:490
  9.4 0.8 %shard_map.69 = (f32[16,4,8,256]{3,2,1,0:T(8,128)S(1)}, f32[16,4,8,256]{3,2,1,0:T(8,128)S(1)}, f32[16,8,128]{2,1,0:T(8,128)S(1)}, f32[16,3,8,128]{3,2,1,0:T(8,128)S(1)}) custom-call(f32[2,4,128,128]{3,2,1,0:T(8,128)S(1)} %get-tuple-element.28.n_ref, f32[2,128,128]{2,1,0:T(8,128)S(1)} %get-tuple-element.29.a_ref, f32[2,128,128]{2,1,0:T(8,128)S(1)} %get-tuple-element.30.b_ref, ...), custom_call_target="tpu_custom_call" | custom-call | flops 1000000 | bytes 1048576 | tf_op jit(solution)/shard_map/pallas_call | solution.py:441
  10.2 1.9 %shard_map.70 = (f32[16,4,8,256]{3,2,1,0:T(8,128)S(1)}, f32[3,2,4,8,256]{4,3,2,1,0:T(8,128)S(1)}, f32[4,8,128]{2,1,0:T(8,128)S(1)}, f32[4,3,8,128]{3,2,1,0:T(8,128)S(1)}) custom-call(f32[16,4,8,256]{3,2,1,0:T(8,128)S(1)} %get-tuple-element.33.y_ref, f32[16,4,8,256]{3,2,1,0:T(8,128)S(1)} %get-tuple-element.34.w_ref, ...), custom_call_target="tpu_custom_call" | custom-call | flops 10000000 | bytes 1277952 | tf_op jit(solution)/shard_map/pallas_call | solution.py:441
  12.1 0.0 collective-permute-done.2.tail_ref
  12.1 0.8 %shard_map.71 = (f32[4,4,8,256]{3,2,1,0:T(8,128)S(1)}, f32[4,8,128]{2,1,0:T(8,128)S(1)}, f32[4,3,8,128]{3,2,1,0:T(8,128)S(1)}) custom-call(f32[16,4,8,256]{3,2,1,0:T(8,128)S(1)} %get-tuple-element.33.y_ref, f32[16,4,8,256]{3,2,1,0:T(8,128)S(1)} %get-tuple-element.34.w_ref, f32[3,2,4,8,256]{4,3,2,1,0:T(8,128)S(1)} %get-tuple-element.37.keep_ref, ...), custom_call_target="tpu_custom_call" | custom-call | flops 1000000 | bytes 1482752 | tf_op jit(solution)/shard_map/pallas_call | solution.py:441
  12.9 0.0 collective-permute-done.3.left_ref
  12.9 0.0 collective-permute-done.4.right_ref
  12.9 0.8 %shard_map.74 = (f32[16,4,8,256]{3,2,1,0:T(8,128)S(1)}, f32[16,8,256]{2,1,0:T(8,128)S(1)}, f32[1,128]{1,0:T(1,128)S(1)}) custom-call(f32[16,4,8,256]{3,2,1,0:T(8,128)S(1)} %get-tuple-element.36.x_ref, f32[4,4,8,256]{3,2,1,0:T(8,128)S(1)} %get-tuple-element.40.xf_ref, f32[16,4,8,256]{3,2,1,0:T(8,128)S(1)} %get-tuple-element.34.w_ref, ...), custom_call_target="tpu_custom_call" | custom-call | bytes 1622016 | tf_op jit(solution)/shard_map/pallas_call | solution.py:441
  13.8 19.2 %all_to_all.5.all_ref = f32[32,1,128]{2,1,0:T(1,128)S(1)} all-to-all(f32[32,1,128]{2,1,0:T(1,128)S(1)} %broadcast_in_dim.3), channel_id=1, replica_groups=mesh['lat'=8,'lon'=4] {'lat','lon'}, dimensions={0} | all-to-all | bytes 32768 | tf_op jit(solution)/shard_map/all_to_all | solution.py:537
  33.0 1.0 %shard_map.75 = (f32[4,128,256]{2,1,0:T(8,128)}, f32[1,1]{1,0:T(1,128)}) custom-call(f32[16,4,8,256]{3,2,1,0:T(8,128)S(1)} %get-tuple-element.49.x_ref, f32[16,4,8,256]{3,2,1,0:T(8,128)S(1)} %get-tuple-element.34.w_ref, f32[16,8,256]{2,1,0:T(8,128)S(1)} %get-tuple-element.50.var_ref, f32[32,1,128]{2,1,0:T(1,128)S(1)} %all_to_all.5.all_ref), custom_call_target="tpu_custom_call" | custom-call | bytes 1196032 | tf_op jit(solution)/shard_map/pallas_call | solution.py:441
  (1 shorter events, 0.0 us)
Async XLA Ops:
  2.2 2.3 %collective-permute-start = (f32[4,7,8,256]{3,2,1,0:T(8,128)S(1)}, f32[4,7,8,256]{3,2,1,0:T(8,128)S(1)}, u32[]{:S(2)}, u32[]{:S(2)}) collective-permute-start(f32[4,7,8,256]{3,2,1,0:T(8,128)S(1)} %get-tuple-element.35), channel_id=1, source_target_pairs={{0,4},{4,0},{8,12},{12,8},{16,20},{20,16},{24,28},{28,24},{1,5},{5... | collective-permute-start | bytes 688136 | tf_op jit(solution)/shard_map/ppermute | solution.py:476
  2.8 9.3 %collective-permute-start.2 = (f32[3,7,8,256]{3,2,1,0:T(8,128)S(1)}, f32[3,7,8,256]{3,2,1,0:T(8,128)S(1)}, u32[]{:S(2)}, u32[]{:S(2)}) collective-permute-start(f32[3,7,8,256]{3,2,1,0:T(8,128)S(1)} %get-tuple-element.39), channel_id=1, source_target_pairs={{4,8},{8,4},{12,16},{16,12},{20,24},{24,20},{5,9},{9,5},{13,17},{1... | collective-permute-start | bytes 516104 | tf_op jit(solution)/shard_map/ppermute | solution.py:478
  3.5 1.1 %collective-permute-start.1 = (f32[16,8,128]{2,1,0:T(8,128)S(1)}, f32[16,8,128]{2,1,0:T(8,128)S(1)}, u32[]{:S(2)}, u32[]{:S(2)}) collective-permute-start(f32[16,8,128]{2,1,0:T(8,128)S(1)} %get-tuple-element.38), channel_id=1, source_target_pairs={{4,8},{8,4},{12,16},{16,12},{20,24},{24,20},{5,9},{9,5},{13,17},{1... | collective-permute-start | bytes 196616 | tf_op jit(solution)/shard_map/ppermute | solution.py:477
  4.7 8.3 %collective-permute-start.3 = (f32[6,8,128]{2,1,0:T(8,128)S(1)}, f32[6,8,128]{2,1,0:T(8,128)S(1)}, u32[]{:S(2)}, u32[]{:S(2)}) collective-permute-start(f32[6,8,128]{2,1,0:T(8,128)S(1)} %get-tuple-element.47), channel_id=1, source_target_pairs={{0,1},{1,2},{2,3},{3,0},{4,5},{5,6},{6,7},{7,4},{8,9},{9,10},{10,1... | collective-permute-start | bytes 73736 | tf_op jit(solution)/shard_map/ppermute | solution.py:489
  7.3 5.6 %collective-permute-start.4 = (f32[6,8,128]{2,1,0:T(8,128)S(1)}, f32[6,8,128]{2,1,0:T(8,128)S(1)}, u32[]{:S(2)}, u32[]{:S(2)}) collective-permute-start(f32[6,8,128]{2,1,0:T(8,128)S(1)} %get-tuple-element.48), channel_id=1, source_target_pairs={{1,0},{2,1},{3,2},{0,3},{5,4},{6,5},{7,6},{4,7},{9,8},{10,9},{11,1... | collective-permute-start | bytes 73736 | tf_op jit(solution)/shard_map/ppermute | solution.py:490
